TPU v7x, 32 devices: a whole 2x2x4 slice. The times are simulated.
32 devices in a mesh: groups: 2 (over y), cand: 4 (over z), tensor: 4 (over x, core).
Axes of the slice: x: 2, y: 2, z: 4, core: 2. Of those that a mesh axis runs over, the one named last changes fastest.
Arguments:
- tokens: bfloat16 [4096, 4608], P(('groups', 'cand'), 'tensor'), parts along dimension 0, may hold values from -32 to 32
- pre_gain: bfloat16 [1, 4608], P(None, 'tensor'), may hold values from 0.5 to 2
- w_query: bfloat16 [4608, 4096], P(None, 'tensor'), may hold values from -8 to 8
- w_key: bfloat16 [4608, 2048], P(None, 'tensor'), may hold values from -8 to 8
- w_value: bfloat16 [4608, 2048], P(None, 'tensor'), may hold values from -0.09375 to 0.09375
- w_out: bfloat16 [4096, 4608], P('tensor'), may hold values from -8 to 8
- post_gain: bfloat16 [1, 4608], P(None, 'tensor'), may hold values from 0.5 to 2
- cand_lengths: int32 [32], P('groups'), parts along dimension 0, may hold values from 1 to 128, 1536 in all
- pair_mask: int32 [32, 16], P('groups'), parts along dimension 0, may hold values 0 or 1
Outputs:
- update: bfloat16 [4096, 4608], P(('groups', 'cand'), 'tensor'), parts along dimension 0
There are 2 independent parts, one for each index of `groups`. A program takes and returns all parts, laid end to end along the dimension named above; an argument that names none is the same for every part. Nothing has to cross between parts.
Inputs may be any that keep to these rules, and one draw needn't show every extreme that they name: Candidate c holds real tokens at positions 0 to cand_lengths[c] - 1, padding after; some candidate of every prompt has all 128 slots real. `pair_mask`: entry [a, b] says whether candidate a's tokens may attend to candidate b's; a candidate always attends to itself whatever its diagonal entry.
All inputs are finite; a program needn't handle non-finite values.
Results may differ from a plain program's by a relative error of at most 0.012.
Values may be sent and summed in bfloat16 or wider, within the bound.
No kernel may reach another device: no remote copies, remote signals or barrier semaphores. Data moves between devices by JAX's collectives and lax.ppermute only.
A program may use at most 192 MiB of HBM per device.

v0:
```python
import jax
import jax.numpy as jnp
from jax import lax
from jax.sharding import PartitionSpec as P

HEADS = 32
KV_HEADS = 16
HEAD = 128
CTOK = 128


epsilon = 1e-06


def per_device(
    tokens, pre_gain, w_query, w_key, w_value, w_out, post_gain, cand_lengths, pair_mask
):
    row_count = tokens.shape[0]
    feature_width = w_query.shape[0]
    query_width = w_query.shape[1]
    kv_width = w_key.shape[1]
    head_group = HEADS // KV_HEADS
    kv_local = kv_width // HEAD
    score_scale = HEAD ** (-0.5)
    weights_all = jnp.concatenate([w_query, w_key, w_value], axis=1)
    local_sq = jnp.sum(jnp.square(tokens.astype(jnp.float32)), axis=1)
    outside_sq = lax.psum(local_sq, "tensor")
    scaled = (
        lax.all_gather(tokens, "tensor", axis=1, tiled=True).astype(jnp.float32)
        * lax.all_gather(pre_gain, "tensor", axis=1, tiled=True).astype(jnp.float32)
    ).astype(jnp.bfloat16)
    projected = jnp.dot(scaled, weights_all, preferred_element_type=jnp.float32)
    inverse = lax.rsqrt(outside_sq / feature_width + epsilon)
    projected = (projected * inverse[:, None]).astype(jnp.bfloat16)
    queries = projected[:, :query_width].reshape(row_count, kv_local, head_group, HEAD)
    keys = projected[:, query_width : query_width + kv_width]
    values = projected[:, query_width + kv_width :]
    cand_local = row_count // CTOK
    cand_total = pair_mask.shape[1]
    first_cand = lax.axis_index("cand") * cand_local
    allow_rows = lax.dynamic_slice_in_dim(pair_mask, first_cand, cand_local, 0)
    everyone = jnp.arange(cand_total, dtype=jnp.int32)
    itself = (first_cand + jnp.arange(cand_local, dtype=jnp.int32))[:, None] == everyone[None, :]
    allowed = jnp.where(itself, 1.0, allow_rows.astype(jnp.float32))
    length_float = cand_lengths.astype(jnp.float32)
    start_max = jnp.full((kv_local, head_group, row_count), -1e30, jnp.float32)
    key_block = lax.all_gather(keys, "cand", axis=0, tiled=True)
    value_block = lax.all_gather(values, "cand", axis=0, tiled=True)
    key_rows = key_block.shape[0]
    key_index = jnp.arange(key_rows, dtype=jnp.int32)
    key_cand = key_index // CTOK
    key_pos = (key_index % CTOK).astype(jnp.float32)
    one_hot = (everyone[:, None] == key_cand[None, :]).astype(jnp.float32)
    pair_ok = jnp.dot(allowed, one_hot)
    key_len = jnp.dot(length_float, one_hot)
    usable = (pair_ok > 0.5) & (key_pos < key_len)[None, :]
    usable = jnp.broadcast_to(usable[:, None, :], (cand_local, CTOK, key_rows)).reshape(
        row_count, key_rows
    )
    key_heads = key_block.reshape(key_rows, kv_local, HEAD)
    value_heads = value_block.reshape(key_rows, kv_local, HEAD)
    scores = (
        jnp.einsum("rkgd,nkd->kgrn", queries, key_heads, preferred_element_type=jnp.float32)
        * score_scale
    )
    scores = jnp.where(usable, scores, -1e30)
    new_max = jnp.maximum(start_max, jnp.max(scores, axis=-1))
    probs = jnp.where(usable, jnp.exp(scores - new_max[..., None]), 0.0)
    denominator = jnp.sum(probs, axis=-1)
    contribution = jnp.einsum(
        "kgrn,nkd->kgrd",
        probs.astype(jnp.bfloat16),
        value_heads,
        preferred_element_type=jnp.float32,
    )
    numerator = contribution
    final_max, denominator, numerator = (new_max, denominator, numerator)
    attended = numerator / denominator[..., None]
    attended = (
        jnp.transpose(attended, (2, 0, 1, 3)).reshape(row_count, query_width).astype(jnp.bfloat16)
    )
    gain_wide = post_gain.astype(jnp.float32)
    reduced = lax.psum_scatter(
        lax.dot_general(
            w_out, attended, (((0,), (1,)), ((), ())), preferred_element_type=jnp.float32
        ).astype(jnp.bfloat16),
        "tensor",
        scatter_dimension=0,
        tiled=True,
    ).astype(jnp.float32)
    mixed = reduced.T
    mixed_sq = lax.psum(jnp.sum(mixed * mixed, axis=1), "tensor")
    inverse_post = lax.rsqrt(mixed_sq / feature_width + epsilon)
    update = (mixed * inverse_post[:, None] * gain_wide).astype(jnp.bfloat16)
    return update


def solution(mesh):
    return jax.shard_map(
        per_device,
        mesh=mesh,
        in_specs=(
            P(("groups", "cand"), "tensor"),
            P(None, "tensor"),
            P(None, "tensor"),
            P(None, "tensor"),
            P(None, "tensor"),
            P("tensor", None),
            P(None, "tensor"),
            P("groups"),
            P("groups", None),
        ),
        out_specs=P(("groups", "cand"), "tensor"),
        check_vma=False,
    )
```

profile of v0, /device:TPU:0, one launch (start us, length us, event | category | flops | bytes accessed | tf_op | source)
XLA Modules:
  0.0 254.6 jit_solution(10155382127516871926)
XLA Ops:
  6.5 0.7 all-gather.4.cloned.1.call-update
  7.3 1.6 multiply_reduce_fusion
  8.9 8.4 %psum.14 = f32[512]{0:T(512)S(1)} all-reduce(f32[512]{0:T(512)S(1)} %multiply_reduce_fusion), channel_id=1, replica_groups=mesh['groups'=2,'cand'=4,'tensor'=4] {'tensor'}, use_global_device_ids=true, to_apply=%region_1.0 | all-reduce | flops 512 | bytes 4096 | tf_op jit(solution)/shard_map/psum | solution.py:27
  17.2 5.4 %all_gather.13 = bf16[1,4608]{1,0:T(2,128)(2,1)S(1)} all-gather(bf16[1,1152]{1,0:T(2,128)(2,1)} %param.10), channel_id=1, replica_groups=mesh['groups'=2,'cand'=4,'tensor'=4] {'tensor'}, dimensions={1}, use_global_device_ids=true | all-gather | bytes 11520 | tf_op jit(solution)/shard_map/all_gather | solution.py:30
  22.7 0.1 convert_reduce_fusion
  22.7 26.3 %all-gather.4.cloned.1.call-done = bf16[512,4608]{1,0:T(8,128)(2,1)} async-done(((bf16[512,1152]{1,0:T(8,128)(2,1)}), bf16[512,4608]{1,0:T(8,128)(2,1)}) %all-gather.4.cloned.1.call-update) | async-done | bytes 4718608 | tf_op jit(solution)/shard_map/all_gather | solution.py:29
  49.1 13.9 %multiply_convert_fusion.2 = bf16[512,2048]{1,0:T(8,128)(2,1)S(1)} fusion(bf16[4608,512]{1,0:T(8,128)(2,1)} %param.13, bf16[4608,512]{1,0:T(8,128)(2,1)} %param.12, bf16[4608,1024]{1,0:T(8,128)(2,1)} %param.11, bf16[512,4608]{1,0:T(8,128)(2,1)} %all-gather.4.cloned.1.call-done, f32[4608]{0:T(1024)S(1)} %convert_reduce_fusion, f32[512]{0:T(512)S(1)} %add_rsqrt_fusion.1), kind=kOutput, calls=%fused_computation.17 | convolution fusion | flops 9729474560 | bytes 25710592 | tf_op jit(solution)/shard_map/dot_general | solution.py:32
  63.0 1.3 copy-done
  64.3 1.0 fusion.50
  65.4 0.0 all-gather.8.cloned.1.call-start
  65.4 0.1 fusion.27
  65.6 0.9 fusion.19
  66.5 0.5 copy.15
  67.0 6.4 %broadcast_in_dim.35 = pred[4,128,2048]{1,0,2:T(4,128)(4,1)S(1)} broadcast(pred[4,2048]{0,1:T(8,128)(4,1)S(1)} %copy.15), dimensions={0,2} | broadcast | bytes 1056768 | tf_op jit(solution)/shard_map/broadcast_in_dim | solution.py:57
  73.4 0.5 copy.38
  73.9 1.3 slice.14
  75.2 1.5 reshape.41
  76.8 0.2 reduce-scatter.4.cloned.1.call-start
  77.0 34.1 %all-gather.6.cloned.1.call-done = bf16[2048,512]{1,0:T(8,128)(2,1)} async-done(((bf16[512,512]{1,0:T(8,128)(2,1)}), bf16[2048,512]{1,0:T(8,128)(2,1)}) %all-gather.6.cloned.1.call-update) | async-done | bytes 2097168 | tf_op jit(solution)/shard_map/all_gather | solution.py:47
  111.2 2.5 reshape.40
  113.7 15.4 %fusion = (f32[4,2,512]{2,1,0:T(2,128)S(1)}, f32[4,2048,512,2]{2,1,3,0:T(8,128)}) fusion(pred[512,2048]{0,1:T(8,128)(4,1)S(1)} %bitcast.43, bf16[512,4,2,128]{3,2,1,0:T(2,128)(2,1)} %reshape.41, bf16[2048,4,128,1]{2,1,0,3:T(4,128)(2,1)S(1)} %bitcast.48), kind=kOutput, calls=%fused_computation.2 | convolution fusion | flops 2172645376 | bytes 37765120 | tf_op jit(solution)/shard_map/rkgd,nkd->kgrn/dot_general | solution.py:63
  129.1 15.0 %fusion.1 = f32[4,2,512]{2,1,0:T(2,128)S(1)} fusion(f32[4,2048,512,2]{2,1,3,0:T(8,128)} %get-tuple-element.8, f32[4,2,512]{2,1,0:T(2,128)S(1)} %broadcast_maximum_fusion, pred[512,2048]{0,1:T(8,128)(4,1)S(1)} %bitcast.44), kind=kLoop, calls=%fused_computation.3 | loop fusion | flops 41938944 | bytes 34635776 | tf_op jit(solution)/shard_map/reduce_sum | solution.py:69
  144.1 13.1 %all-gather.8.cloned.1.call-done = bf16[2048,512]{1,0:T(8,128)(2,1)} async-done(((bf16[512,512]{1,0:T(8,128)(2,1)}), bf16[2048,512]{1,0:T(8,128)(2,1)}) %all-gather.8.cloned.1.call-update) | async-done | bytes 2097168 | tf_op jit(solution)/shard_map/all_gather | solution.py:48
  157.2 2.9 %copy.25 = bf16[2048,512]{0,1:T(8,128)(2,1)S(1)} copy(bf16[2048,512]{1,0:T(8,128)(2,1)} %all-gather.8.cloned.1.call-done) | data formatting | bytes 4194304 | tf_op jit(solution)/shard_map/reshape | solution.py:61
  160.2 14.7 %fusion.20 = bf16[512,4,2,128]{0,3,2,1:T(8,128)(2,1)S(1)} fusion(bf16[2048,4,128,1]{0,2,3,1:T(8,128)(2,1)S(1)} %bitcast.47, f32[4,2048,512,2]{2,1,3,0:T(8,128)} %get-tuple-element.8, f32[4,2,512]{2,1,0:T(2,128)S(1)} %broadcast_maximum_fusion, pred[512,2048]{0,1:T(8,128)(4,1)S(1)} %bitcast.45, f32[512,4,2]{0,2,1:T(2,128)S(1)} %bitcast.49), kind=kOutput, calls=%fused_computation.28 | convolution fusion | flops 2190475264 | bytes 37781504 | tf_op jit(solution)/shard_map/kgrn,nkd->kgrd/dot_general | solution.py:70
  174.9 10.5 %fusion.12 = bf16[4608,512]{0,1:T(8,128)(2,1)} fusion(bf16[512,1024]{0,1:T(8,128)(2,1)S(1)} %bitcast.51, bf16[1024,4608]{1,0:T(8,128)(2,1)} %param.14), kind=kOutput, calls=%fused_computation.15 | convolution fusion | flops 4834197504 | bytes 15204352 | tf_op jit(solution)/shard_map/dot_general | solution.py:84
  185.3 6.6 %copy.26 = bf16[4608,512]{1,0:T(8,128)(2,1)} copy(bf16[4608,512]{0,1:T(8,128)(2,1)} %fusion.12) | data formatting | bytes 9437184
  192.0 46.9 %reduce-scatter.4.cloned.1.call-done = bf16[1152,512]{1,0:T(8,128)(2,1)} async-done(((bf16[4608,512]{1,0:T(8,128)(2,1)}), bf16[1152,512]{1,0:T(8,128)(2,1)}) %reduce-scatter.4.cloned.1.call-update) | async-done | bytes 1179664
  238.9 1.7 copy.27
  240.6 0.3 fusion.16
  240.9 5.8 %psum.15 = f32[512]{0:T(512)S(1)} all-reduce(f32[512]{0:T(512)S(1)} %fusion.16), channel_id=1, replica_groups=mesh['groups'=2,'cand'=4,'tensor'=4] {'tensor'}, use_global_device_ids=true, to_apply=%region_6.7 | all-reduce | flops 512 | bytes 4096 | tf_op jit(solution)/shard_map/psum | solution.py:92
  246.7 1.4 fusion.25
  (17 shorter events, 0.2 us)
Async XLA Ops:
  6.5 42.5 %all-gather.4.cloned.1.call-start = ((), (), s32[]{:S(2)}) async-start(), calls=%async_computation.1 | async-start | bytes 5898240 | tf_op jit(solution)/shard_map/all_gather | solution.py:29
  7.3 103.9 %all-gather.6.cloned.1.call-start = ((), (), s32[]{:S(2)}) async-start(), calls=%async_computation.2 | async-start | bytes 2621440 | tf_op jit(solution)/shard_map/all_gather | solution.py:47
  22.7 42.7 %copy-start.2 = (s32[16]{0:T(128)S(1)}, s32[16]{0:T(128)}, u32[]{:S(2)}) copy-start(s32[16]{0:T(128)} %param.16) | copy-start | bytes 196
  63.0 1.3 copy-start
  65.4 91.9 %all-gather.8.cloned.1.call-start = ((), (), s32[]{:S(2)}) async-start(), calls=%async_computation.3 | async-start | bytes 2621440 | tf_op jit(solution)/shard_map/all_gather | solution.py:48
  76.8 162.1 %reduce-scatter.4.cloned.1.call-start = ((), (), s32[]{:S(2)}) async-start(), calls=%async_computation.4 | async-start | bytes 5898240
  185.3 6.7 %copy-start.1 = (bf16[1,1152]{1,0:T(2,128)(2,1)S(1)}, bf16[1,1152]{1,0:T(2,128)(2,1)}, u32[]{:S(2)}) copy-start(bf16[1,1152]{1,0:T(2,128)(2,1)} %param.15) | copy-start | bytes 6916
Sparse Core Ops, SparseCore 0:
  8.9 40.1 all-gather.3
  65.5 45.6 all-gather.5
  112.7 44.4 all-gather.7
  192.1 46.7 reduce-scatter.3
where the time goes:
time: 255 us
  waiting for transfers between devices  121 us (47%)
  matrix products  55.5 us (22%)
  local copies, waits for them, and re-layouts  26.4 us (10%)
  blocking collectives  19.5 us (8%)
  other arithmetic  18.3 us (7%)
  between operations  13.3 us (5%)
    unnamed x5, waiting for transfers between devices  47.6 us
    all_gather x1, waiting for transfers between devices, per_device(): key_block = lax.all_gather(keys, 'cand', axis=0, tiled=True)  34.1 us
    all_gather x1, waiting for transfers between devices, per_device(): lax.all_gather(tokens, 'tensor', axis=1, tiled=True).astype(jnp.float32)  26.3 us
    dot_general x1, matrix products, per_device(): jnp.einsum('rkgd,nkd->kgrn', queries, key_heads, preferred_element_type=j...  15.4 us
    reduce_sum x1, other arithmetic, per_device(): denominator = jnp.sum(probs, axis=-1)  15 us
    dot_general x1, matrix products, per_device(): jnp.einsum('kgrn,nkd->kgrd', probs.astype(jnp.bfloat16), value_heads, pre...  14.7 us
    dot_general x1, matrix products, per_device(): projected = jnp.dot(scaled, weights_all, preferred_element_type=jnp.float32)  13.9 us
    all_gather x1, waiting for transfers between devices, per_device(): value_block = lax.all_gather(values, 'cand', axis=0, tiled=True)  13.1 us
  transfers between devices with their start and end apart: 4, of which 4 were waited for; matrix products, arithmetic and copies ran while one was open for 18% of the time, Pallas kernels for 0%

commit v1 on v0

v1 whole, which is shorter than its diff:
```python
import functools
import math

import jax
import jax.numpy as jnp
from jax import lax
from jax.experimental import pallas as pl
from jax.experimental.pallas import tpu as pltpu
from jax.sharding import PartitionSpec as P

HEADS = 32
KV_HEADS = 16
HEAD = 128
CTOK = 128
GROUP = HEADS // KV_HEADS
MASKED = -1e30
EXP2_SCALE = HEAD ** (-0.5) * math.log2(math.e)

epsilon = 1e-06


def bias_rows(cand_lengths, pair_mask, first_cand, cand_local, key_cand):
    allow_rows = lax.dynamic_slice_in_dim(pair_mask, first_cand, cand_local, 0)
    everyone = jnp.arange(pair_mask.shape[1], dtype=jnp.int32)
    one_hot = (everyone[:, None] == key_cand[None, :]).astype(jnp.float32)
    own = first_cand + jnp.arange(cand_local, dtype=jnp.int32)
    allowed = jnp.dot(allow_rows.astype(jnp.float32), one_hot) > 0.5
    allowed = allowed | (own[:, None] == key_cand[None, :])
    lengths = jnp.dot(cand_lengths.astype(jnp.float32)[None, :], one_hot)
    position = jnp.arange(CTOK, dtype=jnp.int32).astype(jnp.float32)
    inside = position[None, :] < lengths[0][:, None]
    usable = allowed[:, :, None] & inside[None]
    return jnp.where(usable, 0.0, MASKED).reshape(cand_local, key_cand.shape[0] * CTOK)


def project_body(rank_ref, *refs, weights):
    x_refs = refs[:4]
    inverse_ref = refs[4]
    w_refs = refs[5 : 5 + 4 * weights]
    out_ref = refs[-1]
    inverse = inverse_ref[...]
    for i in range(weights):
        total = None
        for k in range(4):
            part = jnp.dot(
                x_refs[k][...], w_refs[4 * i + k][...], preferred_element_type=jnp.float32
            )
            total = part if total is None else total + part
        out_ref[i] = (total * inverse).astype(jnp.bfloat16)


def project(rank, blocks, inverse, weights, width):
    rows, features = blocks[0].shape
    columns = weights[0].shape[1]
    in_specs = [pl.BlockSpec((rows, features), lambda j, r: (0, 0)) for _ in range(4)]
    in_specs.append(pl.BlockSpec((rows, 1), lambda j, r: (0, 0)))
    operands = []
    for w in weights:
        for k in range(4):
            in_specs.append(pl.BlockSpec((features, width), lambda j, r, k=k: (r[k], j)))
            operands.append(w)
    return pl.pallas_call(
        functools.partial(project_body, weights=len(weights)),
        grid_spec=pltpu.PrefetchScalarGridSpec(
            num_scalar_prefetch=1,
            grid=(columns // width,),
            in_specs=in_specs,
            out_specs=pl.BlockSpec((len(weights), rows, width), lambda j, r: (0, 0, j)),
        ),
        out_shape=jax.ShapeDtypeStruct((len(weights), rows, columns), jnp.bfloat16),
        compiler_params=pltpu.CompilerParams(vmem_limit_bytes=56 * 2**20),
        name="project",
    )(rank, *blocks, inverse, *operands)


def attention_body(bias_ref, q_ref, *refs, slots):
    kv_refs = refs[: 2 * slots]
    out_ref = refs[2 * slots]
    rows = q_ref.shape[1]
    nt = (((1,), (1,)), ((), ()))
    for c in range(rows // CTOK):
        here = slice(c * CTOK, (c + 1) * CTOK)
        q = jnp.concatenate([q_ref[0, here, g * HEAD : (g + 1) * HEAD] for g in range(GROUP)], axis=0)
        scores = []
        start = 0
        for s in range(slots):
            k = kv_refs[2 * s][0]
            part = lax.dot_general(q, k, nt, preferred_element_type=jnp.float32)
            scores.append(part * EXP2_SCALE + bias_ref[c : c + 1, start : start + k.shape[0]])
            start += k.shape[0]
        top = functools.reduce(jnp.maximum, [jnp.max(s, axis=1, keepdims=True) for s in scores])
        denominator = None
        numerator = None
        for s in range(slots):
            p = jnp.exp2(scores[s] - top)
            d = jnp.sum(p, axis=1, keepdims=True)
            n = jnp.dot(
                p.astype(jnp.bfloat16), kv_refs[2 * s + 1][0], preferred_element_type=jnp.float32
            )
            denominator = d if denominator is None else denominator + d
            numerator = n if numerator is None else numerator + n
        out = (numerator / denominator).astype(jnp.bfloat16)
        for g in range(GROUP):
            out_ref[here, g * HEAD : (g + 1) * HEAD] = out[g * CTOK : (g + 1) * CTOK]


def attention(bias, queries, slots):
    _, rows, width = queries.shape
    heads = width // (GROUP * HEAD)
    in_specs = [
        pl.BlockSpec(bias.shape, lambda h: (0, 0)),
        pl.BlockSpec((1, rows, GROUP * HEAD), lambda h: (0, 0, h)),
    ]
    operands = []
    for kv in slots:
        for i in range(2):
            in_specs.append(pl.BlockSpec((1, kv.shape[1], HEAD), lambda h, i=i: (i, 0, h)))
            operands.append(kv)
    return pl.pallas_call(
        functools.partial(attention_body, slots=len(slots)),
        grid=(heads,),
        in_specs=in_specs,
        out_specs=pl.BlockSpec((rows, GROUP * HEAD), lambda h: (0, h)),
        out_shape=jax.ShapeDtypeStruct((rows, width), jnp.bfloat16),
        compiler_params=pltpu.CompilerParams(vmem_limit_bytes=56 * 2**20),
        name="attention",
    )(bias, queries, *operands)


def output_body(block_ref, x_ref, w_ref, out_ref):
    out_ref[0] = jnp.dot(x_ref[...], w_ref[...], preferred_element_type=jnp.float32).astype(
        jnp.bfloat16
    )


def output_blocks(block_ids, attended, w_out, features):
    rows, inner = attended.shape
    width = features // 3
    return pl.pallas_call(
        output_body,
        grid_spec=pltpu.PrefetchScalarGridSpec(
            num_scalar_prefetch=1,
            grid=(block_ids.shape[0], 3),
            in_specs=[
                pl.BlockSpec((rows, inner), lambda b, j, r: (0, 0)),
                pl.BlockSpec((inner, width), lambda b, j, r: (0, r[b] * 3 + j)),
            ],
            out_specs=pl.BlockSpec((1, rows, width), lambda b, j, r: (b, 0, j)),
        ),
        out_shape=jax.ShapeDtypeStruct((block_ids.shape[0], rows, features), jnp.bfloat16),
        compiler_params=pltpu.CompilerParams(vmem_limit_bytes=56 * 2**20),
        name="output",
    )(block_ids, attended, w_out)


def swap(x, bit):
    return lax.ppermute(x, "tensor", [(t, t ^ bit) for t in range(4)])


def sum_over_tensor(x):
    return x + swap(x, 1) + (swap(x, 2) + swap(x, 3))


CHUNKS = 2
CAND_AXIS = 4


def per_device_4x4(
    tokens, pre_gain, w_query, w_key, w_value, w_out, post_gain, cand_lengths, pair_mask
):
    row_count, features = tokens.shape
    model_width = w_query.shape[0]
    cand_local = row_count // CTOK
    rank = lax.axis_index("tensor").astype(jnp.int32)
    place = lax.axis_index("cand").astype(jnp.int32)
    ranks = jnp.stack([rank, rank ^ 1, rank ^ 2, rank ^ 3])
    step = row_count // CHUNKS

    wide = tokens.astype(jnp.float32)
    scaled = (wide * pre_gain.astype(jnp.float32)).astype(jnp.bfloat16)
    square_sum = sum_over_tensor(jnp.sum(wide * wide, axis=1))
    inverse = lax.rsqrt(square_sum / model_width + epsilon)[:, None]

    blocks = []
    for c in range(CHUNKS):
        own = scaled[c * step : (c + 1) * step]
        far = swap(own, 2)
        blocks.append([own, swap(own, 1), far, swap(far, 1)])

    key_values = []
    for c in range(CHUNKS):
        key_values.append(
            project(ranks, blocks[c], inverse[c * step : (c + 1) * step], [w_key, w_value], 256)
        )
    right = [(i, i + 1) for i in range(CAND_AXIS - 1)]
    left = [(i + 1, i) for i in range(CAND_AXIS - 1)]
    from_left = [key_values]
    from_right = [key_values]
    for s in range(CAND_AXIS - 1):
        from_left.append([lax.ppermute(x, "cand", right) for x in from_left[-1]])
        from_right.append([lax.ppermute(x, "cand", left) for x in from_right[-1]])
    slots = list(key_values)
    shards = [place]
    for s in range(1, CAND_AXIS):
        shards.append((place - s) % CAND_AXIS)
        for c in range(CHUNKS):
            slots.append(jnp.where(place >= s, from_left[s][c], from_right[CAND_AXIS - s][c]))
    key_cand = jnp.concatenate(
        [s * cand_local + jnp.arange(cand_local, dtype=jnp.int32) for s in shards]
    )
    bias = bias_rows(cand_lengths, pair_mask, place * cand_local, cand_local, key_cand)
    queries = [
        project(ranks, blocks[c], inverse[c * step : (c + 1) * step], [w_query], 512)
        for c in range(CHUNKS)
    ]

    gain_wide = post_gain.astype(jnp.float32)
    other_core = jnp.stack([rank ^ 3, rank ^ 1])
    this_core = jnp.stack([rank ^ 2, rank])
    cands = step // CTOK
    updates = []
    for c in range(CHUNKS):
        attended = attention(bias[c * cands : (c + 1) * cands], queries[c], slots)
        away = swap(output_blocks(other_core, attended, w_out, features), 1)
        home = output_blocks(this_core, attended, w_out, features)
        far = (home[0].astype(jnp.float32) + away[0].astype(jnp.float32)).astype(jnp.bfloat16)
        far = swap(far, 2)
        near = home[1].astype(jnp.float32) + away[1].astype(jnp.float32)
        mixed = near + far.astype(jnp.float32)
        mixed_sq = sum_over_tensor(jnp.sum(mixed * mixed, axis=1))
        inverse_post = lax.rsqrt(mixed_sq / model_width + epsilon)
        updates.append((mixed * inverse_post[:, None] * gain_wide).astype(jnp.bfloat16))
    return jnp.concatenate(updates, axis=0)


def per_device(
    tokens, pre_gain, w_query, w_key, w_value, w_out, post_gain, cand_lengths, pair_mask
):
    row_count = tokens.shape[0]
    model_width, query_width = w_query.shape
    kv_width = w_key.shape[1]
    weights_all = jnp.concatenate([w_query, w_key, w_value], axis=1)
    wide = tokens.astype(jnp.float32)
    square_sum = lax.psum(jnp.sum(wide * wide, axis=1), "tensor")
    scaled = (wide * pre_gain.astype(jnp.float32)).astype(jnp.bfloat16)
    scaled = lax.all_gather(scaled, "tensor", axis=1, tiled=True)
    inverse = lax.rsqrt(square_sum / model_width + epsilon)
    projected = jnp.dot(scaled, weights_all, preferred_element_type=jnp.float32)
    projected = (projected * inverse[:, None]).astype(jnp.bfloat16)
    keys = projected[:, query_width : query_width + kv_width]
    values = projected[:, query_width + kv_width :]
    cand_local = row_count // CTOK
    first_cand = lax.axis_index("cand").astype(jnp.int32) * cand_local
    key_cand = jnp.arange(pair_mask.shape[1], dtype=jnp.int32)
    bias = bias_rows(cand_lengths, pair_mask, first_cand, cand_local, key_cand)
    gathered = lax.all_gather(jnp.stack([keys, values]), "cand", axis=1, tiled=True)
    attended = attention(bias, projected[None, :, :query_width], [gathered])
    partial = jnp.dot(attended, w_out, preferred_element_type=jnp.float32).astype(jnp.bfloat16)
    mixed = lax.psum_scatter(partial.T, "tensor", scatter_dimension=0, tiled=True)
    mixed = mixed.astype(jnp.float32).T
    mixed_sq = lax.psum(jnp.sum(mixed * mixed, axis=1), "tensor")
    inverse_post = lax.rsqrt(mixed_sq / model_width + epsilon)
    return (mixed * inverse_post[:, None] * post_gain.astype(jnp.float32)).astype(jnp.bfloat16)


def solution(mesh):
    small = mesh.shape["tensor"] == 4 and mesh.shape["cand"] == CAND_AXIS
    return jax.shard_map(
        per_device_4x4 if small else per_device,
        mesh=mesh,
        in_specs=(
            P(("groups", "cand"), "tensor"),
            P(None, "tensor"),
            P(None, "tensor"),
            P(None, "tensor"),
            P(None, "tensor"),
            P("tensor", None),
            P(None, "tensor"),
            P("groups"),
            P("groups", None),
        ),
        out_specs=P(("groups", "cand"), "tensor"),
        check_vma=False,
    )
```

time: 255 us -> 217 us (0.85)
  Pallas kernels: 0 us -> 78.9 us
  matrix products: 55.5 us -> 1.42 us
  waiting for transfers between devices: 121 us -> 68.7 us
  starting transfers between devices: 0.31 us -> 48.2 us
  local copies, waits for them, and re-layouts: 26.4 us -> 4.62 us
  blocking collectives: 19.5 us -> 0 us
  between operations: 13.3 us -> 0.35 us
  other arithmetic: 18.3 us -> 13.6 us
    pallas_call x0 -> x10, Pallas kernels: none -> 78.9 us  [the longest x4 32.2 us: project(): pl.pallas_call(functools.partial(project_body, weights=len(weights)), gri...]
    all_gather x3 -> x0, waiting for transfers between devices: 73.6 us -> none  [the longest x1 34.1 us: per_device(): key_block = lax.all_gather(keys, 'cand', axis=0, tiled=True)]
    ppermute x0 -> x31, waiting for transfers between devices: none -> 68.7 us  [the longest x19 50 us: swap(): return lax.ppermute(x, 'tensor', [(t, t ^ bit) for t in range(4)])]
    dot_general x6 -> x2, matrix products: 55.5 us -> 1.42 us  [the longest x1 0.82 us: bias_rows(): allowed = jnp.dot(allow_rows.astype(jnp.float32), one_hot) > 0.5]
    ppermute x0 -> x31, starting transfers between devices: none -> 48.2 us  [the longest x6 27.2 us: per_device_4x4(): from_left.append([lax.ppermute(x, 'cand', right) for x in from_left[-1]])]
    unnamed x5 -> x0, waiting for transfers between devices: 47.6 us -> none
    reduce_sum x3, other arithmetic: 16.9 us -> 2.39 us  [the longest x1 1.7 us: per_device_4x4(): square_sum = sum_over_tensor(jnp.sum(wide * wide, axis=1))]
    psum x2 -> x0, blocking collectives: 14.1 us -> none  [the longest x1 8.37 us: per_device(): outside_sq = lax.psum(local_sq, 'tensor')]
  transfers between devices with their start and end apart: 4 -> 31, of which waited for: 4 -> 12; matrix products, arithmetic and copies ran while one was open for 18% -> 6% of each run, Pallas kernels for 0% -> 29%
where the time goes in v1:
time: 217 us; the launch traced here: 216 us
  Pallas kernels  78.9 us (36%)
  waiting for transfers between devices  68.7 us (32%)
  starting transfers between devices  48.2 us (22%)
  other arithmetic  13.6 us (6%)
  local copies, waits for them, and re-layouts  4.62 us (2%)
    ppermute x19, waiting for transfers between devices, swap(): return lax.ppermute(x, 'tensor', [(t, t ^ bit) for t in range(4)])  50 us
    pallas_call x4, Pallas kernels, project(): pl.pallas_call(functools.partial(project_body, weights=len(weights)), gri...  32.2 us
    pallas_call x4, Pallas kernels, output_blocks(): pl.pallas_call(output_body, grid_spec=pltpu.PrefetchScalarGridSpec(num_sc...  28.6 us
    ppermute x6, starting transfers between devices, per_device_4x4(): from_left.append([lax.ppermute(x, 'cand', right) for x in from_left[-1]])  27.2 us
    ppermute x6, waiting for transfers between devices, per_device_4x4(): from_right.append([lax.ppermute(x, 'cand', left) for x in from_right[-1]])  18.2 us
    pallas_call x2, Pallas kernels, attention(): pl.pallas_call(functools.partial(attention_body, slots=len(slots)), grid=...  18.1 us
    ppermute x19, starting transfers between devices, swap(): return lax.ppermute(x, 'tensor', [(t, t ^ bit) for t in range(4)])  13.3 us
    ppermute x6, starting transfers between devices, per_device_4x4(): from_right.append([lax.ppermute(x, 'cand', left) for x in from_right[-1]])  7.71 us
  transfers between devices with their start and end apart: 31, of which 12 were waited for; matrix products, arithmetic and copies ran while one was open for 6% of the time, Pallas kernels for 29%

profile of v1, /device:TPU:0, one launch (start us, length us, event | category | flops | bytes accessed | tf_op | source)
XLA Modules:
  0.0 215.8 jit_solution(6311651732592378798)
XLA Ops:
  0.7 1.7 fusion.1
  2.5 3.0 %collective-permute-start.1 = (bf16[256,1152]{1,0:T(8,128)(2,1)S(1)}, bf16[256,1152]{1,0:T(8,128)(2,1)S(1)}, u32[]{:S(2)}, u32[]{:S(2)}) collective-permute-start(bf16[256,1152]{1,0:T(8,128)(2,1)S(1)} %get-tuple-element.5.refs_0_), channel_id=1, source_target_pairs={{0,2},{1,3},{2,0},{3,1},{4,6},{5,7},{6,4},{7,5},{8,10},{9,11},{10,... | collective-permute-start | bytes 1769480 | tf_op jit(solution)/shard_map/ppermute | solution.py:157
  7.8 23.1 %collective-permute-done.5 = f32[512]{0:T(512)S(1)} collective-permute-done((f32[512]{0:T(512)S(1)}, f32[512]{0:T(512)S(1)}, u32[]{:S(2)}, u32[]{:S(2)}) %collective-permute-start.5) | collective-permute-done | bytes 2080 | tf_op jit(solution)/shard_map/ppermute | solution.py:157
  33.6 1.5 collective-permute-done.3
  38.4 8.1 %project.5.refs_0_.refs_1_ = bf16[2,256,512]{2,1,0:T(8,128)(2,1)} custom-call(s32[4]{0:T(128)} %pad_add_fusion.2.rank_ref, bf16[256,1152]{1,0:T(8,128)(2,1)} %copy-done.2, bf16[256,1152]{1,0:T(8,128)(2,1)} %copy-done.5, bf16[256,1152]{1,0:T(8,128)(2,1)} %copy-done.4, bf16[256,1152]{1,0:T(8,128)(2,1)} %copy-done.7, f32[256,1]{1,0:T(8,128)} %copy.10.refs_4_, ...), custom_call_target="tpu_custom_call" | custom-call | tf_op jit(solution)/shard_map/project/pallas_call | solution.py:62
  46.6 1.3 collective-permute-start.10
  47.9 4.6 %collective-permute-start.9 = (bf16[2,256,512]{2,1,0:T(8,128)(2,1)}, bf16[2,256,512]{2,1,0:T(8,128)(2,1)S(1)}, u32[]{:S(2)}, u32[]{:S(2)}) collective-permute-start(bf16[2,256,512]{2,1,0:T(8,128)(2,1)} %project.5.refs_0_.refs_1_), channel_id=1, source_target_pairs={{0,4},{4,8},{8,12},{1,5},{5,9},{9,13},{2,6},{6,10},{10,14},{3,7},{... | collective-permute-start | bytes 1572872 | tf_op jit(solution)/shard_map/ppermute | solution.py:200
  52.5 8.2 %project.6.refs_2_.refs_3_ = bf16[2,256,512]{2,1,0:T(8,128)(2,1)} custom-call(s32[4]{0:T(128)} %pad_add_fusion.2.rank_ref, bf16[256,1152]{1,0:T(8,128)(2,1)} %copy-done.3, bf16[256,1152]{1,0:T(8,128)(2,1)} %collective-permute-done.6.refs_1_, bf16[256,1152]{1,0:T(8,128)(2,1)} %copy-done.6, bf16[256,1152]{1,0:T(8,128)(2,1)} %collective-permute-done.8.refs_3_, ...), custom_call_target="tpu_custom_call" | custom-call | tf_op jit(solution)/shard_map/project/pallas_call | solution.py:62
  62.0 4.6 %collective-permute-start.13 = (bf16[2,256,512]{2,1,0:T(8,128)(2,1)}, bf16[2,256,512]{2,1,0:T(8,128)(2,1)S(1)}, u32[]{:S(2)}, u32[]{:S(2)}) collective-permute-start(bf16[2,256,512]{2,1,0:T(8,128)(2,1)} %project.6.refs_2_.refs_3_), channel_id=1, source_target_pairs={{0,4},{4,8},{8,12},{1,5},{5,9},{9,13},{2,6},{6,10},{10,14},{3,7},{... | collective-permute-start | bytes 1572872 | tf_op jit(solution)/shard_map/ppermute | solution.py:200
  68.8 4.6 %collective-permute-start.17 = (bf16[2,256,512]{2,1,0:T(8,128)(2,1)S(1)}, bf16[2,256,512]{2,1,0:T(8,128)(2,1)S(1)}, u32[]{:S(2)}, u32[]{:S(2)}) collective-permute-start(bf16[2,256,512]{2,1,0:T(8,128)(2,1)S(1)} %collective-permute-done.9), channel_id=1, source_target_pairs={{0,4},{4,8},{8,12},{1,5},{5,9},{9,13},{2,6},{6,10},{10,14},{3,7},{... | collective-permute-start | bytes 1572872 | tf_op jit(solution)/shard_map/ppermute | solution.py:200
  73.4 4.2 %collective-permute-done.14 = bf16[2,256,512]{2,1,0:T(8,128)(2,1)S(1)} collective-permute-done((bf16[2,256,512]{2,1,0:T(8,128)(2,1)}, bf16[2,256,512]{2,1,0:T(8,128)(2,1)S(1)}, u32[]{:S(2)}, u32[]{:S(2)}) %collective-permute-start.14) | collective-permute-done | bytes 524320 | tf_op jit(solution)/shard_map/ppermute | solution.py:201
  79.1 4.3 %collective-permute-start.18 = (bf16[2,256,512]{2,1,0:T(8,128)(2,1)S(1)}, bf16[2,256,512]{2,1,0:T(8,128)(2,1)S(1)}, u32[]{:S(2)}, u32[]{:S(2)}) collective-permute-start(bf16[2,256,512]{2,1,0:T(8,128)(2,1)S(1)} %collective-permute-done.13), channel_id=1, source_target_pairs={{0,4},{4,8},{8,12},{1,5},{5,9},{9,13},{2,6},{6,10},{10,14},{3,7},{... | collective-permute-start | bytes 1572872 | tf_op jit(solution)/shard_map/ppermute | solution.py:200
  84.8 8.0 %project.7.q_ref = bf16[1,256,1024]{2,1,0:T(8,128)(2,1)} custom-call(s32[4]{0:T(128)} %pad_add_fusion.2.rank_ref, bf16[256,1152]{1,0:T(8,128)(2,1)} %copy-done.3, bf16[256,1152]{1,0:T(8,128)(2,1)} %collective-permute-done.6.refs_1_, bf16[256,1152]{1,0:T(8,128)(2,1)} %copy-done.6, bf16[256,1152]{1,0:T(8,128)(2,1)} %collective-permute-done.8.refs_3_, ...), custom_call_target="tpu_custom_call" | custom-call | tf_op jit(solution)/shard_map/project/pallas_call | solution.py:62
  92.8 1.3 collective-permute-start.12
  94.2 4.6 %collective-permute-start.19 = (bf16[2,256,512]{2,1,0:T(8,128)(2,1)S(1)}, bf16[2,256,512]{2,1,0:T(8,128)(2,1)S(1)}, u32[]{:S(2)}, u32[]{:S(2)}) collective-permute-start(bf16[2,256,512]{2,1,0:T(8,128)(2,1)S(1)} %collective-permute-done.17), channel_id=1, source_target_pairs={{0,4},{4,8},{8,12},{1,5},{5,9},{9,13},{2,6},{6,10},{10,14},{3,7},{... | collective-permute-start | bytes 1572872 | tf_op jit(solution)/shard_map/ppermute | solution.py:200
  98.7 1.3 collective-permute-done.15
  101.5 4.6 %collective-permute-start.20 = (bf16[2,256,512]{2,1,0:T(8,128)(2,1)S(1)}, bf16[2,256,512]{2,1,0:T(8,128)(2,1)S(1)}, u32[]{:S(2)}, u32[]{:S(2)}) collective-permute-start(bf16[2,256,512]{2,1,0:T(8,128)(2,1)S(1)} %collective-permute-done.18), channel_id=1, source_target_pairs={{0,4},{4,8},{8,12},{1,5},{5,9},{9,13},{2,6},{6,10},{10,14},{3,7},{... | collective-permute-start | bytes 1572872 | tf_op jit(solution)/shard_map/ppermute | solution.py:200
  107.9 3.4 %collective-permute-done.12 = bf16[2,256,512]{2,1,0:T(8,128)(2,1)S(1)} collective-permute-done((bf16[2,256,512]{2,1,0:T(8,128)(2,1)S(1)}, bf16[2,256,512]{2,1,0:T(8,128)(2,1)S(1)}, u32[]{:S(2)}, u32[]{:S(2)}) %collective-permute-start.12) | collective-permute-done | bytes 524320 | tf_op jit(solution)/shard_map/ppermute | solution.py:201
  112.1 9.3 %collective-permute-done.16 = bf16[2,256,512]{2,1,0:T(8,128)(2,1)S(1)} collective-permute-done((bf16[2,256,512]{2,1,0:T(8,128)(2,1)S(1)}, bf16[2,256,512]{2,1,0:T(8,128)(2,1)S(1)}, u32[]{:S(2)}, u32[]{:S(2)}) %collective-permute-start.16) | collective-permute-done | bytes 524320 | tf_op jit(solution)/shard_map/ppermute | solution.py:201
  124.0 9.1 %attention.3.x_ref = bf16[256,1024]{1,0:T(8,128)(2,1)} custom-call(f32[2,2048]{1,0:T(2,128)} %bitcast.37, bf16[1,256,1024]{2,1,0:T(8,128)(2,1)} %project.7.q_ref, bf16[2,256,512]{2,1,0:T(8,128)(2,1)} %project.5.refs_0_.refs_1_, bf16[2,256,512]{2,1,0:T(8,128)(2,1)} %project.5.refs_0_.refs_1_, bf16[2,256,512]{2,1,0:T(8,128)(2,1)} %project.6.refs_2_.refs_3_, ...), custom_call_target="tpu_custom_call" | custom-call | tf_op jit(solution)/shard_map/attention/pallas_call | solution.py:119
  133.1 7.2 %output.7 = bf16[2,256,1152]{2,1,0:T(8,128)(2,1)} custom-call(s32[2]{0:T(128)} %pad_add_fusion.3.block_ref, bf16[256,1024]{1,0:T(8,128)(2,1)} %attention.3.x_ref, bf16[1024,4608]{1,0:T(8,128)(2,1)} %w_ref.7), custom_call_target="tpu_custom_call" | custom-call | tf_op jit(solution)/shard_map/output/pallas_call | solution.py:139
  140.9 7.9 %project.4.q_ref = bf16[1,256,1024]{2,1,0:T(8,128)(2,1)} custom-call(s32[4]{0:T(128)} %pad_add_fusion.2.rank_ref, bf16[256,1152]{1,0:T(8,128)(2,1)} %copy-done.2, bf16[256,1152]{1,0:T(8,128)(2,1)} %copy-done.5, bf16[256,1152]{1,0:T(8,128)(2,1)} %copy-done.4, bf16[256,1152]{1,0:T(8,128)(2,1)} %copy-done.7, f32[256,1]{1,0:T(8,128)} %copy.10.refs_4_, ...), custom_call_target="tpu_custom_call" | custom-call | tf_op jit(solution)/shard_map/project/pallas_call | solution.py:62
  148.8 9.0 %attention.2.x_ref = bf16[256,1024]{1,0:T(8,128)(2,1)} custom-call(f32[2,2048]{1,0:T(2,128)} %bitcast.38, bf16[1,256,1024]{2,1,0:T(8,128)(2,1)} %project.4.q_ref, bf16[2,256,512]{2,1,0:T(8,128)(2,1)} %project.5.refs_0_.refs_1_, bf16[2,256,512]{2,1,0:T(8,128)(2,1)} %project.5.refs_0_.refs_1_, bf16[2,256,512]{2,1,0:T(8,128)(2,1)} %project.6.refs_2_.refs_3_, ...), custom_call_target="tpu_custom_call" | custom-call | tf_op jit(solution)/shard_map/attention/pallas_call | solution.py:119
  157.9 7.1 %output.5 = bf16[2,256,1152]{2,1,0:T(8,128)(2,1)} custom-call(s32[2]{0:T(128)} %pad_add_fusion.3.block_ref, bf16[256,1024]{1,0:T(8,128)(2,1)} %attention.2.x_ref, bf16[1024,4608]{1,0:T(8,128)(2,1)} %w_ref.7), custom_call_target="tpu_custom_call" | custom-call | tf_op jit(solution)/shard_map/output/pallas_call | solution.py:139
  166.2 7.1 %output.4 = bf16[2,256,1152]{2,1,0:T(8,128)(2,1)} custom-call(s32[2]{0:T(128)} %pad_add_fusion.block_ref, bf16[256,1024]{1,0:T(8,128)(2,1)} %attention.2.x_ref, bf16[1024,4608]{1,0:T(8,128)(2,1)} %w_ref.7), custom_call_target="tpu_custom_call" | custom-call | tf_op jit(solution)/shard_map/output/pallas_call | solution.py:139
  173.3 7.1 %output.6 = bf16[2,256,1152]{2,1,0:T(8,128)(2,1)} custom-call(s32[2]{0:T(128)} %pad_add_fusion.block_ref, bf16[256,1024]{1,0:T(8,128)(2,1)} %attention.3.x_ref, bf16[1024,4608]{1,0:T(8,128)(2,1)} %w_ref.7), custom_call_target="tpu_custom_call" | custom-call | tf_op jit(solution)/shard_map/output/pallas_call | solution.py:139
  180.5 1.3 fusion.4
  181.8 1.7 collective-permute-start.27
  184.2 13.9 %collective-permute-done.27 = bf16[256,1152]{1,0:T(8,128)(2,1)S(1)} collective-permute-done((bf16[256,1152]{1,0:T(8,128)(2,1)S(1)}, bf16[256,1152]{1,0:T(8,128)(2,1)S(1)}, u32[]{:S(2)}, u32[]{:S(2)}) %collective-permute-start.27) | collective-permute-done | bytes 589856 | tf_op jit(solution)/shard_map/ppermute | solution.py:157
  198.5 1.7 collective-permute-start.29
  200.4 9.4 %collective-permute-done.22 = bf16[256,1152]{1,0:T(8,128)(2,1)S(1)} collective-permute-done((bf16[256,1152]{1,0:T(8,128)(2,1)S(1)}, bf16[256,1152]{1,0:T(8,128)(2,1)S(1)}, u32[]{:S(2)}, u32[]{:S(2)}) %collective-permute-start.22) | collective-permute-done | bytes 589856 | tf_op jit(solution)/shard_map/ppermute | solution.py:157
  210.5 1.4 collective-permute-start.24
  (106 shorter events, 29.8 us)
Async XLA Ops:
  2.5 44.1 %copy-start.3 = (bf16[256,1152]{1,0:T(8,128)(2,1)}, bf16[256,1152]{1,0:T(8,128)(2,1)S(1)}, u32[]{:S(2)}) copy-start(bf16[256,1152]{1,0:T(8,128)(2,1)S(1)} %get-tuple-element.6.refs_0_) | copy-start | bytes 1769476
  2.5 29.2 %collective-permute-start.1 = (bf16[256,1152]{1,0:T(8,128)(2,1)S(1)}, bf16[256,1152]{1,0:T(8,128)(2,1)S(1)}, u32[]{:S(2)}, u32[]{:S(2)}) collective-permute-start(bf16[256,1152]{1,0:T(8,128)(2,1)S(1)} %get-tuple-element.5.refs_0_), channel_id=1, source_target_pairs={{0,2},{1,3},{2,0},{3,1},{4,6},{5,7},{6,4},{7,5},{8,10},{9,11},{10,... | collective-permute-start | bytes 1769480 | tf_op jit(solution)/shard_map/ppermute | solution.py:157
  5.6 26.2 %collective-permute-start.7 = (bf16[256,1152]{1,0:T(8,128)(2,1)S(1)}, bf16[256,1152]{1,0:T(8,128)(2,1)S(1)}, u32[]{:S(2)}, u32[]{:S(2)}) collective-permute-start(bf16[256,1152]{1,0:T(8,128)(2,1)S(1)} %get-tuple-element.6.refs_0_), channel_id=1, source_target_pairs={{0,2},{1,3},{2,0},{3,1},{4,6},{5,7},{6,4},{7,5},{8,10},{9,11},{10,... | collective-permute-start | bytes 1769480 | tf_op jit(solution)/shard_map/ppermute | solution.py:157
  5.6 25.2 %collective-permute-start.5 = (f32[512]{0:T(512)S(1)}, f32[512]{0:T(512)S(1)}, u32[]{:S(2)}, u32[]{:S(2)}) collective-permute-start(f32[512]{0:T(512)S(1)} %get-tuple-element.7), channel_id=1, source_target_pairs={{0,3},{1,2},{2,1},{3,0},{4,7},{5,6},{6,5},{7,4},{8,11},{9,10},{10,... | collective-permute-start | bytes 6152 | tf_op jit(solution)/shard_map/ppermute | solution.py:157
  6.5 26.4 %collective-permute-start.4 = (f32[512]{0:T(512)S(1)}, f32[512]{0:T(512)S(1)}, u32[]{:S(2)}, u32[]{:S(2)}) collective-permute-start(f32[512]{0:T(512)S(1)} %get-tuple-element.7), channel_id=1, source_target_pairs={{0,2},{1,3},{2,0},{3,1},{4,6},{5,7},{6,4},{7,5},{8,10},{9,11},{10,... | collective-permute-start | bytes 6152 | tf_op jit(solution)/shard_map/ppermute | solution.py:157
  7.6 29.2 %collective-permute-start = (bf16[256,1152]{1,0:T(8,128)(2,1)S(1)}, bf16[256,1152]{1,0:T(8,128)(2,1)S(1)}, u32[]{:S(2)}, u32[]{:S(2)}) collective-permute-start(bf16[256,1152]{1,0:T(8,128)(2,1)S(1)} %get-tuple-element.5.refs_0_), channel_id=1, source_target_pairs={{0,1},{1,0},{2,3},{3,2},{4,5},{5,4},{6,7},{7,6},{8,9},{9,8},{10,11... | collective-permute-start | bytes 1769480 | tf_op jit(solution)/shard_map/ppermute | solution.py:157
  30.9 21.7 %collective-permute-start.6 = (bf16[256,1152]{1,0:T(8,128)(2,1)S(1)}, bf16[256,1152]{1,0:T(8,128)(2,1)}, u32[]{:S(2)}, u32[]{:S(2)}) collective-permute-start(bf16[256,1152]{1,0:T(8,128)(2,1)S(1)} %get-tuple-element.6.refs_0_), channel_id=1, source_target_pairs={{0,1},{1,0},{2,3},{3,2},{4,5},{5,4},{6,7},{7,6},{8,9},{9,8},{10,11... | collective-permute-start | bytes 1769480 | tf_op jit(solution)/shard_map/ppermute | solution.py:157
  31.7 5.1 %collective-permute-start.2 = (bf16[256,1152]{1,0:T(8,128)(2,1)S(1)}, bf16[256,1152]{1,0:T(8,128)(2,1)S(1)}, u32[]{:S(2)}, u32[]{:S(2)}) collective-permute-start(bf16[256,1152]{1,0:T(8,128)(2,1)S(1)} %collective-permute-done.1.refs_2_), channel_id=1, source_target_pairs={{0,1},{1,0},{2,3},{3,2},{4,5},{5,4},{6,7},{7,6},{8,9},{9,8},{10,11... | collective-permute-start | bytes 1769480 | tf_op jit(solution)/shard_map/ppermute | solution.py:157
  31.8 20.7 %collective-permute-start.8 = (bf16[256,1152]{1,0:T(8,128)(2,1)S(1)}, bf16[256,1152]{1,0:T(8,128)(2,1)}, u32[]{:S(2)}, u32[]{:S(2)}) collective-permute-start(bf16[256,1152]{1,0:T(8,128)(2,1)S(1)} %collective-permute-done.7.refs_2_), channel_id=1, source_target_pairs={{0,1},{1,0},{2,3},{3,2},{4,5},{5,4},{6,7},{7,6},{8,9},{9,8},{10,11... | collective-permute-start | bytes 1769480 | tf_op jit(solution)/shard_map/ppermute | solution.py:157
  32.9 2.3 %collective-permute-start.3 = (f32[512]{0:T(512)S(1)}, f32[512]{0:T(512)S(1)}, u32[]{:S(2)}, u32[]{:S(2)}) collective-permute-start(f32[512]{0:T(512)S(1)} %get-tuple-element.7), channel_id=1, source_target_pairs={{0,1},{1,0},{2,3},{3,2},{4,5},{5,4},{6,7},{7,6},{8,9},{9,8},{10,11... | collective-permute-start | bytes 6152 | tf_op jit(solution)/shard_map/ppermute | solution.py:157
  46.6 20.9 %collective-permute-start.10 = (bf16[2,256,512]{2,1,0:T(8,128)(2,1)}, bf16[2,256,512]{2,1,0:T(8,128)(2,1)S(1)}, u32[]{:S(2)}, u32[]{:S(2)}) collective-permute-start(bf16[2,256,512]{2,1,0:T(8,128)(2,1)} %project.5.refs_0_.refs_1_), channel_id=1, source_target_pairs={{4,0},{8,4},{12,8},{5,1},{9,5},{13,9},{6,2},{10,6},{14,10},{7,3},{... | collective-permute-start | bytes 1572872 | tf_op jit(solution)/shard_map/ppermute | solution.py:201
  47.9 20.9 %collective-permute-start.9 = (bf16[2,256,512]{2,1,0:T(8,128)(2,1)}, bf16[2,256,512]{2,1,0:T(8,128)(2,1)S(1)}, u32[]{:S(2)}, u32[]{:S(2)}) collective-permute-start(bf16[2,256,512]{2,1,0:T(8,128)(2,1)} %project.5.refs_0_.refs_1_), channel_id=1, source_target_pairs={{0,4},{4,8},{8,12},{1,5},{5,9},{9,13},{2,6},{6,10},{10,14},{3,7},{... | collective-permute-start | bytes 1572872 | tf_op jit(solution)/shard_map/ppermute | solution.py:200
  60.7 16.9 %collective-permute-start.14 = (bf16[2,256,512]{2,1,0:T(8,128)(2,1)}, bf16[2,256,512]{2,1,0:T(8,128)(2,1)S(1)}, u32[]{:S(2)}, u32[]{:S(2)}) collective-permute-start(bf16[2,256,512]{2,1,0:T(8,128)(2,1)} %project.6.refs_2_.refs_3_), channel_id=1, source_target_pairs={{4,0},{8,4},{12,8},{5,1},{9,5},{13,9},{6,2},{10,6},{14,10},{7,3},{... | collective-permute-start | bytes 1572872 | tf_op jit(solution)/shard_map/ppermute | solution.py:201
  62.0 17.2 %collective-permute-start.13 = (bf16[2,256,512]{2,1,0:T(8,128)(2,1)}, bf16[2,256,512]{2,1,0:T(8,128)(2,1)S(1)}, u32[]{:S(2)}, u32[]{:S(2)}) collective-permute-start(bf16[2,256,512]{2,1,0:T(8,128)(2,1)} %project.6.refs_2_.refs_3_), channel_id=1, source_target_pairs={{0,4},{4,8},{8,12},{1,5},{5,9},{9,13},{2,6},{6,10},{10,14},{3,7},{... | collective-permute-start | bytes 1572872 | tf_op jit(solution)/shard_map/ppermute | solution.py:200
  67.5 25.4 %collective-permute-start.11 = (bf16[2,256,512]{2,1,0:T(8,128)(2,1)S(1)}, bf16[2,256,512]{2,1,0:T(8,128)(2,1)S(1)}, u32[]{:S(2)}, u32[]{:S(2)}) collective-permute-start(bf16[2,256,512]{2,1,0:T(8,128)(2,1)S(1)} %collective-permute-done.10), channel_id=1, source_target_pairs={{4,0},{8,4},{12,8},{5,1},{9,5},{13,9},{6,2},{10,6},{14,10},{7,3},{... | collective-permute-start | bytes 1572872 | tf_op jit(solution)/shard_map/ppermute | solution.py:201
  68.8 25.4 %collective-permute-start.17 = (bf16[2,256,512]{2,1,0:T(8,128)(2,1)S(1)}, bf16[2,256,512]{2,1,0:T(8,128)(2,1)S(1)}, u32[]{:S(2)}, u32[]{:S(2)}) collective-permute-start(bf16[2,256,512]{2,1,0:T(8,128)(2,1)S(1)} %collective-permute-done.9), channel_id=1, source_target_pairs={{0,4},{4,8},{8,12},{1,5},{5,9},{9,13},{2,6},{6,10},{10,14},{3,7},{... | collective-permute-start | bytes 1572872 | tf_op jit(solution)/shard_map/ppermute | solution.py:200
  77.6 22.5 %collective-permute-start.15 = (bf16[2,256,512]{2,1,0:T(8,128)(2,1)S(1)}, bf16[2,256,512]{2,1,0:T(8,128)(2,1)S(1)}, u32[]{:S(2)}, u32[]{:S(2)}) collective-permute-start(bf16[2,256,512]{2,1,0:T(8,128)(2,1)S(1)} %collective-permute-done.14), channel_id=1, source_target_pairs={{4,0},{8,4},{12,8},{5,1},{9,5},{13,9},{6,2},{10,6},{14,10},{7,3},{... | collective-permute-start | bytes 1572872 | tf_op jit(solution)/shard_map/ppermute | solution.py:201
  79.1 22.4 %collective-permute-start.18 = (bf16[2,256,512]{2,1,0:T(8,128)(2,1)S(1)}, bf16[2,256,512]{2,1,0:T(8,128)(2,1)S(1)}, u32[]{:S(2)}, u32[]{:S(2)}) collective-permute-start(bf16[2,256,512]{2,1,0:T(8,128)(2,1)S(1)} %collective-permute-done.13), channel_id=1, source_target_pairs={{0,4},{4,8},{8,12},{1,5},{5,9},{9,13},{2,6},{6,10},{10,14},{3,7},{... | collective-permute-start | bytes 1572872 | tf_op jit(solution)/shard_map/ppermute | solution.py:200
  92.8 18.4 %collective-permute-start.12 = (bf16[2,256,512]{2,1,0:T(8,128)(2,1)S(1)}, bf16[2,256,512]{2,1,0:T(8,128)(2,1)S(1)}, u32[]{:S(2)}, u32[]{:S(2)}) collective-permute-start(bf16[2,256,512]{2,1,0:T(8,128)(2,1)S(1)} %collective-permute-done.11), channel_id=1, source_target_pairs={{4,0},{8,4},{12,8},{5,1},{9,5},{13,9},{6,2},{10,6},{14,10},{7,3},{... | collective-permute-start | bytes 1572872 | tf_op jit(solution)/shard_map/ppermute | solution.py:201
  94.2 28.2 %collective-permute-start.19 = (bf16[2,256,512]{2,1,0:T(8,128)(2,1)S(1)}, bf16[2,256,512]{2,1,0:T(8,128)(2,1)S(1)}, u32[]{:S(2)}, u32[]{:S(2)}) collective-permute-start(bf16[2,256,512]{2,1,0:T(8,128)(2,1)S(1)} %collective-permute-done.17), channel_id=1, source_target_pairs={{0,4},{4,8},{8,12},{1,5},{5,9},{9,13},{2,6},{6,10},{10,14},{3,7},{... | collective-permute-start | bytes 1572872 | tf_op jit(solution)/shard_map/ppermute | solution.py:200
  100.0 21.4 %collective-permute-start.16 = (bf16[2,256,512]{2,1,0:T(8,128)(2,1)S(1)}, bf16[2,256,512]{2,1,0:T(8,128)(2,1)S(1)}, u32[]{:S(2)}, u32[]{:S(2)}) collective-permute-start(bf16[2,256,512]{2,1,0:T(8,128)(2,1)S(1)} %collective-permute-done.15), channel_id=1, source_target_pairs={{4,0},{8,4},{12,8},{5,1},{9,5},{13,9},{6,2},{10,6},{14,10},{7,3},{... | collective-permute-start | bytes 1572872 | tf_op jit(solution)/shard_map/ppermute | solution.py:201
  101.5 21.6 %collective-permute-start.20 = (bf16[2,256,512]{2,1,0:T(8,128)(2,1)S(1)}, bf16[2,256,512]{2,1,0:T(8,128)(2,1)S(1)}, u32[]{:S(2)}, u32[]{:S(2)}) collective-permute-start(bf16[2,256,512]{2,1,0:T(8,128)(2,1)S(1)} %collective-permute-done.18), channel_id=1, source_target_pairs={{0,4},{4,8},{8,12},{1,5},{5,9},{9,13},{2,6},{6,10},{10,14},{3,7},{... | collective-permute-start | bytes 1572872 | tf_op jit(solution)/shard_map/ppermute | solution.py:200
  140.3 40.2 %collective-permute-start.26 = (bf16[2,256,1152]{2,1,0:T(8,128)(2,1)}, bf16[2,256,1152]{2,1,0:T(8,128)(2,1)S(1)}, u32[]{:S(2)}, u32[]{:S(2)}) collective-permute-start(bf16[2,256,1152]{2,1,0:T(8,128)(2,1)} %output.7), channel_id=1, source_target_pairs={{0,1},{1,0},{2,3},{3,2},{4,5},{5,4},{6,7},{7,6},{8,9},{9,8},{10,11... | collective-permute-start | bytes 3538952 | tf_op jit(solution)/shard_map/ppermute | solution.py:157
  165.0 18.5 %collective-permute-start.21 = (bf16[2,256,1152]{2,1,0:T(8,128)(2,1)}, bf16[2,256,1152]{2,1,0:T(8,128)(2,1)S(1)}, u32[]{:S(2)}, u32[]{:S(2)}) collective-permute-start(bf16[2,256,1152]{2,1,0:T(8,128)(2,1)} %output.5), channel_id=1, source_target_pairs={{0,1},{1,0},{2,3},{3,2},{4,5},{5,4},{6,7},{7,6},{8,9},{9,8},{10,11... | collective-permute-start | bytes 3538952 | tf_op jit(solution)/shard_map/ppermute | solution.py:157
  181.8 16.3 %collective-permute-start.27 = (bf16[256,1152]{1,0:T(8,128)(2,1)S(1)}, bf16[256,1152]{1,0:T(8,128)(2,1)S(1)}, u32[]{:S(2)}, u32[]{:S(2)}) collective-permute-start(bf16[256,1152]{1,0:T(8,128)(2,1)S(1)} %fusion.4), channel_id=1, source_target_pairs={{0,2},{1,3},{2,0},{3,1},{4,6},{5,7},{6,4},{7,5},{8,10},{9,11},{10,... | collective-permute-start | bytes 1769480 | tf_op jit(solution)/shard_map/ppermute | solution.py:157
  183.7 26.1 %collective-permute-start.22 = (bf16[256,1152]{1,0:T(8,128)(2,1)S(1)}, bf16[256,1152]{1,0:T(8,128)(2,1)S(1)}, u32[]{:S(2)}, u32[]{:S(2)}) collective-permute-start(bf16[256,1152]{1,0:T(8,128)(2,1)S(1)} %fusion.3), channel_id=1, source_target_pairs={{0,2},{1,3},{2,0},{3,1},{4,6},{5,7},{6,4},{7,5},{8,10},{9,11},{10,... | collective-permute-start | bytes 1769480 | tf_op jit(solution)/shard_map/ppermute | solution.py:157
  198.4 13.5 %collective-permute-start.30 = (f32[256]{0:T(256)S(1)}, f32[256]{0:T(256)S(1)}, u32[]{:S(2)}, u32[]{:S(2)}) collective-permute-start(f32[256]{0:T(256)S(1)} %multiply_reduce_fusion), channel_id=1, source_target_pairs={{0,3},{1,2},{2,1},{3,0},{4,7},{5,6},{6,5},{7,4},{8,11},{9,10},{10,... | collective-permute-start | bytes 3080 | tf_op jit(solution)/shard_map/ppermute | solution.py:157
  198.5 13.5 %collective-permute-start.29 = (f32[256]{0:T(256)S(1)}, f32[256]{0:T(256)S(1)}, u32[]{:S(2)}, u32[]{:S(2)}) collective-permute-start(f32[256]{0:T(256)S(1)} %multiply_reduce_fusion), channel_id=1, source_target_pairs={{0,2},{1,3},{2,0},{3,1},{4,6},{5,7},{6,4},{7,5},{8,10},{9,11},{10,... | collective-permute-start | bytes 3080 | tf_op jit(solution)/shard_map/ppermute | solution.py:157
  200.2 11.9 %collective-permute-start.28 = (f32[256]{0:T(256)S(1)}, f32[256]{0:T(256)S(1)}, u32[]{:S(2)}, u32[]{:S(2)}) collective-permute-start(f32[256]{0:T(256)S(1)} %multiply_reduce_fusion), channel_id=1, source_target_pairs={{0,1},{1,0},{2,3},{3,2},{4,5},{5,4},{6,7},{7,6},{8,9},{9,8},{10,11... | collective-permute-start | bytes 3080 | tf_op jit(solution)/shard_map/ppermute | solution.py:157
  210.1 3.1 %collective-permute-start.25 = (f32[256]{0:T(256)S(1)}, f32[256]{0:T(256)S(1)}, u32[]{:S(2)}, u32[]{:S(2)}) collective-permute-start(f32[256]{0:T(256)S(1)} %multiply_reduce_fusion.1), channel_id=1, source_target_pairs={{0,3},{1,2},{2,1},{3,0},{4,7},{5,6},{6,5},{7,4},{8,11},{9,10},{10,... | collective-permute-start | bytes 3080 | tf_op jit(solution)/shard_map/ppermute | solution.py:157
  210.5 3.6 %collective-permute-start.24 = (f32[256]{0:T(256)S(1)}, f32[256]{0:T(256)S(1)}, u32[]{:S(2)}, u32[]{:S(2)}) collective-permute-start(f32[256]{0:T(256)S(1)} %multiply_reduce_fusion.1), channel_id=1, source_target_pairs={{0,2},{1,3},{2,0},{3,1},{4,6},{5,7},{6,4},{7,5},{8,10},{9,11},{10,... | collective-permute-start | bytes 3080 | tf_op jit(solution)/shard_map/ppermute | solution.py:157
  211.9 2.2 %collective-permute-start.23 = (f32[256]{0:T(256)S(1)}, f32[256]{0:T(256)S(1)}, u32[]{:S(2)}, u32[]{:S(2)}) collective-permute-start(f32[256]{0:T(256)S(1)} %multiply_reduce_fusion.1), channel_id=1, source_target_pairs={{0,1},{1,0},{2,3},{3,2},{4,5},{5,4},{6,7},{7,6},{8,9},{9,8},{10,11... | collective-permute-start | bytes 3080 | tf_op jit(solution)/shard_map/ppermute | solution.py:157
  (14 other events, 216.6 us)

commit v2 on v1

--- a/solution.py
+++ b/solution.py
@@ -68,29 +68,45 @@
             out_specs=pl.BlockSpec((len(weights), rows, width), lambda j, r: (0, 0, j)),
         ),
         out_shape=jax.ShapeDtypeStruct((len(weights), rows, columns), jnp.bfloat16),
-        compiler_params=pltpu.CompilerParams(vmem_limit_bytes=56 * 2**20),
+        compiler_params=pltpu.CompilerParams(vmem_limit_bytes=32 * 2**20),
         name="project",
     )(rank, *blocks, inverse, *operands)
 
 
-def attention_body(bias_ref, q_ref, *refs, slots):
+def scaled_scores(q, k, bias):
+    scores = lax.dot_general(q, k, (((1,), (1,)), ((), ())), preferred_element_type=jnp.float32)
+    return scores * EXP2_SCALE + bias
+
+
+def attention_body(bias_ref, q_ref, *refs, slots, begun, ends):
     kv_refs = refs[: 2 * slots]
-    out_ref = refs[2 * slots]
+    state_refs = refs[2 * slots : 2 * slots + (3 if begun else 0)]
+    out_refs = refs[2 * slots + len(state_refs) :]
     rows = q_ref.shape[1]
-    nt = (((1,), (1,)), ((), ()))
     for c in range(rows // CTOK):
         here = slice(c * CTOK, (c + 1) * CTOK)
-        q = jnp.concatenate([q_ref[0, here, g * HEAD : (g + 1) * HEAD] for g in range(GROUP)], axis=0)
+
+        def stacked(ref):
+            return jnp.concatenate(
+                [ref[here, g * HEAD : (g + 1) * HEAD] for g in range(GROUP)], axis=0
+            )
+
+        q = stacked(q_ref.at[0])
         scores = []
         start = 0
         for s in range(slots):
             k = kv_refs[2 * s][0]
-            part = lax.dot_general(q, k, nt, preferred_element_type=jnp.float32)
-            scores.append(part * EXP2_SCALE + bias_ref[c : c + 1, start : start + k.shape[0]])
+            scores.append(scaled_scores(q, k, bias_ref[c : c + 1, start : start + k.shape[0]]))
             start += k.shape[0]
         top = functools.reduce(jnp.maximum, [jnp.max(s, axis=1, keepdims=True) for s in scores])
         denominator = None
         numerator = None
+        if begun:
+            old_top = stacked(state_refs[1])
+            top = jnp.maximum(old_top[:, :1], top)
+            fade = jnp.exp2(old_top - top)
+            numerator = stacked(state_refs[0]) * fade
+            denominator = stacked(state_refs[2])[:, :1] * fade[:, :1]
         for s in range(slots):
             p = jnp.exp2(scores[s] - top)
             d = jnp.sum(p, axis=1, keepdims=True)
@@ -99,14 +115,21 @@
             )
             denominator = d if denominator is None else denominator + d
             numerator = n if numerator is None else numerator + n
-        out = (numerator / denominator).astype(jnp.bfloat16)
-        for g in range(GROUP):
-            out_ref[here, g * HEAD : (g + 1) * HEAD] = out[g * CTOK : (g + 1) * CTOK]
-
-
-def attention(bias, queries, slots):
+        if ends:
+            results = [(numerator / denominator).astype(jnp.bfloat16)]
+        else:
+            results = [numerator] + [
+                jnp.broadcast_to(x, numerator.shape) for x in (top, denominator)
+            ]
+        for ref, result in zip(out_refs, results):
+            for g in range(GROUP):
+                ref[here, g * HEAD : (g + 1) * HEAD] = result[g * CTOK : (g + 1) * CTOK]
+
+
+def attention(bias, queries, slots, state=(), ends=True):
     _, rows, width = queries.shape
     heads = width // (GROUP * HEAD)
+    own = pl.BlockSpec((rows, GROUP * HEAD), lambda h: (0, h))
     in_specs = [
         pl.BlockSpec(bias.shape, lambda h: (0, 0)),
         pl.BlockSpec((1, rows, GROUP * HEAD), lambda h: (0, 0, h)),
@@ -116,39 +139,41 @@
         for i in range(2):
             in_specs.append(pl.BlockSpec((1, kv.shape[1], HEAD), lambda h, i=i: (i, 0, h)))
             operands.append(kv)
+    if ends:
+        out_specs, out_shape = own, jax.ShapeDtypeStruct((rows, width), jnp.bfloat16)
+    else:
+        out_specs = (own,) * 3
+        out_shape = (jax.ShapeDtypeStruct((rows, width), jnp.float32),) * 3
     return pl.pallas_call(
-        functools.partial(attention_body, slots=len(slots)),
+        functools.partial(attention_body, slots=len(slots), begun=len(state) > 0, ends=ends),
         grid=(heads,),
-        in_specs=in_specs,
-        out_specs=pl.BlockSpec((rows, GROUP * HEAD), lambda h: (0, h)),
-        out_shape=jax.ShapeDtypeStruct((rows, width), jnp.bfloat16),
-        compiler_params=pltpu.CompilerParams(vmem_limit_bytes=56 * 2**20),
+        in_specs=in_specs + [own] * len(state),
+        out_specs=out_specs,
+        out_shape=out_shape,
+        compiler_params=pltpu.CompilerParams(vmem_limit_bytes=40 * 2**20),
         name="attention",
-    )(bias, queries, *operands)
+    )(bias, queries, *operands, *state)
 
 
 def output_body(block_ref, x_ref, w_ref, out_ref):
-    out_ref[0] = jnp.dot(x_ref[...], w_ref[...], preferred_element_type=jnp.float32).astype(
-        jnp.bfloat16
-    )
+    width = out_ref.shape[2]
+    for b in range(out_ref.shape[0]):
+        w = w_ref[:, pl.ds(pl.multiple_of(block_ref[b] * width, HEAD), width)]
+        out_ref[b] = jnp.dot(x_ref[...], w, preferred_element_type=jnp.float32).astype(jnp.bfloat16)
 
 
 def output_blocks(block_ids, attended, w_out, features):
-    rows, inner = attended.shape
-    width = features // 3
+    rows = attended.shape[0]
     return pl.pallas_call(
         output_body,
-        grid_spec=pltpu.PrefetchScalarGridSpec(
-            num_scalar_prefetch=1,
-            grid=(block_ids.shape[0], 3),
-            in_specs=[
-                pl.BlockSpec((rows, inner), lambda b, j, r: (0, 0)),
-                pl.BlockSpec((inner, width), lambda b, j, r: (0, r[b] * 3 + j)),
-            ],
-            out_specs=pl.BlockSpec((1, rows, width), lambda b, j, r: (b, 0, j)),
-        ),
+        in_specs=[
+            pl.BlockSpec(memory_space=pltpu.SMEM),
+            pl.BlockSpec(memory_space=pltpu.VMEM),
+            pl.BlockSpec(memory_space=pltpu.VMEM),
+        ],
+        out_specs=pl.BlockSpec(memory_space=pltpu.VMEM),
         out_shape=jax.ShapeDtypeStruct((block_ids.shape[0], rows, features), jnp.bfloat16),
-        compiler_params=pltpu.CompilerParams(vmem_limit_bytes=56 * 2**20),
+        compiler_params=pltpu.CompilerParams(vmem_limit_bytes=24 * 2**20),
         name="output",
     )(block_ids, attended, w_out)
 
@@ -161,7 +186,8 @@
     return x + swap(x, 1) + (swap(x, 2) + swap(x, 3))
 
 
-CHUNKS = 2
+TOKEN_CHUNKS = (1, 1, 2)
+OUTPUT_CHUNKS = 2
 CAND_AXIS = 4
 
 
@@ -174,56 +200,94 @@
     rank = lax.axis_index("tensor").astype(jnp.int32)
     place = lax.axis_index("cand").astype(jnp.int32)
     ranks = jnp.stack([rank, rank ^ 1, rank ^ 2, rank ^ 3])
-    step = row_count // CHUNKS
 
     wide = tokens.astype(jnp.float32)
     scaled = (wide * pre_gain.astype(jnp.float32)).astype(jnp.bfloat16)
-    square_sum = sum_over_tensor(jnp.sum(wide * wide, axis=1))
+    bounds = [0]
+    for share in TOKEN_CHUNKS:
+        bounds.append(bounds[-1] + row_count * share // sum(TOKEN_CHUNKS))
+    spans = [slice(a, b) for a, b in zip(bounds[:-1], bounds[1:])]
+
+    blocks = []
+    for c, span in enumerate(spans):
+        own = scaled[span]
+        if c == 1:
+            own, square_sum = lax.optimization_barrier((own, square_sum))
+        far = swap(own, 2)
+        if c == 0:
+            squares = jnp.sum(wide * wide, axis=1)
+            squares, own = lax.optimization_barrier((squares, own))
+            square_sum = sum_over_tensor(squares)
+        blocks.append([own, swap(own, 1), far, swap(far, 1)])
     inverse = lax.rsqrt(square_sum / model_width + epsilon)[:, None]
 
-    blocks = []
-    for c in range(CHUNKS):
-        own = scaled[c * step : (c + 1) * step]
-        far = swap(own, 2)
-        blocks.append([own, swap(own, 1), far, swap(far, 1)])
-
-    key_values = []
-    for c in range(CHUNKS):
-        key_values.append(
-            project(ranks, blocks[c], inverse[c * step : (c + 1) * step], [w_key, w_value], 256)
-        )
-    right = [(i, i + 1) for i in range(CAND_AXIS - 1)]
-    left = [(i + 1, i) for i in range(CAND_AXIS - 1)]
-    from_left = [key_values]
-    from_right = [key_values]
-    for s in range(CAND_AXIS - 1):
-        from_left.append([lax.ppermute(x, "cand", right) for x in from_left[-1]])
-        from_right.append([lax.ppermute(x, "cand", left) for x in from_right[-1]])
-    slots = list(key_values)
-    shards = [place]
-    for s in range(1, CAND_AXIS):
-        shards.append((place - s) % CAND_AXIS)
-        for c in range(CHUNKS):
-            slots.append(jnp.where(place >= s, from_left[s][c], from_right[CAND_AXIS - s][c]))
+    key_values = [
+        project(ranks, blocks[c], inverse[span], [w_key, w_value], 256)
+        for c, span in enumerate(spans)
+    ]
+    def outer(parts):
+        return [lax.ppermute(x, "cand", [(0, 1), (1, 0), (2, 3), (3, 2)]) for x in parts]
+
+    def inner(parts):
+        return [lax.ppermute(x, "cand", [(0, 0), (1, 2), (2, 1), (3, 3)]) for x in parts]
+
+    outer_1 = outer(key_values)
+    inner_1 = inner(key_values)
+    outer_2 = outer(inner_1)
+    inner_2 = inner(outer_1)
+    outer_3 = outer(inner_2)
+    at_end = (place == 0) | (place == CAND_AXIS - 1)
+
+    def joined(parts, others):
+        return jnp.where(at_end, jnp.concatenate(parts, axis=1), jnp.concatenate(others, axis=1))
+
+    slots = [
+        jnp.concatenate(key_values, axis=1),
+        jnp.concatenate(outer_1, axis=1),
+        joined(outer_2, inner_1),
+    ]
+    last_slot = joined(outer_3, inner_2)
+    high = place >= 2
+    shards = [
+        place,
+        place ^ 1,
+        jnp.where(high, 1, 2),
+        jnp.where(high, 0, 3),
+    ]
     key_cand = jnp.concatenate(
         [s * cand_local + jnp.arange(cand_local, dtype=jnp.int32) for s in shards]
     )
     bias = bias_rows(cand_lengths, pair_mask, place * cand_local, cand_local, key_cand)
-    queries = [
-        project(ranks, blocks[c], inverse[c * step : (c + 1) * step], [w_query], 512)
-        for c in range(CHUNKS)
-    ]
+    queries = jnp.concatenate(
+        [
+            project(ranks, blocks[c], inverse[span], [w_query], 512)
+            for c, span in enumerate(spans)
+        ],
+        axis=1,
+    )
+    seen = 3 * row_count
+    state = attention(bias[:, :seen], queries, slots, ends=False)
+    state, last_slot = lax.optimization_barrier((state, last_slot))
 
     gain_wide = post_gain.astype(jnp.float32)
     other_core = jnp.stack([rank ^ 3, rank ^ 1])
     this_core = jnp.stack([rank ^ 2, rank])
+    step = row_count // OUTPUT_CHUNKS
     cands = step // CTOK
     updates = []
-    for c in range(CHUNKS):
-        attended = attention(bias[c * cands : (c + 1) * cands], queries[c], slots)
+    for c in range(OUTPUT_CHUNKS):
+        span = slice(c * step, (c + 1) * step)
+        attended = attention(
+            bias[c * cands : (c + 1) * cands, seen:],
+            queries[:, span],
+            [last_slot],
+            state=[x[span] for x in state],
+        )
         away = swap(output_blocks(other_core, attended, w_out, features), 1)
         home = output_blocks(this_core, attended, w_out, features)
         far = (home[0].astype(jnp.float32) + away[0].astype(jnp.float32)).astype(jnp.bfloat16)
+        if c + 1 < OUTPUT_CHUNKS:
+            far, last_slot = lax.optimization_barrier((far, last_slot))
         far = swap(far, 2)
         near = home[1].astype(jnp.float32) + away[1].astype(jnp.float32)
         mixed = near + far.astype(jnp.float32)

time: 217 us -> 206 us (0.949)
  local copies, waits for them, and re-layouts: 4.62 us -> 29.3 us
  Pallas kernels: 78.9 us -> 56.1 us
  waiting for transfers between devices: 68.7 us -> 54.7 us
  starting transfers between devices: 48.2 us -> 50.4 us
    unnamed x33 -> x47, local copies, waits for them, and re-layouts: 2.92 us -> 24.2 us
    pallas_call x6 -> x7, Pallas kernels: 46.7 us -> 30.1 us  [the longest x3 21.8 us: attention(): pl.pallas_call(functools.partial(attention_body, slots=len(slots), begun=...]
    ppermute x19 -> x22, waiting for transfers between devices: 50 us -> 42.8 us  [swap(): return lax.ppermute(x, 'tensor', [(t, t ^ bit) for t in range(4)])]
    ppermute x12 -> x15, waiting for transfers between devices: 18.7 us -> 11.9 us  [the longest x9 11.9 us: outer(): lax.ppermute(x, 'cand', [(0, 1), (1, 0), (2, 3), (3, 2)])]
    pallas_call x4 -> x6, Pallas kernels: 32.2 us -> 26 us  [project(): pl.pallas_call(functools.partial(project_body, weights=len(weights)), gri...]
    slice x4 -> x12, local copies, waits for them, and re-layouts: 1.7 us -> 4.99 us  [the longest x5 3.56 us: per_device_4x4(): inverse[span]]
    concatenate x0 -> x4, other arithmetic: none -> 3.25 us  [the longest x1 1.25 us: per_device_4x4(): jnp.concatenate(outer_1, axis=1)]
    select_n x6 -> x2, other arithmetic: 5.19 us -> 2.97 us  [joined(): jnp.where(at_end, jnp.concatenate(parts, axis=1), jnp.concatenate(others,...]
  transfers between devices with their start and end apart: 31 -> 37, of which waited for: 12 -> 7; matrix products, arithmetic and copies ran while one was open for 6% -> 6% of each run, Pallas kernels for 29% -> 21%
where the time goes in v2:
time: 206 us; the launch traced here: 204 us
  Pallas kernels  56.1 us (27%)
  waiting for transfers between devices  54.7 us (27%)
  starting transfers between devices  50.4 us (24%)
  local copies, waits for them, and re-layouts  29.3 us (14%)
  other arithmetic  12.4 us (6%)
    ppermute x22, waiting for transfers between devices, swap(): return lax.ppermute(x, 'tensor', [(t, t ^ bit) for t in range(4)])  42.8 us
    pallas_call x6, Pallas kernels, project(): pl.pallas_call(functools.partial(project_body, weights=len(weights)), gri...  26 us
    unnamed x47, local copies, waits for them, and re-layouts  24.2 us
    pallas_call x3, Pallas kernels, attention(): pl.pallas_call(functools.partial(attention_body, slots=len(slots), begun=...  21.8 us
    ppermute x9, starting transfers between devices, outer(): lax.ppermute(x, 'cand', [(0, 1), (1, 0), (2, 3), (3, 2)])  17.9 us
    ppermute x6, starting transfers between devices, inner(): lax.ppermute(x, 'cand', [(0, 0), (1, 2), (2, 1), (3, 3)])  17.2 us
    ppermute x22, starting transfers between devices, swap(): return lax.ppermute(x, 'tensor', [(t, t ^ bit) for t in range(4)])  15.3 us
    ppermute x9, waiting for transfers between devices, outer(): lax.ppermute(x, 'cand', [(0, 1), (1, 0), (2, 3), (3, 2)])  11.9 us
  transfers between devices with their start and end apart: 37, of which 7 were waited for; matrix products, arithmetic and copies ran while one was open for 6% of the time, Pallas kernels for 21%

profile of v2, /device:TPU:0, one launch (start us, length us, event | category | flops | bytes accessed | tf_op | source)
XLA Modules:
  0.0 204.3 jit_solution(11067227086042795173)
XLA Ops:
  2.5 3.0 %collective-permute-start.10 = (bf16[256,1152]{1,0:T(8,128)(2,1)S(1)}, bf16[256,1152]{1,0:T(8,128)(2,1)S(1)}, u32[]{:S(2)}, u32[]{:S(2)}) collective-permute-start(bf16[256,1152]{1,0:T(8,128)(2,1)S(1)} %slice.113.refs_0_), channel_id=1, source_target_pairs={{0,2},{1,3},{2,0},{3,1},{4,6},{5,7},{6,4},{7,5},{8,10},{9,11},{10,... | collective-permute-start | bytes 1769480 | tf_op jit(solution)/shard_map/ppermute | solution.py:182
  8.0 10.9 %collective-permute-done.10.refs_2_ = bf16[256,1152]{1,0:T(8,128)(2,1)S(1)} collective-permute-done((bf16[256,1152]{1,0:T(8,128)(2,1)S(1)}, bf16[256,1152]{1,0:T(8,128)(2,1)S(1)}, u32[]{:S(2)}, u32[]{:S(2)}) %collective-permute-start.10) | collective-permute-done | bytes 589856 | tf_op jit(solution)/shard_map/ppermute | solution.py:182
  21.9 2.3 %copy-done.2 = bf16[4608,512]{1,0:T(8,128)(2,1)S(1)} copy-done((bf16[4608,512]{1,0:T(8,128)(2,1)S(1)}, bf16[4608,512]{1,0:T(8,128)(2,1)}, u32[]{:S(2)}) %copy-start.2) | copy-done | bytes 4718616
  24.2 2.3 %copy-done.5 = bf16[4608,512]{1,0:T(8,128)(2,1)S(1)} copy-done((bf16[4608,512]{1,0:T(8,128)(2,1)S(1)}, bf16[4608,512]{1,0:T(8,128)(2,1)}, u32[]{:S(2)}) %copy-start.5) | copy-done | bytes 4718616
  27.5 4.5 %project.11 = bf16[2,256,512]{2,1,0:T(8,128)(2,1)S(1)} custom-call(s32[4]{0:T(128)S(1)} %pad_add_fusion.2.rank_ref, bf16[256,1152]{1,0:T(8,128)(2,1)S(1)} %slice.113.refs_0_, bf16[256,1152]{1,0:T(8,128)(2,1)S(1)} %collective-permute-done.9.refs_1_, bf16[256,1152]{1,0:T(8,128)(2,1)S(1)} %collective-permute-done.10.refs_2_, ...), custom_call_target="tpu_custom_call" | custom-call | tf_op jit(solution)/shard_map/project/pallas_call | solution.py:62
  37.1 6.4 %collective-permute-done.7.refs_2_ = bf16[128,1152]{1,0:T(8,128)(2,1)} collective-permute-done((bf16[128,1152]{1,0:T(8,128)(2,1)S(1)}, bf16[128,1152]{1,0:T(8,128)(2,1)}, u32[]{:S(2)}, u32[]{:S(2)}) %collective-permute-start.7) | collective-permute-done | bytes 294944 | tf_op jit(solution)/shard_map/ppermute | solution.py:182
  43.4 2.3 %copy-done.3 = bf16[4608,512]{1,0:T(8,128)(2,1)S(1)} copy-done((bf16[4608,512]{1,0:T(8,128)(2,1)S(1)}, bf16[4608,512]{1,0:T(8,128)(2,1)}, u32[]{:S(2)}) %copy-start.3) | copy-done | bytes 4718616
  45.8 2.3 %copy-done.6 = bf16[4608,512]{1,0:T(8,128)(2,1)S(1)} copy-done((bf16[4608,512]{1,0:T(8,128)(2,1)S(1)}, bf16[4608,512]{1,0:T(8,128)(2,1)}, u32[]{:S(2)}) %copy-start.6) | copy-done | bytes 4718616
  48.1 4.5 %project.9 = bf16[2,128,512]{2,1,0:T(8,128)(2,1)} custom-call(s32[4]{0:T(128)S(1)} %pad_add_fusion.2.rank_ref, bf16[128,1152]{1,0:T(8,128)(2,1)S(1)} %get-tuple-element.18.refs_0_, bf16[128,1152]{1,0:T(8,128)(2,1)} %collective-permute-done.refs_1_, bf16[128,1152]{1,0:T(8,128)(2,1)} %collective-permute-done.1.refs_2_, ...), custom_call_target="tpu_custom_call" | custom-call | tf_op jit(solution)/shard_map/project/pallas_call | solution.py:62
  54.5 5.4 %collective-permute-start.25 = (bf16[2,256,512]{2,1,0:T(8,128)(2,1)}, bf16[2,256,512]{2,1,0:T(8,128)(2,1)}, u32[]{:S(2)}, u32[]{:S(2)}) collective-permute-start(bf16[2,256,512]{2,1,0:T(8,128)(2,1)} %collective-permute-done.14), channel_id=1, source_target_pairs={{0,0},{4,8},{8,4},{12,12},{1,1},{5,9},{9,5},{13,13},{2,2},{6,10},{... | collective-permute-start | bytes 1572872 | tf_op jit(solution)/shard_map/ppermute | solution.py:232
  62.0 3.6 %collective-permute-start.15 = (bf16[2,128,512]{2,1,0:T(8,128)(2,1)}, bf16[2,128,512]{2,1,0:T(8,128)(2,1)}, u32[]{:S(2)}, u32[]{:S(2)}) collective-permute-start(bf16[2,128,512]{2,1,0:T(8,128)(2,1)} %project.9), channel_id=1, source_target_pairs={{0,0},{4,8},{8,4},{12,12},{1,1},{5,9},{9,5},{13,13},{2,2},{6,10},{... | collective-permute-start | bytes 786440 | tf_op jit(solution)/shard_map/ppermute | solution.py:232
  65.6 2.3 %copy-done.4 = bf16[4608,512]{1,0:T(8,128)(2,1)S(1)} copy-done((bf16[4608,512]{1,0:T(8,128)(2,1)S(1)}, bf16[4608,512]{1,0:T(8,128)(2,1)}, u32[]{:S(2)}) %copy-start.4) | copy-done | bytes 4718616
  67.9 2.3 %copy-done.7 = bf16[4608,512]{1,0:T(8,128)(2,1)S(1)} copy-done((bf16[4608,512]{1,0:T(8,128)(2,1)S(1)}, bf16[4608,512]{1,0:T(8,128)(2,1)}, u32[]{:S(2)}) %copy-start.7) | copy-done | bytes 4718616
  71.1 4.6 %project.10 = bf16[2,128,512]{2,1,0:T(8,128)(2,1)} custom-call(s32[4]{0:T(128)S(1)} %pad_add_fusion.2.rank_ref, bf16[128,1152]{1,0:T(8,128)(2,1)S(1)} %get-tuple-element.21.refs_0_, bf16[128,1152]{1,0:T(8,128)(2,1)} %collective-permute-done.6.refs_1_, bf16[128,1152]{1,0:T(8,128)(2,1)} %collective-permute-done.7.refs_2_, ...), custom_call_target="tpu_custom_call" | custom-call | tf_op jit(solution)/shard_map/project/pallas_call | solution.py:62
  76.2 3.6 %collective-permute-start.17 = (bf16[2,128,512]{2,1,0:T(8,128)(2,1)}, bf16[2,128,512]{2,1,0:T(8,128)(2,1)}, u32[]{:S(2)}, u32[]{:S(2)}) collective-permute-start(bf16[2,128,512]{2,1,0:T(8,128)(2,1)} %project.10), channel_id=1, source_target_pairs={{0,0},{4,8},{8,4},{12,12},{1,1},{5,9},{9,5},{13,13},{2,2},{6,10},{... | collective-permute-start | bytes 786440 | tf_op jit(solution)/shard_map/ppermute | solution.py:232
  80.5 3.7 %copy-done = bf16[4608,1024]{1,0:T(8,128)(2,1)S(1)} copy-done((bf16[4608,1024]{1,0:T(8,128)(2,1)S(1)}, bf16[4608,1024]{1,0:T(8,128)(2,1)}, u32[]{:S(2)}) %copy-start) | copy-done | bytes 9437208
  84.1 4.3 %project.6 = bf16[1,128,1024]{2,1,0:T(8,128)(2,1)S(1)} custom-call(s32[4]{0:T(128)S(1)} %pad_add_fusion.2.rank_ref, bf16[128,1152]{1,0:T(8,128)(2,1)S(1)} %get-tuple-element.18.refs_0_, bf16[128,1152]{1,0:T(8,128)(2,1)} %collective-permute-done.refs_1_, bf16[128,1152]{1,0:T(8,128)(2,1)} %collective-permute-done.1.refs_2_, ...), custom_call_target="tpu_custom_call" | custom-call | tf_op jit(solution)/shard_map/project/pallas_call | solution.py:62
  88.5 3.7 %copy-done.1 = bf16[4608,1024]{1,0:T(8,128)(2,1)S(1)} copy-done((bf16[4608,1024]{1,0:T(8,128)(2,1)S(1)}, bf16[4608,1024]{1,0:T(8,128)(2,1)}, u32[]{:S(2)}) %copy-start.1) | copy-done | bytes 9437208
  92.1 3.8 %project.7 = bf16[1,128,1024]{2,1,0:T(8,128)(2,1)S(1)} custom-call(s32[4]{0:T(128)S(1)} %pad_add_fusion.2.rank_ref, bf16[128,1152]{1,0:T(8,128)(2,1)S(1)} %get-tuple-element.21.refs_0_, bf16[128,1152]{1,0:T(8,128)(2,1)} %collective-permute-done.6.refs_1_, bf16[128,1152]{1,0:T(8,128)(2,1)} %collective-permute-done.7.refs_2_, ...), custom_call_target="tpu_custom_call" | custom-call | tf_op jit(solution)/shard_map/project/pallas_call | solution.py:62
  96.0 2.6 %collective-permute-start.16 = (bf16[2,128,512]{2,1,0:T(8,128)(2,1)}, bf16[2,128,512]{2,1,0:T(8,128)(2,1)S(1)}, u32[]{:S(2)}, u32[]{:S(2)}) collective-permute-start(bf16[2,128,512]{2,1,0:T(8,128)(2,1)} %collective-permute-done.15), channel_id=1, source_target_pairs={{0,4},{4,0},{8,12},{12,8},{1,5},{5,1},{9,13},{13,9},{2,6},{6,2},{1... | collective-permute-start | bytes 786440 | tf_op jit(solution)/shard_map/ppermute | solution.py:229
  99.5 4.4 %project.8.q_ref = bf16[1,256,1024]{2,1,0:T(8,128)(2,1)S(1)} custom-call(s32[4]{0:T(128)S(1)} %pad_add_fusion.2.rank_ref, bf16[256,1152]{1,0:T(8,128)(2,1)S(1)} %slice.113.refs_0_, bf16[256,1152]{1,0:T(8,128)(2,1)S(1)} %collective-permute-done.9.refs_1_, bf16[256,1152]{1,0:T(8,128)(2,1)S(1)} %collective-permute-done.10.refs_2_, ...), custom_call_target="tpu_custom_call" | custom-call | tf_op jit(solution)/shard_map/project/pallas_call | solution.py:62
  107.1 4.9 %collective-permute-start.26 = (bf16[2,256,512]{2,1,0:T(8,128)(2,1)}, bf16[2,256,512]{2,1,0:T(8,128)(2,1)S(1)}, u32[]{:S(2)}, u32[]{:S(2)}) collective-permute-start(bf16[2,256,512]{2,1,0:T(8,128)(2,1)} %collective-permute-done.25), channel_id=1, source_target_pairs={{0,4},{4,0},{8,12},{12,8},{1,5},{5,1},{9,13},{13,9},{2,6},{6,2},{1... | collective-permute-start | bytes 1572872 | tf_op jit(solution)/shard_map/ppermute | solution.py:229
  113.3 3.9 %collective-permute-start.22 = (bf16[2,128,512]{2,1,0:T(8,128)(2,1)S(1)}, bf16[2,128,512]{2,1,0:T(8,128)(2,1)S(1)}, u32[]{:S(2)}, u32[]{:S(2)}) collective-permute-start(bf16[2,128,512]{2,1,0:T(8,128)(2,1)S(1)} %collective-permute-done.21), channel_id=1, source_target_pairs={{0,4},{4,0},{8,12},{12,8},{1,5},{5,1},{9,13},{13,9},{2,6},{6,2},{1... | collective-permute-start | bytes 786440 | tf_op jit(solution)/shard_map/ppermute | solution.py:229
  117.1 3.7 %collective-permute-start.24 = (bf16[2,128,512]{2,1,0:T(8,128)(2,1)S(1)}, bf16[2,128,512]{2,1,0:T(8,128)(2,1)S(1)}, u32[]{:S(2)}, u32[]{:S(2)}) collective-permute-start(bf16[2,128,512]{2,1,0:T(8,128)(2,1)S(1)} %collective-permute-done.23), channel_id=1, source_target_pairs={{0,4},{4,0},{8,12},{12,8},{1,5},{5,1},{9,13},{13,9},{2,6},{6,2},{1... | collective-permute-start | bytes 786440 | tf_op jit(solution)/shard_map/ppermute | solution.py:229
  122.2 11.9 %collective-permute-done.18 = bf16[2,128,512]{2,1,0:T(8,128)(2,1)S(1)} collective-permute-done((bf16[2,128,512]{2,1,0:T(8,128)(2,1)}, bf16[2,128,512]{2,1,0:T(8,128)(2,1)S(1)}, u32[]{:S(2)}, u32[]{:S(2)}) %collective-permute-start.18) | collective-permute-done | bytes 262176 | tf_op jit(solution)/shard_map/ppermute | solution.py:229
  135.5 11.8 %attention.3 = (f32[512,1024]{1,0:T(8,128)S(1)}, f32[512,1024]{1,0:T(8,128)S(1)}, f32[512,1024]{1,0:T(8,128)S(1)}) custom-call(f32[4,1536]{1,0:T(4,128)S(1)} %copy-done.13, bf16[1,512,1024]{2,1,0:T(8,128)(2,1)S(1)} %pad_maximum_fusion.1.q_ref, bf16[2,512,512]{2,1,0:T(8,128)(2,1)S(1)} %pad_maximum_fusion.2.refs_0_.refs_1_, ...), custom_call_target="tpu_custom_call" | custom-call | tf_op jit(solution)/shard_map/attention/pallas_call | solution.py:147
  150.6 4.9 %attention.4.x_ref = bf16[256,1024]{1,0:T(8,128)(2,1)S(1)} custom-call(f32[2,512]{1,0:T(2,128)S(1)} %get-tuple-element.41.bias_ref, bf16[1,256,1024]{2,1,0:T(8,128)(2,1)S(1)} %copy-done.8, bf16[2,512,512]{2,1,0:T(8,128)(2,1)S(1)} %maximum_select_fusion.1.refs_0_.refs_1_, bf16[2,512,512]{2,1,0:T(8,128)(2,1)S(1)} %maximum_select_fusion.1.refs_0_.refs_1_, ...), custom_call_target="tpu_custom_call" | custom-call | tf_op jit(solution)/shard_map/attention/pallas_call | solution.py:147
  155.6 2.1 %output.5 = bf16[2,256,1152]{2,1,0:T(8,128)(2,1)S(1)} custom-call(s32[2]{0:T(128)S(1)} %pad_add_fusion.3.block_ref, bf16[256,1024]{1,0:T(8,128)(2,1)S(1)} %attention.4.x_ref, bf16[1024,4608]{1,0:T(8,128)(2,1)S(1)} %bitcast.42), custom_call_target="tpu_custom_call" | custom-call | tf_op jit(solution)/shard_map/output/pallas_call | solution.py:167
  160.7 5.1 %attention.5.x_ref = bf16[256,1024]{1,0:T(8,128)(2,1)S(1)} custom-call(f32[2,512]{1,0:T(2,128)S(1)} %get-tuple-element.42.bias_ref, bf16[1,256,1024]{2,1,0:T(8,128)(2,1)S(1)} %project.8.q_ref, bf16[2,512,512]{2,1,0:T(8,128)(2,1)S(1)} %maximum_select_fusion.1.refs_0_.refs_1_, bf16[2,512,512]{2,1,0:T(8,128)(2,1)S(1)} %maximum_select_fusion.1.refs_0_.refs_1_, ...), custom_call_target="tpu_custom_call" | custom-call | tf_op jit(solution)/shard_map/attention/pallas_call | solution.py:147
  165.8 2.1 %output.7 = bf16[2,256,1152]{2,1,0:T(8,128)(2,1)S(1)} custom-call(s32[2]{0:T(128)S(1)} %pad_add_fusion.3.block_ref, bf16[256,1024]{1,0:T(8,128)(2,1)S(1)} %attention.5.x_ref, bf16[1024,4608]{1,0:T(8,128)(2,1)S(1)} %bitcast.42), custom_call_target="tpu_custom_call" | custom-call | tf_op jit(solution)/shard_map/output/pallas_call | solution.py:167
  172.6 13.9 %collective-permute-done.28 = bf16[256,1152]{1,0:T(8,128)(2,1)S(1)} collective-permute-done((bf16[256,1152]{1,0:T(8,128)(2,1)S(1)}, bf16[256,1152]{1,0:T(8,128)(2,1)S(1)}, u32[]{:S(2)}, u32[]{:S(2)}) %collective-permute-start.28) | collective-permute-done | bytes 589856 | tf_op jit(solution)/shard_map/ppermute | solution.py:182
  189.0 9.5 %collective-permute-done.33 = bf16[256,1152]{1,0:T(8,128)(2,1)S(1)} collective-permute-done((bf16[256,1152]{1,0:T(8,128)(2,1)S(1)}, bf16[256,1152]{1,0:T(8,128)(2,1)S(1)}, u32[]{:S(2)}, u32[]{:S(2)}) %collective-permute-start.33) | collective-permute-done | bytes 589856 | tf_op jit(solution)/shard_map/ppermute | solution.py:182
  (147 shorter events, 47.2 us)
Async XLA Ops:
  2.5 16.4 %collective-permute-start.10 = (bf16[256,1152]{1,0:T(8,128)(2,1)S(1)}, bf16[256,1152]{1,0:T(8,128)(2,1)S(1)}, u32[]{:S(2)}, u32[]{:S(2)}) collective-permute-start(bf16[256,1152]{1,0:T(8,128)(2,1)S(1)} %slice.113.refs_0_), channel_id=1, source_target_pairs={{0,2},{1,3},{2,0},{3,1},{4,6},{5,7},{6,4},{7,5},{8,10},{9,11},{10,... | collective-permute-start | bytes 1769480 | tf_op jit(solution)/shard_map/ppermute | solution.py:182
  5.5 13.5 %collective-permute-start.4 = (f32[512]{0:T(512)S(1)}, f32[512]{0:T(512)S(1)}, u32[]{:S(2)}, u32[]{:S(2)}) collective-permute-start(f32[512]{0:T(512)S(1)} %get-tuple-element.19), channel_id=1, source_target_pairs={{0,2},{1,3},{2,0},{3,1},{4,6},{5,7},{6,4},{7,5},{8,10},{9,11},{10,... | collective-permute-start | bytes 6152 | tf_op jit(solution)/shard_map/ppermute | solution.py:182
  5.6 15.2 %collective-permute-start.5 = (f32[512]{0:T(512)S(1)}, f32[512]{0:T(512)S(1)}, u32[]{:S(2)}, u32[]{:S(2)}) collective-permute-start(f32[512]{0:T(512)S(1)} %get-tuple-element.19), channel_id=1, source_target_pairs={{0,3},{1,2},{2,1},{3,0},{4,7},{5,6},{6,5},{7,4},{8,11},{9,10},{10,... | collective-permute-start | bytes 6152 | tf_op jit(solution)/shard_map/ppermute | solution.py:182
  6.5 14.5 %collective-permute-start.3 = (f32[512]{0:T(512)S(1)}, f32[512]{0:T(512)S(1)}, u32[]{:S(2)}, u32[]{:S(2)}) collective-permute-start(f32[512]{0:T(512)S(1)} %get-tuple-element.19), channel_id=1, source_target_pairs={{0,1},{1,0},{2,3},{3,2},{4,5},{5,4},{6,7},{7,6},{8,9},{9,8},{10,11... | collective-permute-start | bytes 6152 | tf_op jit(solution)/shard_map/ppermute | solution.py:182
  7.8 14.1 %collective-permute-start.9 = (bf16[256,1152]{1,0:T(8,128)(2,1)S(1)}, bf16[256,1152]{1,0:T(8,128)(2,1)S(1)}, u32[]{:S(2)}, u32[]{:S(2)}) collective-permute-start(bf16[256,1152]{1,0:T(8,128)(2,1)S(1)} %slice.113.refs_0_), channel_id=1, source_target_pairs={{0,1},{1,0},{2,3},{3,2},{4,5},{5,4},{6,7},{7,6},{8,9},{9,8},{10,11... | collective-permute-start | bytes 1769480 | tf_op jit(solution)/shard_map/ppermute | solution.py:182
  19.1 16.1 %collective-permute-start.1 = (bf16[128,1152]{1,0:T(8,128)(2,1)S(1)}, bf16[128,1152]{1,0:T(8,128)(2,1)}, u32[]{:S(2)}, u32[]{:S(2)}) collective-permute-start(bf16[128,1152]{1,0:T(8,128)(2,1)S(1)} %get-tuple-element.18.refs_0_), channel_id=1, source_target_pairs={{0,2},{1,3},{2,0},{3,1},{4,6},{5,7},{6,4},{7,5},{8,10},{9,11},{10,... | collective-permute-start | bytes 884744 | tf_op jit(solution)/shard_map/ppermute | solution.py:182
  20.8 22.6 %collective-permute-start = (bf16[128,1152]{1,0:T(8,128)(2,1)S(1)}, bf16[128,1152]{1,0:T(8,128)(2,1)}, u32[]{:S(2)}, u32[]{:S(2)}) collective-permute-start(bf16[128,1152]{1,0:T(8,128)(2,1)S(1)} %get-tuple-element.18.refs_0_), channel_id=1, source_target_pairs={{0,1},{1,0},{2,3},{3,2},{4,5},{5,4},{6,7},{7,6},{8,9},{9,8},{10,11... | collective-permute-start | bytes 884744 | tf_op jit(solution)/shard_map/ppermute | solution.py:182
  31.9 22.6 %collective-permute-start.14 = (bf16[2,256,512]{2,1,0:T(8,128)(2,1)S(1)}, bf16[2,256,512]{2,1,0:T(8,128)(2,1)}, u32[]{:S(2)}, u32[]{:S(2)}) collective-permute-start(bf16[2,256,512]{2,1,0:T(8,128)(2,1)S(1)} %project.11), channel_id=1, source_target_pairs={{0,4},{4,0},{8,12},{12,8},{1,5},{5,1},{9,13},{13,9},{2,6},{6,2},{1... | collective-permute-start | bytes 1572872 | tf_op jit(solution)/shard_map/ppermute | solution.py:229
  34.4 9.0 %collective-permute-start.7 = (bf16[128,1152]{1,0:T(8,128)(2,1)S(1)}, bf16[128,1152]{1,0:T(8,128)(2,1)}, u32[]{:S(2)}, u32[]{:S(2)}) collective-permute-start(bf16[128,1152]{1,0:T(8,128)(2,1)S(1)} %get-tuple-element.21.refs_0_), channel_id=1, source_target_pairs={{0,2},{1,3},{2,0},{3,1},{4,6},{5,7},{6,4},{7,5},{8,10},{9,11},{10,... | collective-permute-start | bytes 884744 | tf_op jit(solution)/shard_map/ppermute | solution.py:182
  35.1 8.3 %collective-permute-start.2 = (bf16[128,1152]{1,0:T(8,128)(2,1)}, bf16[128,1152]{1,0:T(8,128)(2,1)}, u32[]{:S(2)}, u32[]{:S(2)}) collective-permute-start(bf16[128,1152]{1,0:T(8,128)(2,1)} %collective-permute-done.1.refs_2_), channel_id=1, source_target_pairs={{0,1},{1,0},{2,3},{3,2},{4,5},{5,4},{6,7},{7,6},{8,9},{9,8},{10,11... | collective-permute-start | bytes 884744 | tf_op jit(solution)/shard_map/ppermute | solution.py:182
  35.2 26.8 %collective-permute-start.6 = (bf16[128,1152]{1,0:T(8,128)(2,1)S(1)}, bf16[128,1152]{1,0:T(8,128)(2,1)}, u32[]{:S(2)}, u32[]{:S(2)}) collective-permute-start(bf16[128,1152]{1,0:T(8,128)(2,1)S(1)} %get-tuple-element.21.refs_0_), channel_id=1, source_target_pairs={{0,1},{1,0},{2,3},{3,2},{4,5},{5,4},{6,7},{7,6},{8,9},{9,8},{10,11... | collective-permute-start | bytes 884744 | tf_op jit(solution)/shard_map/ppermute | solution.py:182
  43.4 22.1 %collective-permute-start.8 = (bf16[128,1152]{1,0:T(8,128)(2,1)}, bf16[128,1152]{1,0:T(8,128)(2,1)}, u32[]{:S(2)}, u32[]{:S(2)}) collective-permute-start(bf16[128,1152]{1,0:T(8,128)(2,1)} %collective-permute-done.7.refs_2_), channel_id=1, source_target_pairs={{0,1},{1,0},{2,3},{3,2},{4,5},{5,4},{6,7},{7,6},{8,9},{9,8},{10,11... | collective-permute-start | bytes 884744 | tf_op jit(solution)/shard_map/ppermute | solution.py:182
  52.7 23.5 %collective-permute-start.12 = (bf16[2,128,512]{2,1,0:T(8,128)(2,1)}, bf16[2,128,512]{2,1,0:T(8,128)(2,1)}, u32[]{:S(2)}, u32[]{:S(2)}) collective-permute-start(bf16[2,128,512]{2,1,0:T(8,128)(2,1)} %project.9), channel_id=1, source_target_pairs={{0,4},{4,0},{8,12},{12,8},{1,5},{5,1},{9,13},{13,9},{2,6},{6,2},{1... | collective-permute-start | bytes 786440 | tf_op jit(solution)/shard_map/ppermute | solution.py:229
  53.1 45.5 %collective-permute-start.19 = (bf16[2,256,512]{2,1,0:T(8,128)(2,1)S(1)}, bf16[2,256,512]{2,1,0:T(8,128)(2,1)}, u32[]{:S(2)}, u32[]{:S(2)}) collective-permute-start(bf16[2,256,512]{2,1,0:T(8,128)(2,1)S(1)} %project.11), channel_id=1, source_target_pairs={{0,0},{4,8},{8,4},{12,12},{1,1},{5,9},{9,5},{13,13},{2,2},{6,10},{... | collective-permute-start | bytes 1572872 | tf_op jit(solution)/shard_map/ppermute | solution.py:232
  54.5 52.6 %collective-permute-start.25 = (bf16[2,256,512]{2,1,0:T(8,128)(2,1)}, bf16[2,256,512]{2,1,0:T(8,128)(2,1)}, u32[]{:S(2)}, u32[]{:S(2)}) collective-permute-start(bf16[2,256,512]{2,1,0:T(8,128)(2,1)} %collective-permute-done.14), channel_id=1, source_target_pairs={{0,0},{4,8},{8,4},{12,12},{1,1},{5,9},{9,5},{13,13},{2,2},{6,10},{... | collective-permute-start | bytes 1572872 | tf_op jit(solution)/shard_map/ppermute | solution.py:232
  62.0 34.0 %collective-permute-start.15 = (bf16[2,128,512]{2,1,0:T(8,128)(2,1)}, bf16[2,128,512]{2,1,0:T(8,128)(2,1)}, u32[]{:S(2)}, u32[]{:S(2)}) collective-permute-start(bf16[2,128,512]{2,1,0:T(8,128)(2,1)} %project.9), channel_id=1, source_target_pairs={{0,0},{4,8},{8,4},{12,12},{1,1},{5,9},{9,5},{13,13},{2,2},{6,10},{... | collective-permute-start | bytes 786440 | tf_op jit(solution)/shard_map/ppermute | solution.py:232
  75.6 28.3 %collective-permute-start.13 = (bf16[2,128,512]{2,1,0:T(8,128)(2,1)}, bf16[2,128,512]{2,1,0:T(8,128)(2,1)}, u32[]{:S(2)}, u32[]{:S(2)}) collective-permute-start(bf16[2,128,512]{2,1,0:T(8,128)(2,1)} %project.10), channel_id=1, source_target_pairs={{0,4},{4,0},{8,12},{12,8},{1,5},{5,1},{9,13},{13,9},{2,6},{6,2},{1... | collective-permute-start | bytes 786440 | tf_op jit(solution)/shard_map/ppermute | solution.py:229
  76.2 29.4 %collective-permute-start.17 = (bf16[2,128,512]{2,1,0:T(8,128)(2,1)}, bf16[2,128,512]{2,1,0:T(8,128)(2,1)}, u32[]{:S(2)}, u32[]{:S(2)}) collective-permute-start(bf16[2,128,512]{2,1,0:T(8,128)(2,1)} %project.10), channel_id=1, source_target_pairs={{0,0},{4,8},{8,4},{12,12},{1,1},{5,9},{9,5},{13,13},{2,2},{6,10},{... | collective-permute-start | bytes 786440 | tf_op jit(solution)/shard_map/ppermute | solution.py:232
  96.0 17.1 %collective-permute-start.16 = (bf16[2,128,512]{2,1,0:T(8,128)(2,1)}, bf16[2,128,512]{2,1,0:T(8,128)(2,1)S(1)}, u32[]{:S(2)}, u32[]{:S(2)}) collective-permute-start(bf16[2,128,512]{2,1,0:T(8,128)(2,1)} %collective-permute-done.15), channel_id=1, source_target_pairs={{0,4},{4,0},{8,12},{12,8},{1,5},{5,1},{9,13},{13,9},{2,6},{6,2},{1... | collective-permute-start | bytes 786440 | tf_op jit(solution)/shard_map/ppermute | solution.py:229
  98.6 35.5 %collective-permute-start.20 = (bf16[2,256,512]{2,1,0:T(8,128)(2,1)}, bf16[2,256,512]{2,1,0:T(8,128)(2,1)S(1)}, u32[]{:S(2)}, u32[]{:S(2)}) collective-permute-start(bf16[2,256,512]{2,1,0:T(8,128)(2,1)} %collective-permute-done.19), channel_id=1, source_target_pairs={{0,4},{4,0},{8,12},{12,8},{1,5},{5,1},{9,13},{13,9},{2,6},{6,2},{1... | collective-permute-start | bytes 1572872 | tf_op jit(solution)/shard_map/ppermute | solution.py:229
  103.9 9.3 %collective-permute-start.21 = (bf16[2,128,512]{2,1,0:T(8,128)(2,1)}, bf16[2,128,512]{2,1,0:T(8,128)(2,1)S(1)}, u32[]{:S(2)}, u32[]{:S(2)}) collective-permute-start(bf16[2,128,512]{2,1,0:T(8,128)(2,1)} %collective-permute-done.12), channel_id=1, source_target_pairs={{0,0},{4,8},{8,4},{12,12},{1,1},{5,9},{9,5},{13,13},{2,2},{6,10},{... | collective-permute-start | bytes 786440 | tf_op jit(solution)/shard_map/ppermute | solution.py:232
  105.5 11.6 %collective-permute-start.23 = (bf16[2,128,512]{2,1,0:T(8,128)(2,1)}, bf16[2,128,512]{2,1,0:T(8,128)(2,1)S(1)}, u32[]{:S(2)}, u32[]{:S(2)}) collective-permute-start(bf16[2,128,512]{2,1,0:T(8,128)(2,1)} %collective-permute-done.13), channel_id=1, source_target_pairs={{0,0},{4,8},{8,4},{12,12},{1,1},{5,9},{9,5},{13,13},{2,2},{6,10},{... | collective-permute-start | bytes 786440 | tf_op jit(solution)/shard_map/ppermute | solution.py:232
  107.1 40.2 %collective-permute-start.26 = (bf16[2,256,512]{2,1,0:T(8,128)(2,1)}, bf16[2,256,512]{2,1,0:T(8,128)(2,1)S(1)}, u32[]{:S(2)}, u32[]{:S(2)}) collective-permute-start(bf16[2,256,512]{2,1,0:T(8,128)(2,1)} %collective-permute-done.25), channel_id=1, source_target_pairs={{0,4},{4,0},{8,12},{12,8},{1,5},{5,1},{9,13},{13,9},{2,6},{6,2},{1... | collective-permute-start | bytes 1572872 | tf_op jit(solution)/shard_map/ppermute | solution.py:229
  113.1 21.0 %collective-permute-start.18 = (bf16[2,128,512]{2,1,0:T(8,128)(2,1)}, bf16[2,128,512]{2,1,0:T(8,128)(2,1)S(1)}, u32[]{:S(2)}, u32[]{:S(2)}) collective-permute-start(bf16[2,128,512]{2,1,0:T(8,128)(2,1)} %collective-permute-done.17), channel_id=1, source_target_pairs={{0,4},{4,0},{8,12},{12,8},{1,5},{5,1},{9,13},{13,9},{2,6},{6,2},{1... | collective-permute-start | bytes 786440 | tf_op jit(solution)/shard_map/ppermute | solution.py:229
  113.3 34.1 %collective-permute-start.22 = (bf16[2,128,512]{2,1,0:T(8,128)(2,1)S(1)}, bf16[2,128,512]{2,1,0:T(8,128)(2,1)S(1)}, u32[]{:S(2)}, u32[]{:S(2)}) collective-permute-start(bf16[2,128,512]{2,1,0:T(8,128)(2,1)S(1)} %collective-permute-done.21), channel_id=1, source_target_pairs={{0,4},{4,0},{8,12},{12,8},{1,5},{5,1},{9,13},{13,9},{2,6},{6,2},{1... | collective-permute-start | bytes 786440 | tf_op jit(solution)/shard_map/ppermute | solution.py:229
  117.1 30.2 %collective-permute-start.24 = (bf16[2,128,512]{2,1,0:T(8,128)(2,1)S(1)}, bf16[2,128,512]{2,1,0:T(8,128)(2,1)S(1)}, u32[]{:S(2)}, u32[]{:S(2)}) collective-permute-start(bf16[2,128,512]{2,1,0:T(8,128)(2,1)S(1)} %collective-permute-done.23), channel_id=1, source_target_pairs={{0,4},{4,0},{8,12},{12,8},{1,5},{5,1},{9,13},{13,9},{2,6},{6,2},{1... | collective-permute-start | bytes 786440 | tf_op jit(solution)/shard_map/ppermute | solution.py:229
  170.2 16.3 %collective-permute-start.28 = (bf16[256,1152]{1,0:T(8,128)(2,1)S(1)}, bf16[256,1152]{1,0:T(8,128)(2,1)S(1)}, u32[]{:S(2)}, u32[]{:S(2)}) collective-permute-start(bf16[256,1152]{1,0:T(8,128)(2,1)S(1)} %fusion.3), channel_id=1, source_target_pairs={{0,2},{1,3},{2,0},{3,1},{4,6},{5,7},{6,4},{7,5},{8,10},{9,11},{10,... | collective-permute-start | bytes 1769480 | tf_op jit(solution)/shard_map/ppermute | solution.py:182
  171.0 27.5 %collective-permute-start.33 = (bf16[256,1152]{1,0:T(8,128)(2,1)S(1)}, bf16[256,1152]{1,0:T(8,128)(2,1)S(1)}, u32[]{:S(2)}, u32[]{:S(2)}) collective-permute-start(bf16[256,1152]{1,0:T(8,128)(2,1)S(1)} %fusion.4), channel_id=1, source_target_pairs={{0,2},{1,3},{2,0},{3,1},{4,6},{5,7},{6,4},{7,5},{8,10},{9,11},{10,... | collective-permute-start | bytes 1769480 | tf_op jit(solution)/shard_map/ppermute | solution.py:182
  186.8 13.0 %collective-permute-start.30 = (f32[256]{0:T(256)S(1)}, f32[256]{0:T(256)S(1)}, u32[]{:S(2)}, u32[]{:S(2)}) collective-permute-start(f32[256]{0:T(256)S(1)} %multiply_reduce_fusion.1), channel_id=1, source_target_pairs={{0,2},{1,3},{2,0},{3,1},{4,6},{5,7},{6,4},{7,5},{8,10},{9,11},{10,... | collective-permute-start | bytes 3080 | tf_op jit(solution)/shard_map/ppermute | solution.py:182
  187.5 13.7 %collective-permute-start.31 = (f32[256]{0:T(256)S(1)}, f32[256]{0:T(256)S(1)}, u32[]{:S(2)}, u32[]{:S(2)}) collective-permute-start(f32[256]{0:T(256)S(1)} %multiply_reduce_fusion.1), channel_id=1, source_target_pairs={{0,3},{1,2},{2,1},{3,0},{4,7},{5,6},{6,5},{7,4},{8,11},{9,10},{10,... | collective-permute-start | bytes 3080 | tf_op jit(solution)/shard_map/ppermute | solution.py:182
  187.5 13.7 %collective-permute-start.29 = (f32[256]{0:T(256)S(1)}, f32[256]{0:T(256)S(1)}, u32[]{:S(2)}, u32[]{:S(2)}) collective-permute-start(f32[256]{0:T(256)S(1)} %multiply_reduce_fusion.1), channel_id=1, source_target_pairs={{0,1},{1,0},{2,3},{3,2},{4,5},{5,4},{6,7},{7,6},{8,9},{9,8},{10,11... | collective-permute-start | bytes 3080 | tf_op jit(solution)/shard_map/ppermute | solution.py:182
  198.9 3.6 %collective-permute-start.35 = (f32[256]{0:T(256)S(1)}, f32[256]{0:T(256)S(1)}, u32[]{:S(2)}, u32[]{:S(2)}) collective-permute-start(f32[256]{0:T(256)S(1)} %multiply_reduce_fusion), channel_id=1, source_target_pairs={{0,2},{1,3},{2,0},{3,1},{4,6},{5,7},{6,4},{7,5},{8,10},{9,11},{10,... | collective-permute-start | bytes 3080 | tf_op jit(solution)/shard_map/ppermute | solution.py:182
  (28 other events, 139.8 us)

commit v3 on v2

--- a/solution.py
+++ b/solution.py
@@ -33,44 +33,45 @@
     return jnp.where(usable, 0.0, MASKED).reshape(cand_local, key_cand.shape[0] * CTOK)
 
 
-def project_body(rank_ref, *refs, weights):
-    x_refs = refs[:4]
-    inverse_ref = refs[4]
-    w_refs = refs[5 : 5 + 4 * weights]
+LONG = pl.CostEstimate(flops=10**10, transcendentals=0, bytes_accessed=10**6)
+SHORT = pl.CostEstimate(flops=1, transcendentals=0, bytes_accessed=1)
+
+
+def project_body(rank_ref, inverse_ref, *refs, chunks):
+    x_refs = refs[: 4 * chunks]
+    w_refs = refs[4 * chunks : -1]
     out_ref = refs[-1]
-    inverse = inverse_ref[...]
-    for i in range(weights):
-        total = None
-        for k in range(4):
-            part = jnp.dot(
-                x_refs[k][...], w_refs[4 * i + k][...], preferred_element_type=jnp.float32
-            )
-            total = part if total is None else total + part
-        out_ref[i] = (total * inverse).astype(jnp.bfloat16)
-
-
-def project(rank, blocks, inverse, weights, width):
-    rows, features = blocks[0].shape
-    columns = weights[0].shape[1]
-    in_specs = [pl.BlockSpec((rows, features), lambda j, r: (0, 0)) for _ in range(4)]
-    in_specs.append(pl.BlockSpec((rows, 1), lambda j, r: (0, 0)))
-    operands = []
-    for w in weights:
-        for k in range(4):
-            in_specs.append(pl.BlockSpec((features, width), lambda j, r, k=k: (r[k], j)))
-            operands.append(w)
+    features = x_refs[0].shape[1]
+    start = 0
+    for c in range(chunks):
+        span = slice(start, start + x_refs[4 * c].shape[0])
+        start = span.stop
+        for i, w_ref in enumerate(w_refs):
+            total = None
+            for k in range(4):
+                rows = pl.ds(pl.multiple_of(rank_ref[k] * features, HEAD), features)
+                part = jnp.dot(
+                    x_refs[4 * c + k][...], w_ref[rows, :], preferred_element_type=jnp.float32
+                )
+                total = part if total is None else total + part
+            out_ref[i, span] = (total * inverse_ref[span]).astype(jnp.bfloat16)
+
+
+def project(ranks, chunks, inverse, weights):
+    vmem = pl.BlockSpec(memory_space=pltpu.VMEM)
+    blocks = [x for chunk in chunks for x in chunk]
     return pl.pallas_call(
-        functools.partial(project_body, weights=len(weights)),
-        grid_spec=pltpu.PrefetchScalarGridSpec(
-            num_scalar_prefetch=1,
-            grid=(columns // width,),
-            in_specs=in_specs,
-            out_specs=pl.BlockSpec((len(weights), rows, width), lambda j, r: (0, 0, j)),
+        functools.partial(project_body, chunks=len(chunks)),
+        in_specs=[pl.BlockSpec(memory_space=pltpu.SMEM)]
+        + [vmem] * (1 + len(blocks) + len(weights)),
+        out_specs=vmem,
+        out_shape=jax.ShapeDtypeStruct(
+            (len(weights), inverse.shape[0], weights[0].shape[1]), jnp.bfloat16
         ),
-        out_shape=jax.ShapeDtypeStruct((len(weights), rows, columns), jnp.bfloat16),
-        compiler_params=pltpu.CompilerParams(vmem_limit_bytes=32 * 2**20),
+        compiler_params=pltpu.CompilerParams(vmem_limit_bytes=24 * 2**20),
+        cost_estimate=LONG,
         name="project",
-    )(rank, *blocks, inverse, *operands)
+    )(ranks, inverse, *blocks, *weights)
 
 
 def scaled_scores(q, k, bias):
@@ -150,7 +151,8 @@
         in_specs=in_specs + [own] * len(state),
         out_specs=out_specs,
         out_shape=out_shape,
-        compiler_params=pltpu.CompilerParams(vmem_limit_bytes=40 * 2**20),
+        compiler_params=pltpu.CompilerParams(vmem_limit_bytes=20 * 2**20),
+        cost_estimate=LONG,
         name="attention",
     )(bias, queries, *operands, *state)
 
@@ -174,6 +176,7 @@
         out_specs=pl.BlockSpec(memory_space=pltpu.VMEM),
         out_shape=jax.ShapeDtypeStruct((block_ids.shape[0], rows, features), jnp.bfloat16),
         compiler_params=pltpu.CompilerParams(vmem_limit_bytes=24 * 2**20),
+        cost_estimate=SHORT,
         name="output",
     )(block_ids, attended, w_out)
 
@@ -213,6 +216,8 @@
         own = scaled[span]
         if c == 1:
             own, square_sum = lax.optimization_barrier((own, square_sum))
+        if c > 1:
+            own, _ = lax.optimization_barrier((own, blocks[c - 2][2]))
         far = swap(own, 2)
         if c == 0:
             squares = jnp.sum(wide * wide, axis=1)
@@ -221,15 +226,18 @@
         blocks.append([own, swap(own, 1), far, swap(far, 1)])
     inverse = lax.rsqrt(square_sum / model_width + epsilon)[:, None]
 
-    key_values = [
-        project(ranks, blocks[c], inverse[span], [w_key, w_value], 256)
-        for c, span in enumerate(spans)
-    ]
+    key_values = []
+    for c, span in enumerate(spans):
+        if c:
+            blocks[c][0], key_values[-1] = lax.optimization_barrier((blocks[c][0], key_values[-1]))
+        key_values.append(project(ranks, [blocks[c]], inverse[span], [w_key, w_value]))
     def outer(parts):
         return [lax.ppermute(x, "cand", [(0, 1), (1, 0), (2, 3), (3, 2)]) for x in parts]
 
+    inner_pairs = [(0, 4), (4, 0), (3, 7), (7, 3), (1, 2), (2, 1), (5, 6), (6, 5)]
+
     def inner(parts):
-        return [lax.ppermute(x, "cand", [(0, 0), (1, 2), (2, 1), (3, 3)]) for x in parts]
+        return [lax.ppermute(x, ("groups", "cand"), inner_pairs) for x in parts]
 
     outer_1 = outer(key_values)
     inner_1 = inner(key_values)
@@ -258,13 +266,7 @@
         [s * cand_local + jnp.arange(cand_local, dtype=jnp.int32) for s in shards]
     )
     bias = bias_rows(cand_lengths, pair_mask, place * cand_local, cand_local, key_cand)
-    queries = jnp.concatenate(
-        [
-            project(ranks, blocks[c], inverse[span], [w_query], 512)
-            for c, span in enumerate(spans)
-        ],
-        axis=1,
-    )
+    queries = project(ranks, blocks, inverse, [w_query])
     seen = 3 * row_count
     state = attention(bias[:, :seen], queries, slots, ends=False)
     state, last_slot = lax.optimization_barrier((state, last_slot))
@@ -277,12 +279,10 @@
     updates = []
     for c in range(OUTPUT_CHUNKS):
         span = slice(c * step, (c + 1) * step)
-        attended = attention(
-            bias[c * cands : (c + 1) * cands, seen:],
-            queries[:, span],
-            [last_slot],
-            state=[x[span] for x in state],
-        )
+        part_bias = bias[c * cands : (c + 1) * cands, seen:]
+        part_queries = queries[:, span]
+        part_state = [x[span] for x in state]
+        attended = attention(part_bias, part_queries, [last_slot], state=part_state)
         away = swap(output_blocks(other_core, attended, w_out, features), 1)
         home = output_blocks(this_core, attended, w_out, features)
         far = (home[0].astype(jnp.float32) + away[0].astype(jnp.float32)).astype(jnp.bfloat16)
@@ -329,6 +329,7 @@
 
 def solution(mesh):
     small = mesh.shape["tensor"] == 4 and mesh.shape["cand"] == CAND_AXIS
+    small = small and mesh.shape["groups"] == 2
     return jax.shard_map(
         per_device_4x4 if small else per_device,
         mesh=mesh,

time: 206 us -> 160 us (0.78)
  local copies, waits for them, and re-layouts: 29.3 us -> 6.09 us
  starting transfers between devices: 50.4 us -> 34.3 us
  waiting for transfers between devices: 54.7 us -> 68 us
  Pallas kernels: 56.1 us -> 44 us
  other arithmetic: 12.4 us -> 6.43 us
    unnamed x47 -> x27, local copies, waits for them, and re-layouts: 24.2 us -> 4.82 us
    pallas_call x6 -> x4, Pallas kernels: 26 us -> 13.9 us  [project(): pl.pallas_call(functools.partial(project_body, chunks=len(chunks)), in_sp...]
    ppermute x6, waiting for transfers between devices: 0.02 us -> 9.74 us  [inner(): return [lax.ppermute(x, ('groups', 'cand'), inner_pairs) for x in parts]]
    ppermute x6, starting transfers between devices: 17.2 us -> 8.82 us  [inner(): return [lax.ppermute(x, ('groups', 'cand'), inner_pairs) for x in parts]]
    ppermute x9, waiting for transfers between devices: 11.9 us -> 19.6 us  [outer(): lax.ppermute(x, 'cand', [(0, 1), (1, 0), (2, 3), (3, 2)])]
    ppermute x9, starting transfers between devices: 17.9 us -> 11.6 us  [outer(): lax.ppermute(x, 'cand', [(0, 1), (1, 0), (2, 3), (3, 2)])]
    ppermute x22, waiting for transfers between devices: 42.8 us -> 38.6 us  [swap(): return lax.ppermute(x, 'tensor', [(t, t ^ bit) for t in range(4)])]
    slice x5, local copies, waits for them, and re-layouts: 3.56 us -> 0.37 us  [per_device_4x4(): inverse[span]]
  transfers between devices with their start and end apart: 37 -> 37, of which waited for: 7 -> 14; matrix products, arithmetic and copies ran while one was open for 6% -> 2% of each run, Pallas kernels for 21% -> 19%
where the time goes in v3:
time: 160 us
  waiting for transfers between devices  68 us (42%)
  Pallas kernels  44 us (28%)
  starting transfers between devices  34.3 us (21%)
  other arithmetic  6.43 us (4%)
  local copies, waits for them, and re-layouts  6.09 us (4%)
    ppermute x22, waiting for transfers between devices, swap(): return lax.ppermute(x, 'tensor', [(t, t ^ bit) for t in range(4)])  38.6 us
    pallas_call x3, Pallas kernels, attention(): pl.pallas_call(functools.partial(attention_body, slots=len(slots), begun=...  21.8 us
    ppermute x9, waiting for transfers between devices, outer(): lax.ppermute(x, 'cand', [(0, 1), (1, 0), (2, 3), (3, 2)])  19.6 us
    pallas_call x4, Pallas kernels, project(): pl.pallas_call(functools.partial(project_body, chunks=len(chunks)), in_sp...  13.9 us
    ppermute x22, starting transfers between devices, swap(): return lax.ppermute(x, 'tensor', [(t, t ^ bit) for t in range(4)])  13.8 us
    ppermute x9, starting transfers between devices, outer(): lax.ppermute(x, 'cand', [(0, 1), (1, 0), (2, 3), (3, 2)])  11.6 us
    ppermute x6, waiting for transfers between devices, inner(): return [lax.ppermute(x, ('groups', 'cand'), inner_pairs) for x in parts]  9.74 us
    ppermute x6, starting transfers between devices, inner(): return [lax.ppermute(x, ('groups', 'cand'), inner_pairs) for x in parts]  8.82 us
  transfers between devices with their start and end apart: 37, of which 14 were waited for; matrix products, arithmetic and copies ran while one was open for 2% of the time, Pallas kernels for 19%

profile of v3, /device:TPU:0, one launch (start us, length us, event | category | flops | bytes accessed | tf_op | source)
XLA Modules:
  0.0 160.2 jit_solution(12731521329337424651)
XLA Ops:
  3.0 2.6 %collective-permute-start.1 = (f32[512]{0:T(512)S(1)}, f32[512]{0:T(512)S(1)}, u32[]{:S(2)}, u32[]{:S(2)}) collective-permute-start(f32[512]{0:T(512)S(1)} %get-tuple-element.23), channel_id=1, source_target_pairs={{0,2},{1,3},{2,0},{3,1},{4,6},{5,7},{6,4},{7,5},{8,10},{9,11},{10,... | collective-permute-start | bytes 6152 | tf_op jit(solution)/shard_map/ppermute | solution.py:185
  9.5 6.0 %collective-permute-done.4.refs_2_ = bf16[128,1152]{1,0:T(8,128)(2,1)S(1)} collective-permute-done((bf16[128,1152]{1,0:T(8,128)(2,1)S(1)}, bf16[128,1152]{1,0:T(8,128)(2,1)S(1)}, u32[]{:S(2)}, u32[]{:S(2)}) %collective-permute-start.4) | collective-permute-done | bytes 294944 | tf_op jit(solution)/shard_map/ppermute | solution.py:185
  16.0 1.8 %collective-permute-start.10 = (bf16[256,1152]{1,0:T(8,128)(2,1)S(1)}, bf16[256,1152]{1,0:T(8,128)(2,1)S(1)}, u32[]{:S(2)}, u32[]{:S(2)}) collective-permute-start(bf16[256,1152]{1,0:T(8,128)(2,1)S(1)} %slice.115.refs_8_.refs_0_), channel_id=1, source_target_pairs={{0,2},{1,3},{2,0},{3,1},{4,6},{5,7},{6,4},{7,5},{8,10},{9,11},{10,... | collective-permute-start | bytes 1769480 | tf_op jit(solution)/shard_map/ppermute | solution.py:185
  18.1 3.7 %collective-permute-done.7.refs_2_.refs_6_ = bf16[128,1152]{1,0:T(8,128)(2,1)S(1)} collective-permute-done((bf16[128,1152]{1,0:T(8,128)(2,1)S(1)}, bf16[128,1152]{1,0:T(8,128)(2,1)S(1)}, u32[]{:S(2)}, u32[]{:S(2)}) %collective-permute-start.7) | collective-permute-done | bytes 294944 | tf_op jit(solution)/shard_map/ppermute | solution.py:185
  21.8 2.3 %copy-done = bf16[4608,512]{1,0:T(8,128)(2,1)S(1)} copy-done((bf16[4608,512]{1,0:T(8,128)(2,1)S(1)}, bf16[4608,512]{1,0:T(8,128)(2,1)}, u32[]{:S(2)}) %copy-start) | copy-done | bytes 4718616
  24.2 2.3 %copy-done.1 = bf16[4608,512]{1,0:T(8,128)(2,1)S(1)} copy-done((bf16[4608,512]{1,0:T(8,128)(2,1)S(1)}, bf16[4608,512]{1,0:T(8,128)(2,1)}, u32[]{:S(2)}) %copy-start.1) | copy-done | bytes 4718616
  26.5 2.1 %project.4 = bf16[2,128,512]{2,1,0:T(8,128)(2,1)S(1)} custom-call(s32[4]{0:T(128)S(1)} %pad_add_fusion.2.rank_ref, f32[128,1]{1,0:T(8,128)S(1)} %copy.12.inverse_ref, bf16[128,1152]{1,0:T(8,128)(2,1)S(1)} %get-tuple-element.25.refs_0_, bf16[128,1152]{1,0:T(8,128)(2,1)S(1)} %collective-permute-done.3.refs_1_, ...), custom_call_target="tpu_custom_call" | custom-call | flops 10000000000 | bytes 1000000 | tf_op jit(solution)/shard_map/project/pallas_call | solution.py:63
  28.7 1.9 %collective-permute-start.12 = (bf16[2,128,512]{2,1,0:T(8,128)(2,1)S(1)}, bf16[2,128,512]{2,1,0:T(8,128)(2,1)S(1)}, u32[]{:S(2)}, u32[]{:S(2)}) collective-permute-start(bf16[2,128,512]{2,1,0:T(8,128)(2,1)S(1)} %project.4), channel_id=1, source_target_pairs={{0,4},{4,0},{8,12},{12,8},{1,5},{5,1},{9,13},{13,9},{2,6},{6,2},{1... | collective-permute-start | bytes 786440 | tf_op jit(solution)/shard_map/ppermute | solution.py:235
  32.1 1.8 %collective-permute-done.10.refs_10_.refs_2_ = bf16[256,1152]{1,0:T(8,128)(2,1)S(1)} collective-permute-done((bf16[256,1152]{1,0:T(8,128)(2,1)S(1)}, bf16[256,1152]{1,0:T(8,128)(2,1)S(1)}, u32[]{:S(2)}, u32[]{:S(2)}) %collective-permute-start.10) | collective-permute-done | bytes 589856 | tf_op jit(solution)/shard_map/ppermute | solution.py:185
  33.9 2.1 %project.5 = bf16[2,128,512]{2,1,0:T(8,128)(2,1)S(1)} custom-call(s32[4]{0:T(128)S(1)} %pad_add_fusion.2.rank_ref, f32[128,1]{1,0:T(8,128)S(1)} %copy.13.inverse_ref, bf16[128,1152]{1,0:T(8,128)(2,1)S(1)} %get-tuple-element.27.refs_0_.refs_4_, bf16[128,1152]{1,0:T(8,128)(2,1)S(1)} %collective-permute-done.6.refs_1_.refs_5_, ...), custom_call_target="tpu_custom_call" | custom-call | flops 10000000000 | bytes 1000000 | tf_op jit(solution)/shard_map/project/pallas_call | solution.py:63
  36.1 1.9 %collective-permute-start.13 = (bf16[2,128,512]{2,1,0:T(8,128)(2,1)S(1)}, bf16[2,128,512]{2,1,0:T(8,128)(2,1)S(1)}, u32[]{:S(2)}, u32[]{:S(2)}) collective-permute-start(bf16[2,128,512]{2,1,0:T(8,128)(2,1)S(1)} %project.5), channel_id=1, source_target_pairs={{0,4},{4,0},{8,12},{12,8},{1,5},{5,1},{9,13},{13,9},{2,6},{6,2},{1... | collective-permute-start | bytes 786440 | tf_op jit(solution)/shard_map/ppermute | solution.py:235
  38.0 3.4 %project.7 = bf16[2,256,512]{2,1,0:T(8,128)(2,1)S(1)} custom-call(s32[4]{0:T(128)S(1)} %pad_add_fusion.2.rank_ref, f32[256,1]{1,0:T(8,128)S(1)} %copy.15.inverse_ref, bf16[256,1152]{1,0:T(8,128)(2,1)S(1)} %slice.115.refs_8_.refs_0_, bf16[256,1152]{1,0:T(8,128)(2,1)S(1)} %collective-permute-done.9.refs_9_.refs_1_, ...), custom_call_target="tpu_custom_call" | custom-call | flops 10000000000 | bytes 1000000 | tf_op jit(solution)/shard_map/project/pallas_call | solution.py:63
  41.7 1.8 %collective-permute-start.19 = (bf16[2,256,512]{2,1,0:T(8,128)(2,1)S(1)}, bf16[2,256,512]{2,1,0:T(8,128)(2,1)S(1)}, u32[]{:S(2)}, u32[]{:S(2)}) collective-permute-start(bf16[2,256,512]{2,1,0:T(8,128)(2,1)S(1)} %project.7), channel_id=1, source_target_pairs={{0,16},{16,0},{12,28},{28,12},{4,8},{8,4},{20,24},{24,20},{1,17},{... | collective-permute-start | bytes 1572872 | tf_op jit(solution)/shard_map/ppermute | solution.py:240
  43.5 6.2 %project.6.q_ref = bf16[1,512,1024]{2,1,0:T(8,128)(2,1)S(1)} custom-call(s32[4]{0:T(128)S(1)} %pad_add_fusion.2.rank_ref, f32[512,1]{1,0:T(8,128)S(1)} %copy.14.inverse_ref, bf16[128,1152]{1,0:T(8,128)(2,1)S(1)} %get-tuple-element.25.refs_0_, bf16[128,1152]{1,0:T(8,128)(2,1)S(1)} %collective-permute-done.3.refs_1_, ...), custom_call_target="tpu_custom_call" | custom-call | flops 10000000000 | bytes 1000000 | tf_op jit(solution)/shard_map/project/pallas_call | solution.py:63
  50.0 1.8 %collective-permute-start.21 = (bf16[2,128,512]{2,1,0:T(8,128)(2,1)S(1)}, bf16[2,128,512]{2,1,0:T(8,128)(2,1)S(1)}, u32[]{:S(2)}, u32[]{:S(2)}) collective-permute-start(bf16[2,128,512]{2,1,0:T(8,128)(2,1)S(1)} %collective-permute-done.12), channel_id=1, source_target_pairs={{0,16},{16,0},{12,28},{28,12},{4,8},{8,4},{20,24},{24,20},{1,17},{... | collective-permute-start | bytes 786440 | tf_op jit(solution)/shard_map/ppermute | solution.py:240
  51.8 4.3 %collective-permute-done.14 = bf16[2,256,512]{2,1,0:T(8,128)(2,1)S(1)} collective-permute-done((bf16[2,256,512]{2,1,0:T(8,128)(2,1)S(1)}, bf16[2,256,512]{2,1,0:T(8,128)(2,1)S(1)}, u32[]{:S(2)}, u32[]{:S(2)}) %collective-permute-start.14) | collective-permute-done | bytes 524320 | tf_op jit(solution)/shard_map/ppermute | solution.py:235
  60.0 2.1 %collective-permute-done.17 = bf16[2,128,512]{2,1,0:T(8,128)(2,1)S(1)} collective-permute-done((bf16[2,128,512]{2,1,0:T(8,128)(2,1)S(1)}, bf16[2,128,512]{2,1,0:T(8,128)(2,1)S(1)}, u32[]{:S(2)}, u32[]{:S(2)}) %collective-permute-start.17) | collective-permute-done | bytes 262176 | tf_op jit(solution)/shard_map/ppermute | solution.py:240
  62.1 1.8 %collective-permute-start.23 = (bf16[2,128,512]{2,1,0:T(8,128)(2,1)S(1)}, bf16[2,128,512]{2,1,0:T(8,128)(2,1)S(1)}, u32[]{:S(2)}, u32[]{:S(2)}) collective-permute-start(bf16[2,128,512]{2,1,0:T(8,128)(2,1)S(1)} %collective-permute-done.13), channel_id=1, source_target_pairs={{0,16},{16,0},{12,28},{28,12},{4,8},{8,4},{20,24},{24,20},{1,17},{... | collective-permute-start | bytes 786440 | tf_op jit(solution)/shard_map/ppermute | solution.py:240
  63.9 3.9 %collective-permute-done.21 = bf16[2,128,512]{2,1,0:T(8,128)(2,1)S(1)} collective-permute-done((bf16[2,128,512]{2,1,0:T(8,128)(2,1)S(1)}, bf16[2,128,512]{2,1,0:T(8,128)(2,1)S(1)}, u32[]{:S(2)}, u32[]{:S(2)}) %collective-permute-start.21) | collective-permute-done | bytes 262176 | tf_op jit(solution)/shard_map/ppermute | solution.py:240
  67.7 1.8 %collective-permute-start.18 = (bf16[2,128,512]{2,1,0:T(8,128)(2,1)S(1)}, bf16[2,128,512]{2,1,0:T(8,128)(2,1)S(1)}, u32[]{:S(2)}, u32[]{:S(2)}) collective-permute-start(bf16[2,128,512]{2,1,0:T(8,128)(2,1)S(1)} %collective-permute-done.17), channel_id=1, source_target_pairs={{0,4},{4,0},{8,12},{12,8},{1,5},{5,1},{9,13},{13,9},{2,6},{6,2},{1... | collective-permute-start | bytes 786440 | tf_op jit(solution)/shard_map/ppermute | solution.py:235
  69.7 8.6 %collective-permute-done.16 = bf16[2,128,512]{2,1,0:T(8,128)(2,1)S(1)} collective-permute-done((bf16[2,128,512]{2,1,0:T(8,128)(2,1)S(1)}, bf16[2,128,512]{2,1,0:T(8,128)(2,1)S(1)}, u32[]{:S(2)}, u32[]{:S(2)}) %collective-permute-start.16) | collective-permute-done | bytes 262176 | tf_op jit(solution)/shard_map/ppermute | solution.py:235
  79.9 3.8 %collective-permute-done.23 = bf16[2,128,512]{2,1,0:T(8,128)(2,1)S(1)} collective-permute-done((bf16[2,128,512]{2,1,0:T(8,128)(2,1)S(1)}, bf16[2,128,512]{2,1,0:T(8,128)(2,1)S(1)}, u32[]{:S(2)}, u32[]{:S(2)}) %collective-permute-start.23) | collective-permute-done | bytes 262176 | tf_op jit(solution)/shard_map/ppermute | solution.py:240
  86.2 11.8 %attention.3 = (f32[512,1024]{1,0:T(8,128)S(1)}, f32[512,1024]{1,0:T(8,128)S(1)}, f32[512,1024]{1,0:T(8,128)S(1)}) custom-call(f32[4,1536]{1,0:T(4,128)S(1)} %slice.117.bias_ref, bf16[1,512,1024]{2,1,0:T(8,128)(2,1)S(1)} %project.6.q_ref, bf16[2,512,512]{2,1,0:T(8,128)(2,1)S(1)} %pad_maximum_fusion.1.refs_0_.refs_1_, ...), custom_call_target="tpu_custom_call" | custom-call | flops 10000000000 | bytes 1000000 | tf_op jit(solution)/shard_map/attention/pallas_call | solution.py:148
  98.0 6.7 %collective-permute-done.26 = bf16[2,256,512]{2,1,0:T(8,128)(2,1)S(1)} collective-permute-done((bf16[2,256,512]{2,1,0:T(8,128)(2,1)S(1)}, bf16[2,256,512]{2,1,0:T(8,128)(2,1)S(1)}, u32[]{:S(2)}, u32[]{:S(2)}) %collective-permute-start.26) | collective-permute-done | bytes 524320 | tf_op jit(solution)/shard_map/ppermute | solution.py:235
  105.6 4.9 %attention.4.x_ref = bf16[256,1024]{1,0:T(8,128)(2,1)S(1)} custom-call(f32[2,512]{1,0:T(2,128)S(1)} %get-tuple-element.53.bias_ref, bf16[1,256,1024]{2,1,0:T(8,128)(2,1)S(1)} %get-tuple-element.51.q_ref, bf16[2,512,512]{2,1,0:T(8,128)(2,1)S(1)} %maximum_select_fusion.1.refs_0_.refs_1_, bf16[2,512,512]{2,1,0:T(8,128)(2,1)S(1)} %maximum_select_fusion.1.refs_0_.refs_1_, ...), custom_call_target="tpu_custom_call" | custom-call | flops 10000000000 | bytes 1000000 | tf_op jit(solution)/shard_map/attention/pallas_call | solution.py:148
  110.5 2.1 %output.5 = bf16[2,256,1152]{2,1,0:T(8,128)(2,1)S(1)} custom-call(s32[2]{0:T(128)S(1)} %pad_add_fusion.3.block_ref, bf16[256,1024]{1,0:T(8,128)(2,1)S(1)} %attention.4.x_ref, bf16[1024,4608]{1,0:T(8,128)(2,1)S(1)} %bitcast.41), custom_call_target="tpu_custom_call" | custom-call | flops 1 | bytes 1 | tf_op jit(solution)/shard_map/output/pallas_call | solution.py:169
  112.8 2.1 %output.4 = bf16[2,256,1152]{2,1,0:T(8,128)(2,1)S(1)} custom-call(s32[2]{0:T(128)S(1)} %pad_add_fusion.block_ref, bf16[256,1024]{1,0:T(8,128)(2,1)S(1)} %attention.4.x_ref, bf16[1024,4608]{1,0:T(8,128)(2,1)S(1)} %bitcast.41), custom_call_target="tpu_custom_call" | custom-call | flops 1 | bytes 1 | tf_op jit(solution)/shard_map/output/pallas_call | solution.py:169
  115.7 5.1 %attention.5.x_ref = bf16[256,1024]{1,0:T(8,128)(2,1)S(1)} custom-call(f32[2,512]{1,0:T(2,128)S(1)} %get-tuple-element.54.bias_ref, bf16[1,256,1024]{2,1,0:T(8,128)(2,1)S(1)} %get-tuple-element.52.q_ref, bf16[2,512,512]{2,1,0:T(8,128)(2,1)S(1)} %maximum_select_fusion.1.refs_0_.refs_1_, bf16[2,512,512]{2,1,0:T(8,128)(2,1)S(1)} %maximum_select_fusion.1.refs_0_.refs_1_, ...), custom_call_target="tpu_custom_call" | custom-call | flops 10000000000 | bytes 1000000 | tf_op jit(solution)/shard_map/attention/pallas_call | solution.py:148
  120.8 2.1 %output.7 = bf16[2,256,1152]{2,1,0:T(8,128)(2,1)S(1)} custom-call(s32[2]{0:T(128)S(1)} %pad_add_fusion.3.block_ref, bf16[256,1024]{1,0:T(8,128)(2,1)S(1)} %attention.5.x_ref, bf16[1024,4608]{1,0:T(8,128)(2,1)S(1)} %bitcast.41), custom_call_target="tpu_custom_call" | custom-call | flops 1 | bytes 1 | tf_op jit(solution)/shard_map/output/pallas_call | solution.py:169
  123.1 2.1 %output.6 = bf16[2,256,1152]{2,1,0:T(8,128)(2,1)S(1)} custom-call(s32[2]{0:T(128)S(1)} %pad_add_fusion.block_ref, bf16[256,1024]{1,0:T(8,128)(2,1)S(1)} %attention.5.x_ref, bf16[1024,4608]{1,0:T(8,128)(2,1)S(1)} %bitcast.41), custom_call_target="tpu_custom_call" | custom-call | flops 1 | bytes 1 | tf_op jit(solution)/shard_map/output/pallas_call | solution.py:169
  127.5 13.9 %collective-permute-done.28 = bf16[256,1152]{1,0:T(8,128)(2,1)S(1)} collective-permute-done((bf16[256,1152]{1,0:T(8,128)(2,1)S(1)}, bf16[256,1152]{1,0:T(8,128)(2,1)S(1)}, u32[]{:S(2)}, u32[]{:S(2)}) %collective-permute-start.28) | collective-permute-done | bytes 589856 | tf_op jit(solution)/shard_map/ppermute | solution.py:185
  143.7 9.8 %collective-permute-done.33 = bf16[256,1152]{1,0:T(8,128)(2,1)S(1)} collective-permute-done((bf16[256,1152]{1,0:T(8,128)(2,1)S(1)}, bf16[256,1152]{1,0:T(8,128)(2,1)S(1)}, u32[]{:S(2)}, u32[]{:S(2)}) %collective-permute-start.33) | collective-permute-done | bytes 589856 | tf_op jit(solution)/shard_map/ppermute | solution.py:185
  (126 shorter events, 31.2 us)
Async XLA Ops:
  2.5 6.5 %collective-permute-start = (f32[512]{0:T(512)S(1)}, f32[512]{0:T(512)S(1)}, u32[]{:S(2)}, u32[]{:S(2)}) collective-permute-start(f32[512]{0:T(512)S(1)} %get-tuple-element.23), channel_id=1, source_target_pairs={{0,1},{1,0},{2,3},{3,2},{4,5},{5,4},{6,7},{7,6},{8,9},{9,8},{10,11... | collective-permute-start | bytes 6152 | tf_op jit(solution)/shard_map/ppermute | solution.py:185
  3.0 5.9 %collective-permute-start.1 = (f32[512]{0:T(512)S(1)}, f32[512]{0:T(512)S(1)}, u32[]{:S(2)}, u32[]{:S(2)}) collective-permute-start(f32[512]{0:T(512)S(1)} %get-tuple-element.23), channel_id=1, source_target_pairs={{0,2},{1,3},{2,0},{3,1},{4,6},{5,7},{6,4},{7,5},{8,10},{9,11},{10,... | collective-permute-start | bytes 6152 | tf_op jit(solution)/shard_map/ppermute | solution.py:185
  5.6 9.9 %collective-permute-start.4 = (bf16[128,1152]{1,0:T(8,128)(2,1)S(1)}, bf16[128,1152]{1,0:T(8,128)(2,1)S(1)}, u32[]{:S(2)}, u32[]{:S(2)}) collective-permute-start(bf16[128,1152]{1,0:T(8,128)(2,1)S(1)} %get-tuple-element.25.refs_0_), channel_id=1, source_target_pairs={{0,2},{1,3},{2,0},{3,1},{4,6},{5,7},{6,4},{7,5},{8,10},{9,11},{10,... | collective-permute-start | bytes 884744 | tf_op jit(solution)/shard_map/ppermute | solution.py:185
  7.4 10.5 %collective-permute-start.3 = (bf16[128,1152]{1,0:T(8,128)(2,1)S(1)}, bf16[128,1152]{1,0:T(8,128)(2,1)S(1)}, u32[]{:S(2)}, u32[]{:S(2)}) collective-permute-start(bf16[128,1152]{1,0:T(8,128)(2,1)S(1)} %get-tuple-element.25.refs_0_), channel_id=1, source_target_pairs={{0,1},{1,0},{2,3},{3,2},{4,5},{5,4},{6,7},{7,6},{8,9},{9,8},{10,11... | collective-permute-start | bytes 884744 | tf_op jit(solution)/shard_map/ppermute | solution.py:185
  9.0 12.9 %collective-permute-start.7 = (bf16[128,1152]{1,0:T(8,128)(2,1)S(1)}, bf16[128,1152]{1,0:T(8,128)(2,1)S(1)}, u32[]{:S(2)}, u32[]{:S(2)}) collective-permute-start(bf16[128,1152]{1,0:T(8,128)(2,1)S(1)} %get-tuple-element.27.refs_0_.refs_4_), channel_id=1, source_target_pairs={{0,2},{1,3},{2,0},{3,1},{4,6},{5,7},{6,4},{7,5},{8,10},{9,11},{10,... | collective-permute-start | bytes 884744 | tf_op jit(solution)/shard_map/ppermute | solution.py:185
  9.3 21.2 %collective-permute-start.6 = (bf16[128,1152]{1,0:T(8,128)(2,1)S(1)}, bf16[128,1152]{1,0:T(8,128)(2,1)S(1)}, u32[]{:S(2)}, u32[]{:S(2)}) collective-permute-start(bf16[128,1152]{1,0:T(8,128)(2,1)S(1)} %get-tuple-element.27.refs_0_.refs_4_), channel_id=1, source_target_pairs={{0,1},{1,0},{2,3},{3,2},{4,5},{5,4},{6,7},{7,6},{8,9},{9,8},{10,11... | collective-permute-start | bytes 884744 | tf_op jit(solution)/shard_map/ppermute | solution.py:185
  15.5 6.3 %collective-permute-start.5 = (bf16[128,1152]{1,0:T(8,128)(2,1)S(1)}, bf16[128,1152]{1,0:T(8,128)(2,1)S(1)}, u32[]{:S(2)}, u32[]{:S(2)}) collective-permute-start(bf16[128,1152]{1,0:T(8,128)(2,1)S(1)} %collective-permute-done.4.refs_2_), channel_id=1, source_target_pairs={{0,1},{1,0},{2,3},{3,2},{4,5},{5,4},{6,7},{7,6},{8,9},{9,8},{10,11... | collective-permute-start | bytes 884744 | tf_op jit(solution)/shard_map/ppermute | solution.py:185
  16.0 17.8 %collective-permute-start.10 = (bf16[256,1152]{1,0:T(8,128)(2,1)S(1)}, bf16[256,1152]{1,0:T(8,128)(2,1)S(1)}, u32[]{:S(2)}, u32[]{:S(2)}) collective-permute-start(bf16[256,1152]{1,0:T(8,128)(2,1)S(1)} %slice.115.refs_8_.refs_0_), channel_id=1, source_target_pairs={{0,2},{1,3},{2,0},{3,1},{4,6},{5,7},{6,4},{7,5},{8,10},{9,11},{10,... | collective-permute-start | bytes 1769480 | tf_op jit(solution)/shard_map/ppermute | solution.py:185
  17.9 20.1 %collective-permute-start.9 = (bf16[256,1152]{1,0:T(8,128)(2,1)S(1)}, bf16[256,1152]{1,0:T(8,128)(2,1)S(1)}, u32[]{:S(2)}, u32[]{:S(2)}) collective-permute-start(bf16[256,1152]{1,0:T(8,128)(2,1)S(1)} %slice.115.refs_8_.refs_0_), channel_id=1, source_target_pairs={{0,1},{1,0},{2,3},{3,2},{4,5},{5,4},{6,7},{7,6},{8,9},{9,8},{10,11... | collective-permute-start | bytes 1769480 | tf_op jit(solution)/shard_map/ppermute | solution.py:185
  21.8 12.1 %collective-permute-start.8 = (bf16[128,1152]{1,0:T(8,128)(2,1)S(1)}, bf16[128,1152]{1,0:T(8,128)(2,1)S(1)}, u32[]{:S(2)}, u32[]{:S(2)}) collective-permute-start(bf16[128,1152]{1,0:T(8,128)(2,1)S(1)} %collective-permute-done.7.refs_2_.refs_6_), channel_id=1, source_target_pairs={{0,1},{1,0},{2,3},{3,2},{4,5},{5,4},{6,7},{7,6},{8,9},{9,8},{10,11... | collective-permute-start | bytes 884744 | tf_op jit(solution)/shard_map/ppermute | solution.py:185
  28.7 21.0 %collective-permute-start.12 = (bf16[2,128,512]{2,1,0:T(8,128)(2,1)S(1)}, bf16[2,128,512]{2,1,0:T(8,128)(2,1)S(1)}, u32[]{:S(2)}, u32[]{:S(2)}) collective-permute-start(bf16[2,128,512]{2,1,0:T(8,128)(2,1)S(1)} %project.4), channel_id=1, source_target_pairs={{0,4},{4,0},{8,12},{12,8},{1,5},{5,1},{9,13},{13,9},{2,6},{6,2},{1... | collective-permute-start | bytes 786440 | tf_op jit(solution)/shard_map/ppermute | solution.py:235
  30.6 19.5 %collective-permute-start.15 = (bf16[2,128,512]{2,1,0:T(8,128)(2,1)S(1)}, bf16[2,128,512]{2,1,0:T(8,128)(2,1)S(1)}, u32[]{:S(2)}, u32[]{:S(2)}) collective-permute-start(bf16[2,128,512]{2,1,0:T(8,128)(2,1)S(1)} %project.4), channel_id=1, source_target_pairs={{0,16},{16,0},{12,28},{28,12},{4,8},{8,4},{20,24},{24,20},{1,17},{... | collective-permute-start | bytes 786440 | tf_op jit(solution)/shard_map/ppermute | solution.py:240
  33.9 4.1 %collective-permute-start.11 = (bf16[256,1152]{1,0:T(8,128)(2,1)S(1)}, bf16[256,1152]{1,0:T(8,128)(2,1)S(1)}, u32[]{:S(2)}, u32[]{:S(2)}) collective-permute-start(bf16[256,1152]{1,0:T(8,128)(2,1)S(1)} %collective-permute-done.10.refs_10_.refs_2_), channel_id=1, source_target_pairs={{0,1},{1,0},{2,3},{3,2},{4,5},{5,4},{6,7},{7,6},{8,9},{9,8},{10,11... | collective-permute-start | bytes 1769480 | tf_op jit(solution)/shard_map/ppermute | solution.py:185
  36.1 23.5 %collective-permute-start.13 = (bf16[2,128,512]{2,1,0:T(8,128)(2,1)S(1)}, bf16[2,128,512]{2,1,0:T(8,128)(2,1)S(1)}, u32[]{:S(2)}, u32[]{:S(2)}) collective-permute-start(bf16[2,128,512]{2,1,0:T(8,128)(2,1)S(1)} %project.5), channel_id=1, source_target_pairs={{0,4},{4,0},{8,12},{12,8},{1,5},{5,1},{9,13},{13,9},{2,6},{6,2},{1... | collective-permute-start | bytes 786440 | tf_op jit(solution)/shard_map/ppermute | solution.py:235
  41.4 14.7 %collective-permute-start.14 = (bf16[2,256,512]{2,1,0:T(8,128)(2,1)S(1)}, bf16[2,256,512]{2,1,0:T(8,128)(2,1)S(1)}, u32[]{:S(2)}, u32[]{:S(2)}) collective-permute-start(bf16[2,256,512]{2,1,0:T(8,128)(2,1)S(1)} %project.7), channel_id=1, source_target_pairs={{0,4},{4,0},{8,12},{12,8},{1,5},{5,1},{9,13},{13,9},{2,6},{6,2},{1... | collective-permute-start | bytes 1572872 | tf_op jit(solution)/shard_map/ppermute | solution.py:235
  41.7 16.1 %collective-permute-start.19 = (bf16[2,256,512]{2,1,0:T(8,128)(2,1)S(1)}, bf16[2,256,512]{2,1,0:T(8,128)(2,1)S(1)}, u32[]{:S(2)}, u32[]{:S(2)}) collective-permute-start(bf16[2,256,512]{2,1,0:T(8,128)(2,1)S(1)} %project.7), channel_id=1, source_target_pairs={{0,16},{16,0},{12,28},{28,12},{4,8},{8,4},{20,24},{24,20},{1,17},{... | collective-permute-start | bytes 1572872 | tf_op jit(solution)/shard_map/ppermute | solution.py:240
  49.7 12.4 %collective-permute-start.17 = (bf16[2,128,512]{2,1,0:T(8,128)(2,1)S(1)}, bf16[2,128,512]{2,1,0:T(8,128)(2,1)S(1)}, u32[]{:S(2)}, u32[]{:S(2)}) collective-permute-start(bf16[2,128,512]{2,1,0:T(8,128)(2,1)S(1)} %project.5), channel_id=1, source_target_pairs={{0,16},{16,0},{12,28},{28,12},{4,8},{8,4},{20,24},{24,20},{1,17},{... | collective-permute-start | bytes 786440 | tf_op jit(solution)/shard_map/ppermute | solution.py:240
  50.0 17.7 %collective-permute-start.21 = (bf16[2,128,512]{2,1,0:T(8,128)(2,1)S(1)}, bf16[2,128,512]{2,1,0:T(8,128)(2,1)S(1)}, u32[]{:S(2)}, u32[]{:S(2)}) collective-permute-start(bf16[2,128,512]{2,1,0:T(8,128)(2,1)S(1)} %collective-permute-done.12), channel_id=1, source_target_pairs={{0,16},{16,0},{12,28},{28,12},{4,8},{8,4},{20,24},{24,20},{1,17},{... | collective-permute-start | bytes 786440 | tf_op jit(solution)/shard_map/ppermute | solution.py:240
  56.1 29.2 %collective-permute-start.25 = (bf16[2,256,512]{2,1,0:T(8,128)(2,1)S(1)}, bf16[2,256,512]{2,1,0:T(8,128)(2,1)S(1)}, u32[]{:S(2)}, u32[]{:S(2)}) collective-permute-start(bf16[2,256,512]{2,1,0:T(8,128)(2,1)S(1)} %collective-permute-done.14), channel_id=1, source_target_pairs={{0,16},{16,0},{12,28},{28,12},{4,8},{8,4},{20,24},{24,20},{1,17},{... | collective-permute-start | bytes 1572872 | tf_op jit(solution)/shard_map/ppermute | solution.py:240
  57.8 27.9 %collective-permute-start.20 = (bf16[2,256,512]{2,1,0:T(8,128)(2,1)S(1)}, bf16[2,256,512]{2,1,0:T(8,128)(2,1)S(1)}, u32[]{:S(2)}, u32[]{:S(2)}) collective-permute-start(bf16[2,256,512]{2,1,0:T(8,128)(2,1)S(1)} %collective-permute-done.19), channel_id=1, source_target_pairs={{0,4},{4,0},{8,12},{12,8},{1,5},{5,1},{9,13},{13,9},{2,6},{6,2},{1... | collective-permute-start | bytes 1572872 | tf_op jit(solution)/shard_map/ppermute | solution.py:235
  59.5 18.7 %collective-permute-start.16 = (bf16[2,128,512]{2,1,0:T(8,128)(2,1)S(1)}, bf16[2,128,512]{2,1,0:T(8,128)(2,1)S(1)}, u32[]{:S(2)}, u32[]{:S(2)}) collective-permute-start(bf16[2,128,512]{2,1,0:T(8,128)(2,1)S(1)} %collective-permute-done.15), channel_id=1, source_target_pairs={{0,4},{4,0},{8,12},{12,8},{1,5},{5,1},{9,13},{13,9},{2,6},{6,2},{1... | collective-permute-start | bytes 786440 | tf_op jit(solution)/shard_map/ppermute | solution.py:235
  62.1 21.6 %collective-permute-start.23 = (bf16[2,128,512]{2,1,0:T(8,128)(2,1)S(1)}, bf16[2,128,512]{2,1,0:T(8,128)(2,1)S(1)}, u32[]{:S(2)}, u32[]{:S(2)}) collective-permute-start(bf16[2,128,512]{2,1,0:T(8,128)(2,1)S(1)} %collective-permute-done.13), channel_id=1, source_target_pairs={{0,16},{16,0},{12,28},{28,12},{4,8},{8,4},{20,24},{24,20},{1,17},{... | collective-permute-start | bytes 786440 | tf_op jit(solution)/shard_map/ppermute | solution.py:240
  67.7 18.0 %collective-permute-start.18 = (bf16[2,128,512]{2,1,0:T(8,128)(2,1)S(1)}, bf16[2,128,512]{2,1,0:T(8,128)(2,1)S(1)}, u32[]{:S(2)}, u32[]{:S(2)}) collective-permute-start(bf16[2,128,512]{2,1,0:T(8,128)(2,1)S(1)} %collective-permute-done.17), channel_id=1, source_target_pairs={{0,4},{4,0},{8,12},{12,8},{1,5},{5,1},{9,13},{13,9},{2,6},{6,2},{1... | collective-permute-start | bytes 786440 | tf_op jit(solution)/shard_map/ppermute | solution.py:235
  78.2 19.7 %collective-permute-start.22 = (bf16[2,128,512]{2,1,0:T(8,128)(2,1)S(1)}, bf16[2,128,512]{2,1,0:T(8,128)(2,1)S(1)}, u32[]{:S(2)}, u32[]{:S(2)}) collective-permute-start(bf16[2,128,512]{2,1,0:T(8,128)(2,1)S(1)} %collective-permute-done.21), channel_id=1, source_target_pairs={{0,4},{4,0},{8,12},{12,8},{1,5},{5,1},{9,13},{13,9},{2,6},{6,2},{1... | collective-permute-start | bytes 786440 | tf_op jit(solution)/shard_map/ppermute | solution.py:235
  83.7 14.3 %collective-permute-start.24 = (bf16[2,128,512]{2,1,0:T(8,128)(2,1)S(1)}, bf16[2,128,512]{2,1,0:T(8,128)(2,1)S(1)}, u32[]{:S(2)}, u32[]{:S(2)}) collective-permute-start(bf16[2,128,512]{2,1,0:T(8,128)(2,1)S(1)} %collective-permute-done.23), channel_id=1, source_target_pairs={{0,4},{4,0},{8,12},{12,8},{1,5},{5,1},{9,13},{13,9},{2,6},{6,2},{1... | collective-permute-start | bytes 786440 | tf_op jit(solution)/shard_map/ppermute | solution.py:235
  85.3 19.4 %collective-permute-start.26 = (bf16[2,256,512]{2,1,0:T(8,128)(2,1)S(1)}, bf16[2,256,512]{2,1,0:T(8,128)(2,1)S(1)}, u32[]{:S(2)}, u32[]{:S(2)}) collective-permute-start(bf16[2,256,512]{2,1,0:T(8,128)(2,1)S(1)} %collective-permute-done.25), channel_id=1, source_target_pairs={{0,4},{4,0},{8,12},{12,8},{1,5},{5,1},{9,13},{13,9},{2,6},{6,2},{1... | collective-permute-start | bytes 1572872 | tf_op jit(solution)/shard_map/ppermute | solution.py:235
  122.9 3.8 %collective-permute-start.32 = (bf16[2,256,1152]{2,1,0:T(8,128)(2,1)S(1)}, bf16[2,256,1152]{2,1,0:T(8,128)(2,1)S(1)}, u32[]{:S(2)}, u32[]{:S(2)}) collective-permute-start(bf16[2,256,1152]{2,1,0:T(8,128)(2,1)S(1)} %output.7), channel_id=1, source_target_pairs={{0,1},{1,0},{2,3},{3,2},{4,5},{5,4},{6,7},{7,6},{8,9},{9,8},{10,11... | collective-permute-start | bytes 3538952 | tf_op jit(solution)/shard_map/ppermute | solution.py:185
  125.2 16.3 %collective-permute-start.28 = (bf16[256,1152]{1,0:T(8,128)(2,1)S(1)}, bf16[256,1152]{1,0:T(8,128)(2,1)S(1)}, u32[]{:S(2)}, u32[]{:S(2)}) collective-permute-start(bf16[256,1152]{1,0:T(8,128)(2,1)S(1)} %fusion.3), channel_id=1, source_target_pairs={{0,2},{1,3},{2,0},{3,1},{4,6},{5,7},{6,4},{7,5},{8,10},{9,11},{10,... | collective-permute-start | bytes 1769480 | tf_op jit(solution)/shard_map/ppermute | solution.py:185
  126.9 26.7 %collective-permute-start.33 = (bf16[256,1152]{1,0:T(8,128)(2,1)S(1)}, bf16[256,1152]{1,0:T(8,128)(2,1)S(1)}, u32[]{:S(2)}, u32[]{:S(2)}) collective-permute-start(bf16[256,1152]{1,0:T(8,128)(2,1)S(1)} %fusion.4), channel_id=1, source_target_pairs={{0,2},{1,3},{2,0},{3,1},{4,6},{5,7},{6,4},{7,5},{8,10},{9,11},{10,... | collective-permute-start | bytes 1769480 | tf_op jit(solution)/shard_map/ppermute | solution.py:185
  141.8 13.7 %collective-permute-start.29 = (f32[256]{0:T(256)S(1)}, f32[256]{0:T(256)S(1)}, u32[]{:S(2)}, u32[]{:S(2)}) collective-permute-start(f32[256]{0:T(256)S(1)} %multiply_reduce_fusion.1), channel_id=1, source_target_pairs={{0,1},{1,0},{2,3},{3,2},{4,5},{5,4},{6,7},{7,6},{8,9},{9,8},{10,11... | collective-permute-start | bytes 3080 | tf_op jit(solution)/shard_map/ppermute | solution.py:185
  141.9 13.9 %collective-permute-start.30 = (f32[256]{0:T(256)S(1)}, f32[256]{0:T(256)S(1)}, u32[]{:S(2)}, u32[]{:S(2)}) collective-permute-start(f32[256]{0:T(256)S(1)} %multiply_reduce_fusion.1), channel_id=1, source_target_pairs={{0,2},{1,3},{2,0},{3,1},{4,6},{5,7},{6,4},{7,5},{8,10},{9,11},{10,... | collective-permute-start | bytes 3080 | tf_op jit(solution)/shard_map/ppermute | solution.py:185
  143.4 12.4 %collective-permute-start.31 = (f32[256]{0:T(256)S(1)}, f32[256]{0:T(256)S(1)}, u32[]{:S(2)}, u32[]{:S(2)}) collective-permute-start(f32[256]{0:T(256)S(1)} %multiply_reduce_fusion.1), channel_id=1, source_target_pairs={{0,3},{1,2},{2,1},{3,0},{4,7},{5,6},{6,5},{7,4},{8,11},{9,10},{10,... | collective-permute-start | bytes 3080 | tf_op jit(solution)/shard_map/ppermute | solution.py:185
  (18 other events, 97.4 us)

commit v4 on v3

--- a/solution.py
+++ b/solution.py
@@ -81,7 +81,7 @@
 
 def attention_body(bias_ref, q_ref, *refs, slots, begun, ends):
     kv_refs = refs[: 2 * slots]
-    state_refs = refs[2 * slots : 2 * slots + (3 if begun else 0)]
+    state_refs = refs[2 * slots : 2 * slots + (2 if begun else 0)]
     out_refs = refs[2 * slots + len(state_refs) :]
     rows = q_ref.shape[1]
     for c in range(rows // CTOK):
@@ -103,11 +103,13 @@
         denominator = None
         numerator = None
         if begun:
-            old_top = stacked(state_refs[1])
-            top = jnp.maximum(old_top[:, :1], top)
-            fade = jnp.exp2(old_top - top)
-            numerator = stacked(state_refs[0]) * fade
-            denominator = stacked(state_refs[2])[:, :1] * fade[:, :1]
+            half = HEAD // GROUP
+            old = jnp.concatenate(
+                [state_refs[1][here, g * half : g * half + 1] for g in range(GROUP)], axis=0
+            )
+            top = jnp.maximum(old, top)
+            denominator = jnp.exp2(old - top)
+            numerator = stacked(state_refs[0]) * denominator
         for s in range(slots):
             p = jnp.exp2(scores[s] - top)
             d = jnp.sum(p, axis=1, keepdims=True)
@@ -116,21 +118,25 @@
             )
             denominator = d if denominator is None else denominator + d
             numerator = n if numerator is None else numerator + n
+        out = numerator / denominator
         if ends:
-            results = [(numerator / denominator).astype(jnp.bfloat16)]
-        else:
-            results = [numerator] + [
-                jnp.broadcast_to(x, numerator.shape) for x in (top, denominator)
-            ]
-        for ref, result in zip(out_refs, results):
+            out = out.astype(jnp.bfloat16)
+        for g in range(GROUP):
+            out_refs[0][here, g * HEAD : (g + 1) * HEAD] = out[g * CTOK : (g + 1) * CTOK]
+        if not ends:
+            level = top + jnp.log2(denominator)
+            half = HEAD // GROUP
             for g in range(GROUP):
-                ref[here, g * HEAD : (g + 1) * HEAD] = result[g * CTOK : (g + 1) * CTOK]
+                out_refs[1][here, g * half : (g + 1) * half] = jnp.broadcast_to(
+                    level[g * CTOK : (g + 1) * CTOK], (CTOK, half)
+                )
 
 
 def attention(bias, queries, slots, state=(), ends=True):
     _, rows, width = queries.shape
     heads = width // (GROUP * HEAD)
     own = pl.BlockSpec((rows, GROUP * HEAD), lambda h: (0, h))
+    level = pl.BlockSpec((rows, HEAD), lambda h: (0, h))
     in_specs = [
         pl.BlockSpec(bias.shape, lambda h: (0, 0)),
         pl.BlockSpec((1, rows, GROUP * HEAD), lambda h: (0, 0, h)),
@@ -143,12 +149,15 @@
     if ends:
         out_specs, out_shape = own, jax.ShapeDtypeStruct((rows, width), jnp.bfloat16)
     else:
-        out_specs = (own,) * 3
-        out_shape = (jax.ShapeDtypeStruct((rows, width), jnp.float32),) * 3
+        out_specs = (own, level)
+        out_shape = (
+            jax.ShapeDtypeStruct((rows, width), jnp.float32),
+            jax.ShapeDtypeStruct((rows, heads * HEAD), jnp.float32),
+        )
     return pl.pallas_call(
         functools.partial(attention_body, slots=len(slots), begun=len(state) > 0, ends=ends),
         grid=(heads,),
-        in_specs=in_specs + [own] * len(state),
+        in_specs=in_specs + ([own, level] if state else []),
         out_specs=out_specs,
         out_shape=out_shape,
         compiler_params=pltpu.CompilerParams(vmem_limit_bytes=20 * 2**20),
@@ -217,13 +226,14 @@
         if c == 1:
             own, square_sum = lax.optimization_barrier((own, square_sum))
         if c > 1:
-            own, _ = lax.optimization_barrier((own, blocks[c - 2][2]))
+            own, blocks[c - 1][1] = lax.optimization_barrier((own, blocks[c - 1][1]))
         far = swap(own, 2)
+        near = swap(own, 1)
         if c == 0:
             squares = jnp.sum(wide * wide, axis=1)
-            squares, own = lax.optimization_barrier((squares, own))
+            squares, near = lax.optimization_barrier((squares, near))
             square_sum = sum_over_tensor(squares)
-        blocks.append([own, swap(own, 1), far, swap(far, 1)])
+        blocks.append([own, near, far, swap(far, 1)])
     inverse = lax.rsqrt(square_sum / model_width + epsilon)[:, None]
 
     key_values = []
@@ -275,21 +285,21 @@
     other_core = jnp.stack([rank ^ 3, rank ^ 1])
     this_core = jnp.stack([rank ^ 2, rank])
     step = row_count // OUTPUT_CHUNKS
-    cands = step // CTOK
+    attended = attention(bias[:, seen:], queries, [last_slot], state=state)
+    pending = []
+    for c in range(OUTPUT_CHUNKS):
+        rows = attended[c * step : (c + 1) * step]
+        if c:
+            rows, far = lax.optimization_barrier((rows, pending[-1][2]))
+            pending[-1] = (*pending[-1][:2], far)
+        away = swap(output_blocks(other_core, rows, w_out, features), 1)
+        home = output_blocks(this_core, rows, w_out, features)
+        far = (home[0].astype(jnp.float32) + away[0].astype(jnp.float32)).astype(jnp.bfloat16)
+        pending.append((home[1], away[1], far))
+    pending = [(home, away, swap(far, 2)) for home, away, far in pending]
     updates = []
-    for c in range(OUTPUT_CHUNKS):
-        span = slice(c * step, (c + 1) * step)
-        part_bias = bias[c * cands : (c + 1) * cands, seen:]
-        part_queries = queries[:, span]
-        part_state = [x[span] for x in state]
-        attended = attention(part_bias, part_queries, [last_slot], state=part_state)
-        away = swap(output_blocks(other_core, attended, w_out, features), 1)
-        home = output_blocks(this_core, attended, w_out, features)
-        far = (home[0].astype(jnp.float32) + away[0].astype(jnp.float32)).astype(jnp.bfloat16)
-        if c + 1 < OUTPUT_CHUNKS:
-            far, last_slot = lax.optimization_barrier((far, last_slot))
-        far = swap(far, 2)
-        near = home[1].astype(jnp.float32) + away[1].astype(jnp.float32)
+    for home, away, far in pending:
+        near = home.astype(jnp.float32) + away.astype(jnp.float32)
         mixed = near + far.astype(jnp.float32)
         mixed_sq = sum_over_tensor(jnp.sum(mixed * mixed, axis=1))
         inverse_post = lax.rsqrt(mixed_sq / model_width + epsilon)

time: 160 us -> 164 us (1.025)
  local copies, waits for them, and re-layouts: 6.09 us -> 17.9 us
  waiting for transfers between devices: 68 us -> 59 us
  other arithmetic: 6.43 us -> 8.59 us
    ppermute x9, waiting for transfers between devices: 19.6 us -> 4.54 us  [outer(): lax.ppermute(x, 'cand', [(0, 1), (1, 0), (2, 3), (3, 2)])]
    unnamed x27 -> x49, local copies, waits for them, and re-layouts: 4.82 us -> 16.1 us
    ppermute x6, waiting for transfers between devices: 9.74 us -> 17.4 us  [inner(): return [lax.ppermute(x, ('groups', 'cand'), inner_pairs) for x in parts]]
    pallas_call x3 -> x2, Pallas kernels: 21.8 us -> 19.4 us  [attention(): pl.pallas_call(functools.partial(attention_body, slots=len(slots), begun=...]
  transfers between devices with their start and end apart: 37 -> 37, of which waited for: 14 -> 12; matrix products, arithmetic and copies ran while one was open for 2% -> 4% of each run, Pallas kernels for 19% -> 19%
where the time goes in v4:
time: 164 us
  waiting for transfers between devices  59 us (36%)
  Pallas kernels  42.5 us (26%)
  starting transfers between devices  34 us (21%)
  local copies, waits for them, and re-layouts  17.9 us (11%)
  other arithmetic  8.59 us (5%)
    ppermute x22, waiting for transfers between devices, swap(): return lax.ppermute(x, 'tensor', [(t, t ^ bit) for t in range(4)])  37.1 us
    pallas_call x2, Pallas kernels, attention(): pl.pallas_call(functools.partial(attention_body, slots=len(slots), begun=...  19.4 us
    ppermute x6, waiting for transfers between devices, inner(): return [lax.ppermute(x, ('groups', 'cand'), inner_pairs) for x in parts]  17.4 us
    unnamed x49, local copies, waits for them, and re-layouts  16.1 us
    ppermute x22, starting transfers between devices, swap(): return lax.ppermute(x, 'tensor', [(t, t ^ bit) for t in range(4)])  15.3 us
    pallas_call x4, Pallas kernels, project(): pl.pallas_call(functools.partial(project_body, chunks=len(chunks)), in_sp...  14.9 us
    ppermute x9, starting transfers between devices, outer(): lax.ppermute(x, 'cand', [(0, 1), (1, 0), (2, 3), (3, 2)])  10.8 us
    pallas_call x4, Pallas kernels, output_blocks(): pl.pallas_call(output_body, in_specs=[pl.BlockSpec(memory_space=pltpu.SME...  8.33 us
  transfers between devices with their start and end apart: 37, of which 12 were waited for; matrix products, arithmetic and copies ran while one was open for 4% of the time, Pallas kernels for 19%

profile of v4, /device:TPU:0, one launch (start us, length us, event | category | flops | bytes accessed | tf_op | source)
XLA Modules:
  0.0 163.5 jit_solution(11772470171690700415)
XLA Ops:
  0.7 1.7 %fusion.1 = (f32[512]{0:T(512)S(1)}, bf16[512,1152]{1,0:T(8,128)(2,1)S(1)}) fusion(bf16[512,1152]{1,0:T(8,128)(2,1)} %param.9, f32[1152]{0:T(1024)S(1)} %convert_reduce_fusion.1), kind=kLoop, calls=%fused_computation.3 | loop fusion | flops 2948608 | bytes 2365952 | tf_op jit(solution)/shard_map/reduce_sum | solution.py:233
  3.9 2.5 %collective-permute-start.4 = (bf16[128,1152]{1,0:T(8,128)(2,1)S(1)}, bf16[128,1152]{1,0:T(8,128)(2,1)S(1)}, u32[]{:S(2)}, u32[]{:S(2)}) collective-permute-start(bf16[128,1152]{1,0:T(8,128)(2,1)S(1)} %get-tuple-element.39.refs_0_), channel_id=1, source_target_pairs={{0,2},{1,3},{2,0},{3,1},{4,6},{5,7},{6,4},{7,5},{8,10},{9,11},{10,... | collective-permute-start | bytes 884744 | tf_op jit(solution)/shard_map/ppermute | solution.py:194
  11.0 3.1 %collective-permute-done.4.refs_2_ = bf16[128,1152]{1,0:T(8,128)(2,1)S(1)} collective-permute-done((bf16[128,1152]{1,0:T(8,128)(2,1)S(1)}, bf16[128,1152]{1,0:T(8,128)(2,1)S(1)}, u32[]{:S(2)}, u32[]{:S(2)}) %collective-permute-start.4) | collective-permute-done | bytes 294944 | tf_op jit(solution)/shard_map/ppermute | solution.py:194
  14.7 1.7 %collective-permute-start.7 = (bf16[128,1152]{1,0:T(8,128)(2,1)S(1)}, bf16[128,1152]{1,0:T(8,128)(2,1)}, u32[]{:S(2)}, u32[]{:S(2)}) collective-permute-start(bf16[128,1152]{1,0:T(8,128)(2,1)S(1)} %get-tuple-element.26.refs_0_.refs_4_), channel_id=1, source_target_pairs={{0,2},{1,3},{2,0},{3,1},{4,6},{5,7},{6,4},{7,5},{8,10},{9,11},{10,... | collective-permute-start | bytes 884744 | tf_op jit(solution)/shard_map/ppermute | solution.py:194
  18.6 6.1 %collective-permute-done.7.refs_2_.refs_6_ = bf16[128,1152]{1,0:T(8,128)(2,1)} collective-permute-done((bf16[128,1152]{1,0:T(8,128)(2,1)S(1)}, bf16[128,1152]{1,0:T(8,128)(2,1)}, u32[]{:S(2)}, u32[]{:S(2)}) %collective-permute-start.7) | collective-permute-done | bytes 294944 | tf_op jit(solution)/shard_map/ppermute | solution.py:194
  24.7 2.3 %copy-done.1 = bf16[4608,512]{1,0:T(8,128)(2,1)S(1)} copy-done((bf16[4608,512]{1,0:T(8,128)(2,1)S(1)}, bf16[4608,512]{1,0:T(8,128)(2,1)}, u32[]{:S(2)}) %copy-start.1) | copy-done | bytes 4718616
  27.1 2.3 %copy-done.2 = bf16[4608,512]{1,0:T(8,128)(2,1)S(1)} copy-done((bf16[4608,512]{1,0:T(8,128)(2,1)S(1)}, bf16[4608,512]{1,0:T(8,128)(2,1)}, u32[]{:S(2)}) %copy-start.2) | copy-done | bytes 4718616
  29.4 2.1 %project.4 = bf16[2,128,512]{2,1,0:T(8,128)(2,1)S(1)} custom-call(s32[4]{0:T(128)S(1)} %pad_add_fusion.2.rank_ref, f32[128,1]{1,0:T(8,128)S(1)} %copy.12.inverse_ref, bf16[128,1152]{1,0:T(8,128)(2,1)S(1)} %get-tuple-element.39.refs_0_, bf16[128,1152]{1,0:T(8,128)(2,1)S(1)} %collective-permute-done.refs_1_, ...), custom_call_target="tpu_custom_call" | custom-call | flops 10000000000 | bytes 1000000 | tf_op jit(solution)/shard_map/project/pallas_call | solution.py:63
  31.6 1.9 %collective-permute-start.12 = (bf16[2,128,512]{2,1,0:T(8,128)(2,1)S(1)}, bf16[2,128,512]{2,1,0:T(8,128)(2,1)}, u32[]{:S(2)}, u32[]{:S(2)}) collective-permute-start(bf16[2,128,512]{2,1,0:T(8,128)(2,1)S(1)} %project.4), channel_id=1, source_target_pairs={{0,4},{4,0},{8,12},{12,8},{1,5},{5,1},{9,13},{13,9},{2,6},{6,2},{1... | collective-permute-start | bytes 786440 | tf_op jit(solution)/shard_map/ppermute | solution.py:245
  36.4 2.7 %project.5 = bf16[2,128,512]{2,1,0:T(8,128)(2,1)S(1)} custom-call(s32[4]{0:T(128)S(1)} %pad_add_fusion.2.rank_ref, f32[128,1]{1,0:T(8,128)S(1)} %copy.13.inverse_ref, bf16[128,1152]{1,0:T(8,128)(2,1)S(1)} %get-tuple-element.26.refs_0_.refs_4_, bf16[128,1152]{1,0:T(8,128)(2,1)S(1)} %copy-done.12, bf16[128,1152]{1,0:T(8,128)(2,1)} %collective-permute-done.7.refs_2_.refs_6_, ...), custom_call_target="tpu_custom_call" | custom-call | flops 10000000000 | bytes 1000000 | tf_op jit(solution)/shard_map/project/pallas_call | solution.py:63
  39.1 3.4 %project.7 = bf16[2,256,512]{2,1,0:T(8,128)(2,1)S(1)} custom-call(s32[4]{0:T(128)S(1)} %pad_add_fusion.2.rank_ref, f32[256,1]{1,0:T(8,128)S(1)} %copy.15.inverse_ref, bf16[256,1152]{1,0:T(8,128)(2,1)S(1)} %slice.87.refs_8_.refs_0_, bf16[256,1152]{1,0:T(8,128)(2,1)S(1)} %collective-permute-done.9.refs_9_.refs_1_, ...), custom_call_target="tpu_custom_call" | custom-call | flops 10000000000 | bytes 1000000 | tf_op jit(solution)/shard_map/project/pallas_call | solution.py:63
  42.6 1.9 %collective-permute-start.14 = (bf16[2,256,512]{2,1,0:T(8,128)(2,1)S(1)}, bf16[2,256,512]{2,1,0:T(8,128)(2,1)}, u32[]{:S(2)}, u32[]{:S(2)}) collective-permute-start(bf16[2,256,512]{2,1,0:T(8,128)(2,1)S(1)} %project.7), channel_id=1, source_target_pairs={{0,4},{4,0},{8,12},{12,8},{1,5},{5,1},{9,13},{13,9},{2,6},{6,2},{1... | collective-permute-start | bytes 1572872 | tf_op jit(solution)/shard_map/ppermute | solution.py:245
  46.3 1.7 %collective-permute-start.16 = (bf16[2,128,512]{2,1,0:T(8,128)(2,1)}, bf16[2,128,512]{2,1,0:T(8,128)(2,1)S(1)}, u32[]{:S(2)}, u32[]{:S(2)}) collective-permute-start(bf16[2,128,512]{2,1,0:T(8,128)(2,1)} %collective-permute-done.15), channel_id=1, source_target_pairs={{0,4},{4,0},{8,12},{12,8},{1,5},{5,1},{9,13},{13,9},{2,6},{6,2},{1... | collective-permute-start | bytes 786440 | tf_op jit(solution)/shard_map/ppermute | solution.py:245
  49.6 9.8 %collective-permute-done.19 = bf16[2,256,512]{2,1,0:T(8,128)(2,1)} collective-permute-done((bf16[2,256,512]{2,1,0:T(8,128)(2,1)S(1)}, bf16[2,256,512]{2,1,0:T(8,128)(2,1)}, u32[]{:S(2)}, u32[]{:S(2)}) %collective-permute-start.19) | collective-permute-done | bytes 524320 | tf_op jit(solution)/shard_map/ppermute | solution.py:250
  62.0 3.7 %copy-done = bf16[4608,1024]{1,0:T(8,128)(2,1)S(1)} copy-done((bf16[4608,1024]{1,0:T(8,128)(2,1)S(1)}, bf16[4608,1024]{1,0:T(8,128)(2,1)}, u32[]{:S(2)}) %copy-start) | copy-done | bytes 9437208
  71.7 6.6 %project.6.q_ref = bf16[1,512,1024]{2,1,0:T(8,128)(2,1)S(1)} custom-call(s32[4]{0:T(128)S(1)} %pad_add_fusion.2.rank_ref, f32[512,1]{1,0:T(8,128)S(1)} %copy.14.inverse_ref, bf16[128,1152]{1,0:T(8,128)(2,1)S(1)} %get-tuple-element.39.refs_0_, bf16[128,1152]{1,0:T(8,128)(2,1)S(1)} %collective-permute-done.refs_1_, bf16[128,1152]{1,0:T(8,128)(2,1)S(1)} %copy-done.8, ...), custom_call_target="tpu_custom_call" | custom-call | flops 10000000000 | bytes 1000000 | tf_op jit(solution)/shard_map/project/pallas_call | solution.py:63
  82.6 5.2 %collective-permute-done.21 = bf16[2,128,512]{2,1,0:T(8,128)(2,1)S(1)} collective-permute-done((bf16[2,128,512]{2,1,0:T(8,128)(2,1)}, bf16[2,128,512]{2,1,0:T(8,128)(2,1)S(1)}, u32[]{:S(2)}, u32[]{:S(2)}) %collective-permute-start.21) | collective-permute-done | bytes 262176 | tf_op jit(solution)/shard_map/ppermute | solution.py:250
  88.7 2.4 %collective-permute-done.23 = bf16[2,128,512]{2,1,0:T(8,128)(2,1)S(1)} collective-permute-done((bf16[2,128,512]{2,1,0:T(8,128)(2,1)S(1)}, bf16[2,128,512]{2,1,0:T(8,128)(2,1)S(1)}, u32[]{:S(2)}, u32[]{:S(2)}) %collective-permute-start.23) | collective-permute-done | bytes 262176 | tf_op jit(solution)/shard_map/ppermute | solution.py:250
  91.5 1.6 collective-permute-start.26
  93.1 1.6 maximum_select_fusion.refs_4_.refs_5_
  94.7 11.8 %attention.2 = (f32[512,1024]{1,0:T(8,128)S(1)}, f32[512,512]{1,0:T(8,128)S(1)}) custom-call(f32[4,1536]{1,0:T(4,128)S(1)} %slice.88.bias_ref, bf16[1,512,1024]{2,1,0:T(8,128)(2,1)S(1)} %project.6.q_ref, bf16[2,512,512]{2,1,0:T(8,128)(2,1)S(1)} %pad_maximum_fusion.1.refs_0_.refs_1_, bf16[2,512,512]{2,1,0:T(8,128)(2,1)S(1)} %pad_maximum_fusion.1.refs_0_.refs_1_, ...), custom_call_target="tpu_custom_call" | custom-call | flops 10000000000 | bytes 1000000 | tf_op jit(solution)/shard_map/attention/pallas_call | solution.py:157
  106.5 4.5 %collective-permute-done.26 = bf16[2,256,512]{2,1,0:T(8,128)(2,1)S(1)} collective-permute-done((bf16[2,256,512]{2,1,0:T(8,128)(2,1)S(1)}, bf16[2,256,512]{2,1,0:T(8,128)(2,1)S(1)}, u32[]{:S(2)}, u32[]{:S(2)}) %collective-permute-start.26) | collective-permute-done | bytes 524320 | tf_op jit(solution)/shard_map/ppermute | solution.py:245
  111.4 7.6 %attention.3 = bf16[512,1024]{1,0:T(8,128)(2,1)S(1)} custom-call(f32[4,512]{1,0:T(4,128)S(1)} %slice.84.bias_ref, bf16[1,512,1024]{2,1,0:T(8,128)(2,1)S(1)} %project.6.q_ref, bf16[2,512,512]{2,1,0:T(8,128)(2,1)S(1)} %maximum_select_fusion.1.refs_0_.refs_1_, bf16[2,512,512]{2,1,0:T(8,128)(2,1)S(1)} %maximum_select_fusion.1.refs_0_.refs_1_, ...), custom_call_target="tpu_custom_call" | custom-call | flops 10000000000 | bytes 1000000 | tf_op jit(solution)/shard_map/attention/pallas_call | solution.py:157
  119.0 2.1 %output.5 = bf16[2,256,1152]{2,1,0:T(8,128)(2,1)S(1)} custom-call(s32[2]{0:T(128)S(1)} %pad_add_fusion.3.block_ref, bf16[256,1024]{1,0:T(8,128)(2,1)S(1)} %get-tuple-element.43.x_ref, bf16[1024,4608]{1,0:T(8,128)(2,1)S(1)} %bitcast.41), custom_call_target="tpu_custom_call" | custom-call | flops 1 | bytes 1 | tf_op jit(solution)/shard_map/output/pallas_call | solution.py:178
  121.3 2.1 %output.4 = bf16[2,256,1152]{2,1,0:T(8,128)(2,1)S(1)} custom-call(s32[2]{0:T(128)S(1)} %pad_add_fusion.block_ref, bf16[256,1024]{1,0:T(8,128)(2,1)S(1)} %get-tuple-element.43.x_ref, bf16[1024,4608]{1,0:T(8,128)(2,1)S(1)} %bitcast.41), custom_call_target="tpu_custom_call" | custom-call | flops 1 | bytes 1 | tf_op jit(solution)/shard_map/output/pallas_call | solution.py:178
  124.2 2.1 %output.7 = bf16[2,256,1152]{2,1,0:T(8,128)(2,1)S(1)} custom-call(s32[2]{0:T(128)S(1)} %pad_add_fusion.3.block_ref, bf16[256,1024]{1,0:T(8,128)(2,1)S(1)} %get-tuple-element.38.x_ref, bf16[1024,4608]{1,0:T(8,128)(2,1)S(1)} %bitcast.41), custom_call_target="tpu_custom_call" | custom-call | flops 1 | bytes 1 | tf_op jit(solution)/shard_map/output/pallas_call | solution.py:178
  126.5 2.1 %output.6 = bf16[2,256,1152]{2,1,0:T(8,128)(2,1)S(1)} custom-call(s32[2]{0:T(128)S(1)} %pad_add_fusion.block_ref, bf16[256,1024]{1,0:T(8,128)(2,1)S(1)} %get-tuple-element.38.x_ref, bf16[1024,4608]{1,0:T(8,128)(2,1)S(1)} %bitcast.41), custom_call_target="tpu_custom_call" | custom-call | flops 1 | bytes 1 | tf_op jit(solution)/shard_map/output/pallas_call | solution.py:178
  128.6 1.6 collective-permute-start.28
  130.9 13.9 %collective-permute-done.28 = bf16[256,1152]{1,0:T(8,128)(2,1)S(1)} collective-permute-done((bf16[256,1152]{1,0:T(8,128)(2,1)S(1)}, bf16[256,1152]{1,0:T(8,128)(2,1)S(1)}, u32[]{:S(2)}, u32[]{:S(2)}) %collective-permute-start.28) | collective-permute-done | bytes 589856 | tf_op jit(solution)/shard_map/ppermute | solution.py:194
  145.2 1.6 collective-permute-start.30
  147.4 9.5 %collective-permute-done.33 = bf16[256,1152]{1,0:T(8,128)(2,1)S(1)} collective-permute-done((bf16[256,1152]{1,0:T(8,128)(2,1)S(1)}, bf16[256,1152]{1,0:T(8,128)(2,1)S(1)}, u32[]{:S(2)}, u32[]{:S(2)}) %collective-permute-start.33) | collective-permute-done | bytes 589856 | tf_op jit(solution)/shard_map/ppermute | solution.py:194
  157.2 1.6 collective-permute-start.35
  (143 shorter events, 38.3 us)
Async XLA Ops:
  3.4 4.2 %collective-permute-start = (bf16[128,1152]{1,0:T(8,128)(2,1)S(1)}, bf16[128,1152]{1,0:T(8,128)(2,1)S(1)}, u32[]{:S(2)}, u32[]{:S(2)}) collective-permute-start(bf16[128,1152]{1,0:T(8,128)(2,1)S(1)} %get-tuple-element.39.refs_0_), channel_id=1, source_target_pairs={{0,1},{1,0},{2,3},{3,2},{4,5},{5,4},{6,7},{7,6},{8,9},{9,8},{10,11... | collective-permute-start | bytes 884744 | tf_op jit(solution)/shard_map/ppermute | solution.py:194
  3.9 10.2 %collective-permute-start.4 = (bf16[128,1152]{1,0:T(8,128)(2,1)S(1)}, bf16[128,1152]{1,0:T(8,128)(2,1)S(1)}, u32[]{:S(2)}, u32[]{:S(2)}) collective-permute-start(bf16[128,1152]{1,0:T(8,128)(2,1)S(1)} %get-tuple-element.39.refs_0_), channel_id=1, source_target_pairs={{0,2},{1,3},{2,0},{3,1},{4,6},{5,7},{6,4},{7,5},{8,10},{9,11},{10,... | collective-permute-start | bytes 884744 | tf_op jit(solution)/shard_map/ppermute | solution.py:194
  7.6 6.5 %collective-permute-start.2 = (f32[512]{0:T(512)S(1)}, f32[512]{0:T(512)S(1)}, u32[]{:S(2)}, u32[]{:S(2)}) collective-permute-start(f32[512]{0:T(512)S(1)} %get-tuple-element.22), channel_id=1, source_target_pairs={{0,2},{1,3},{2,0},{3,1},{4,6},{5,7},{6,4},{7,5},{8,10},{9,11},{10,... | collective-permute-start | bytes 6152 | tf_op jit(solution)/shard_map/ppermute | solution.py:194
  8.0 6.2 %collective-permute-start.3 = (f32[512]{0:T(512)S(1)}, f32[512]{0:T(512)S(1)}, u32[]{:S(2)}, u32[]{:S(2)}) collective-permute-start(f32[512]{0:T(512)S(1)} %get-tuple-element.22), channel_id=1, source_target_pairs={{0,3},{1,2},{2,1},{3,0},{4,7},{5,6},{6,5},{7,4},{8,11},{9,10},{10,... | collective-permute-start | bytes 6152 | tf_op jit(solution)/shard_map/ppermute | solution.py:194
  9.3 4.9 %collective-permute-start.1 = (f32[512]{0:T(512)S(1)}, f32[512]{0:T(512)S(1)}, u32[]{:S(2)}, u32[]{:S(2)}) collective-permute-start(f32[512]{0:T(512)S(1)} %get-tuple-element.22), channel_id=1, source_target_pairs={{0,1},{1,0},{2,3},{3,2},{4,5},{5,4},{6,7},{7,6},{8,9},{9,8},{10,11... | collective-permute-start | bytes 6152 | tf_op jit(solution)/shard_map/ppermute | solution.py:194
  14.1 10.6 %collective-permute-start.5 = (bf16[128,1152]{1,0:T(8,128)(2,1)S(1)}, bf16[128,1152]{1,0:T(8,128)(2,1)S(1)}, u32[]{:S(2)}, u32[]{:S(2)}) collective-permute-start(bf16[128,1152]{1,0:T(8,128)(2,1)S(1)} %collective-permute-done.4.refs_2_), channel_id=1, source_target_pairs={{0,1},{1,0},{2,3},{3,2},{4,5},{5,4},{6,7},{7,6},{8,9},{9,8},{10,11... | collective-permute-start | bytes 884744 | tf_op jit(solution)/shard_map/ppermute | solution.py:194
  14.7 10.0 %collective-permute-start.7 = (bf16[128,1152]{1,0:T(8,128)(2,1)S(1)}, bf16[128,1152]{1,0:T(8,128)(2,1)}, u32[]{:S(2)}, u32[]{:S(2)}) collective-permute-start(bf16[128,1152]{1,0:T(8,128)(2,1)S(1)} %get-tuple-element.26.refs_0_.refs_4_), channel_id=1, source_target_pairs={{0,2},{1,3},{2,0},{3,1},{4,6},{5,7},{6,4},{7,5},{8,10},{9,11},{10,... | collective-permute-start | bytes 884744 | tf_op jit(solution)/shard_map/ppermute | solution.py:194
  17.6 18.8 %collective-permute-start.10 = (bf16[256,1152]{1,0:T(8,128)(2,1)S(1)}, bf16[256,1152]{1,0:T(8,128)(2,1)S(1)}, u32[]{:S(2)}, u32[]{:S(2)}) collective-permute-start(bf16[256,1152]{1,0:T(8,128)(2,1)S(1)} %slice.87.refs_8_.refs_0_), channel_id=1, source_target_pairs={{0,2},{1,3},{2,0},{3,1},{4,6},{5,7},{6,4},{7,5},{8,10},{9,11},{10,... | collective-permute-start | bytes 1769480 | tf_op jit(solution)/shard_map/ppermute | solution.py:194
  24.7 11.7 %collective-permute-start.8 = (bf16[128,1152]{1,0:T(8,128)(2,1)}, bf16[128,1152]{1,0:T(8,128)(2,1)S(1)}, u32[]{:S(2)}, u32[]{:S(2)}) collective-permute-start(bf16[128,1152]{1,0:T(8,128)(2,1)} %collective-permute-done.7.refs_2_.refs_6_), channel_id=1, source_target_pairs={{0,1},{1,0},{2,3},{3,2},{4,5},{5,4},{6,7},{7,6},{8,9},{9,8},{10,11... | collective-permute-start | bytes 884744 | tf_op jit(solution)/shard_map/ppermute | solution.py:194
  31.6 16.8 %collective-permute-start.12 = (bf16[2,128,512]{2,1,0:T(8,128)(2,1)S(1)}, bf16[2,128,512]{2,1,0:T(8,128)(2,1)}, u32[]{:S(2)}, u32[]{:S(2)}) collective-permute-start(bf16[2,128,512]{2,1,0:T(8,128)(2,1)S(1)} %project.4), channel_id=1, source_target_pairs={{0,4},{4,0},{8,12},{12,8},{1,5},{5,1},{9,13},{13,9},{2,6},{6,2},{1... | collective-permute-start | bytes 786440 | tf_op jit(solution)/shard_map/ppermute | solution.py:245
  33.5 12.8 %collective-permute-start.15 = (bf16[2,128,512]{2,1,0:T(8,128)(2,1)S(1)}, bf16[2,128,512]{2,1,0:T(8,128)(2,1)}, u32[]{:S(2)}, u32[]{:S(2)}) collective-permute-start(bf16[2,128,512]{2,1,0:T(8,128)(2,1)S(1)} %project.4), channel_id=1, source_target_pairs={{0,16},{16,0},{12,28},{28,12},{4,8},{8,4},{20,24},{24,20},{1,17},{... | collective-permute-start | bytes 786440 | tf_op jit(solution)/shard_map/ppermute | solution.py:250
  35.0 4.1 %collective-permute-start.9 = (bf16[256,1152]{1,0:T(8,128)(2,1)S(1)}, bf16[256,1152]{1,0:T(8,128)(2,1)S(1)}, u32[]{:S(2)}, u32[]{:S(2)}) collective-permute-start(bf16[256,1152]{1,0:T(8,128)(2,1)S(1)} %slice.87.refs_8_.refs_0_), channel_id=1, source_target_pairs={{0,1},{1,0},{2,3},{3,2},{4,5},{5,4},{6,7},{7,6},{8,9},{9,8},{10,11... | collective-permute-start | bytes 1769480 | tf_op jit(solution)/shard_map/ppermute | solution.py:194
  42.6 17.9 %collective-permute-start.14 = (bf16[2,256,512]{2,1,0:T(8,128)(2,1)S(1)}, bf16[2,256,512]{2,1,0:T(8,128)(2,1)}, u32[]{:S(2)}, u32[]{:S(2)}) collective-permute-start(bf16[2,256,512]{2,1,0:T(8,128)(2,1)S(1)} %project.7), channel_id=1, source_target_pairs={{0,4},{4,0},{8,12},{12,8},{1,5},{5,1},{9,13},{13,9},{2,6},{6,2},{1... | collective-permute-start | bytes 1572872 | tf_op jit(solution)/shard_map/ppermute | solution.py:245
  44.5 14.9 %collective-permute-start.19 = (bf16[2,256,512]{2,1,0:T(8,128)(2,1)S(1)}, bf16[2,256,512]{2,1,0:T(8,128)(2,1)}, u32[]{:S(2)}, u32[]{:S(2)}) collective-permute-start(bf16[2,256,512]{2,1,0:T(8,128)(2,1)S(1)} %project.7), channel_id=1, source_target_pairs={{0,16},{16,0},{12,28},{28,12},{4,8},{8,4},{20,24},{24,20},{1,17},{... | collective-permute-start | bytes 1572872 | tf_op jit(solution)/shard_map/ppermute | solution.py:250
  46.3 32.0 %collective-permute-start.16 = (bf16[2,128,512]{2,1,0:T(8,128)(2,1)}, bf16[2,128,512]{2,1,0:T(8,128)(2,1)S(1)}, u32[]{:S(2)}, u32[]{:S(2)}) collective-permute-start(bf16[2,128,512]{2,1,0:T(8,128)(2,1)} %collective-permute-done.15), channel_id=1, source_target_pairs={{0,4},{4,0},{8,12},{12,8},{1,5},{5,1},{9,13},{13,9},{2,6},{6,2},{1... | collective-permute-start | bytes 786440 | tf_op jit(solution)/shard_map/ppermute | solution.py:245
  48.0 31.8 %collective-permute-start.13 = (bf16[2,128,512]{2,1,0:T(8,128)(2,1)S(1)}, bf16[2,128,512]{2,1,0:T(8,128)(2,1)S(1)}, u32[]{:S(2)}, u32[]{:S(2)}) collective-permute-start(bf16[2,128,512]{2,1,0:T(8,128)(2,1)S(1)} %project.5), channel_id=1, source_target_pairs={{0,4},{4,0},{8,12},{12,8},{1,5},{5,1},{9,13},{13,9},{2,6},{6,2},{1... | collective-permute-start | bytes 786440 | tf_op jit(solution)/shard_map/ppermute | solution.py:245
  48.4 30.5 %collective-permute-start.17 = (bf16[2,128,512]{2,1,0:T(8,128)(2,1)S(1)}, bf16[2,128,512]{2,1,0:T(8,128)(2,1)S(1)}, u32[]{:S(2)}, u32[]{:S(2)}) collective-permute-start(bf16[2,128,512]{2,1,0:T(8,128)(2,1)S(1)} %project.5), channel_id=1, source_target_pairs={{0,16},{16,0},{12,28},{28,12},{4,8},{8,4},{20,24},{24,20},{1,17},{... | collective-permute-start | bytes 786440 | tf_op jit(solution)/shard_map/ppermute | solution.py:250
  59.4 33.7 %collective-permute-start.20 = (bf16[2,256,512]{2,1,0:T(8,128)(2,1)}, bf16[2,256,512]{2,1,0:T(8,128)(2,1)S(1)}, u32[]{:S(2)}, u32[]{:S(2)}) collective-permute-start(bf16[2,256,512]{2,1,0:T(8,128)(2,1)} %collective-permute-done.19), channel_id=1, source_target_pairs={{0,4},{4,0},{8,12},{12,8},{1,5},{5,1},{9,13},{13,9},{2,6},{6,2},{1... | collective-permute-start | bytes 1572872 | tf_op jit(solution)/shard_map/ppermute | solution.py:245
  60.5 31.0 %collective-permute-start.25 = (bf16[2,256,512]{2,1,0:T(8,128)(2,1)}, bf16[2,256,512]{2,1,0:T(8,128)(2,1)S(1)}, u32[]{:S(2)}, u32[]{:S(2)}) collective-permute-start(bf16[2,256,512]{2,1,0:T(8,128)(2,1)} %collective-permute-done.14), channel_id=1, source_target_pairs={{0,16},{16,0},{12,28},{28,12},{4,8},{8,4},{20,24},{24,20},{1,17},{... | collective-permute-start | bytes 1572872 | tf_op jit(solution)/shard_map/ppermute | solution.py:250
  78.3 9.5 %collective-permute-start.21 = (bf16[2,128,512]{2,1,0:T(8,128)(2,1)}, bf16[2,128,512]{2,1,0:T(8,128)(2,1)S(1)}, u32[]{:S(2)}, u32[]{:S(2)}) collective-permute-start(bf16[2,128,512]{2,1,0:T(8,128)(2,1)} %collective-permute-done.12), channel_id=1, source_target_pairs={{0,16},{16,0},{12,28},{28,12},{4,8},{8,4},{20,24},{24,20},{1,17},{... | collective-permute-start | bytes 786440 | tf_op jit(solution)/shard_map/ppermute | solution.py:250
  78.9 14.2 %collective-permute-start.18 = (bf16[2,128,512]{2,1,0:T(8,128)(2,1)S(1)}, bf16[2,128,512]{2,1,0:T(8,128)(2,1)S(1)}, u32[]{:S(2)}, u32[]{:S(2)}) collective-permute-start(bf16[2,128,512]{2,1,0:T(8,128)(2,1)S(1)} %collective-permute-done.17), channel_id=1, source_target_pairs={{0,4},{4,0},{8,12},{12,8},{1,5},{5,1},{9,13},{13,9},{2,6},{6,2},{1... | collective-permute-start | bytes 786440 | tf_op jit(solution)/shard_map/ppermute | solution.py:245
  79.8 11.2 %collective-permute-start.23 = (bf16[2,128,512]{2,1,0:T(8,128)(2,1)S(1)}, bf16[2,128,512]{2,1,0:T(8,128)(2,1)S(1)}, u32[]{:S(2)}, u32[]{:S(2)}) collective-permute-start(bf16[2,128,512]{2,1,0:T(8,128)(2,1)S(1)} %collective-permute-done.13), channel_id=1, source_target_pairs={{0,16},{16,0},{12,28},{28,12},{4,8},{8,4},{20,24},{24,20},{1,17},{... | collective-permute-start | bytes 786440 | tf_op jit(solution)/shard_map/ppermute | solution.py:250
  87.8 18.7 %collective-permute-start.22 = (bf16[2,128,512]{2,1,0:T(8,128)(2,1)S(1)}, bf16[2,128,512]{2,1,0:T(8,128)(2,1)S(1)}, u32[]{:S(2)}, u32[]{:S(2)}) collective-permute-start(bf16[2,128,512]{2,1,0:T(8,128)(2,1)S(1)} %collective-permute-done.21), channel_id=1, source_target_pairs={{0,4},{4,0},{8,12},{12,8},{1,5},{5,1},{9,13},{13,9},{2,6},{6,2},{1... | collective-permute-start | bytes 786440 | tf_op jit(solution)/shard_map/ppermute | solution.py:245
  91.1 15.4 %collective-permute-start.24 = (bf16[2,128,512]{2,1,0:T(8,128)(2,1)S(1)}, bf16[2,128,512]{2,1,0:T(8,128)(2,1)S(1)}, u32[]{:S(2)}, u32[]{:S(2)}) collective-permute-start(bf16[2,128,512]{2,1,0:T(8,128)(2,1)S(1)} %collective-permute-done.23), channel_id=1, source_target_pairs={{0,4},{4,0},{8,12},{12,8},{1,5},{5,1},{9,13},{13,9},{2,6},{6,2},{1... | collective-permute-start | bytes 786440 | tf_op jit(solution)/shard_map/ppermute | solution.py:245
  91.5 19.6 %collective-permute-start.26 = (bf16[2,256,512]{2,1,0:T(8,128)(2,1)S(1)}, bf16[2,256,512]{2,1,0:T(8,128)(2,1)S(1)}, u32[]{:S(2)}, u32[]{:S(2)}) collective-permute-start(bf16[2,256,512]{2,1,0:T(8,128)(2,1)S(1)} %collective-permute-done.25), channel_id=1, source_target_pairs={{0,4},{4,0},{8,12},{12,8},{1,5},{5,1},{9,13},{13,9},{2,6},{6,2},{1... | collective-permute-start | bytes 1572872 | tf_op jit(solution)/shard_map/ppermute | solution.py:245
  126.3 3.9 %collective-permute-start.32 = (bf16[2,256,1152]{2,1,0:T(8,128)(2,1)S(1)}, bf16[2,256,1152]{2,1,0:T(8,128)(2,1)S(1)}, u32[]{:S(2)}, u32[]{:S(2)}) collective-permute-start(bf16[2,256,1152]{2,1,0:T(8,128)(2,1)S(1)} %output.7), channel_id=1, source_target_pairs={{0,1},{1,0},{2,3},{3,2},{4,5},{5,4},{6,7},{7,6},{8,9},{9,8},{10,11... | collective-permute-start | bytes 3538952 | tf_op jit(solution)/shard_map/ppermute | solution.py:194
  128.6 16.3 %collective-permute-start.28 = (bf16[256,1152]{1,0:T(8,128)(2,1)S(1)}, bf16[256,1152]{1,0:T(8,128)(2,1)S(1)}, u32[]{:S(2)}, u32[]{:S(2)}) collective-permute-start(bf16[256,1152]{1,0:T(8,128)(2,1)S(1)} %fusion.3), channel_id=1, source_target_pairs={{0,2},{1,3},{2,0},{3,1},{4,6},{5,7},{6,4},{7,5},{8,10},{9,11},{10,... | collective-permute-start | bytes 1769480 | tf_op jit(solution)/shard_map/ppermute | solution.py:194
  130.3 26.6 %collective-permute-start.33 = (bf16[256,1152]{1,0:T(8,128)(2,1)S(1)}, bf16[256,1152]{1,0:T(8,128)(2,1)S(1)}, u32[]{:S(2)}, u32[]{:S(2)}) collective-permute-start(bf16[256,1152]{1,0:T(8,128)(2,1)S(1)} %fusion.4), channel_id=1, source_target_pairs={{0,2},{1,3},{2,0},{3,1},{4,6},{5,7},{6,4},{7,5},{8,10},{9,11},{10,... | collective-permute-start | bytes 1769480 | tf_op jit(solution)/shard_map/ppermute | solution.py:194
  145.2 13.6 %collective-permute-start.30 = (f32[256]{0:T(256)S(1)}, f32[256]{0:T(256)S(1)}, u32[]{:S(2)}, u32[]{:S(2)}) collective-permute-start(f32[256]{0:T(256)S(1)} %multiply_reduce_fusion.1), channel_id=1, source_target_pairs={{0,2},{1,3},{2,0},{3,1},{4,6},{5,7},{6,4},{7,5},{8,10},{9,11},{10,... | collective-permute-start | bytes 3080 | tf_op jit(solution)/shard_map/ppermute | solution.py:194
  146.7 12.7 %collective-permute-start.31 = (f32[256]{0:T(256)S(1)}, f32[256]{0:T(256)S(1)}, u32[]{:S(2)}, u32[]{:S(2)}) collective-permute-start(f32[256]{0:T(256)S(1)} %multiply_reduce_fusion.1), channel_id=1, source_target_pairs={{0,3},{1,2},{2,1},{3,0},{4,7},{5,6},{6,5},{7,4},{8,11},{9,10},{10,... | collective-permute-start | bytes 3080 | tf_op jit(solution)/shard_map/ppermute | solution.py:194
  146.7 12.7 %collective-permute-start.29 = (f32[256]{0:T(256)S(1)}, f32[256]{0:T(256)S(1)}, u32[]{:S(2)}, u32[]{:S(2)}) collective-permute-start(f32[256]{0:T(256)S(1)} %multiply_reduce_fusion.1), channel_id=1, source_target_pairs={{0,1},{1,0},{2,3},{3,2},{4,5},{5,4},{6,7},{7,6},{8,9},{9,8},{10,11... | collective-permute-start | bytes 3080 | tf_op jit(solution)/shard_map/ppermute | solution.py:194
  157.2 3.6 %collective-permute-start.35 = (f32[256]{0:T(256)S(1)}, f32[256]{0:T(256)S(1)}, u32[]{:S(2)}, u32[]{:S(2)}) collective-permute-start(f32[256]{0:T(256)S(1)} %multiply_reduce_fusion), channel_id=1, source_target_pairs={{0,2},{1,3},{2,0},{3,1},{4,6},{5,7},{6,4},{7,5},{8,10},{9,11},{10,... | collective-permute-start | bytes 3080 | tf_op jit(solution)/shard_map/ppermute | solution.py:194
  (29 other events, 113.3 us)

commit v5 on v4

--- a/solution.py
+++ b/solution.py
@@ -185,7 +185,7 @@
         out_specs=pl.BlockSpec(memory_space=pltpu.VMEM),
         out_shape=jax.ShapeDtypeStruct((block_ids.shape[0], rows, features), jnp.bfloat16),
         compiler_params=pltpu.CompilerParams(vmem_limit_bytes=24 * 2**20),
-        cost_estimate=SHORT,
+        cost_estimate=LONG,
         name="output",
     )(block_ids, attended, w_out)
 
@@ -226,14 +226,13 @@
         if c == 1:
             own, square_sum = lax.optimization_barrier((own, square_sum))
         if c > 1:
-            own, blocks[c - 1][1] = lax.optimization_barrier((own, blocks[c - 1][1]))
+            own, _ = lax.optimization_barrier((own, blocks[c - 2][2]))
         far = swap(own, 2)
-        near = swap(own, 1)
         if c == 0:
             squares = jnp.sum(wide * wide, axis=1)
-            squares, near = lax.optimization_barrier((squares, near))
+            squares, own = lax.optimization_barrier((squares, own))
             square_sum = sum_over_tensor(squares)
-        blocks.append([own, near, far, swap(far, 1)])
+        blocks.append([own, swap(own, 1), far, swap(far, 1)])
     inverse = lax.rsqrt(square_sum / model_width + epsilon)[:, None]
 
     key_values = []

time: 164 us -> 158 us (0.963)
  waiting for transfers between devices: 59 us -> 54.9 us
  local copies, waits for them, and re-layouts: 17.9 us -> 15.3 us
    ppermute x22, waiting for transfers between devices: 37.1 us -> 33.5 us  [swap(): return lax.ppermute(x, 'tensor', [(t, t ^ bit) for t in range(4)])]
    unnamed x49 -> x43, local copies, waits for them, and re-layouts: 16.1 us -> 13.5 us
  transfers between devices with their start and end apart: 37 -> 37, of which waited for: 12 -> 12; matrix products, arithmetic and copies ran while one was open for 4% -> 4% of each run, Pallas kernels for 19% -> 20%
where the time goes in v5:
time: 158 us
  waiting for transfers between devices  54.9 us (35%)
  Pallas kernels  43.3 us (27%)
  starting transfers between devices  34 us (22%)
  local copies, waits for them, and re-layouts  15.3 us (10%)
  other arithmetic  8.62 us (5%)
    ppermute x22, waiting for transfers between devices, swap(): return lax.ppermute(x, 'tensor', [(t, t ^ bit) for t in range(4)])  33.5 us
    pallas_call x2, Pallas kernels, attention(): pl.pallas_call(functools.partial(attention_body, slots=len(slots), begun=...  19.4 us
    ppermute x6, waiting for transfers between devices, inner(): return [lax.ppermute(x, ('groups', 'cand'), inner_pairs) for x in parts]  17.1 us
    pallas_call x4, Pallas kernels, project(): pl.pallas_call(functools.partial(project_body, chunks=len(chunks)), in_sp...  15.6 us
    ppermute x22, starting transfers between devices, swap(): return lax.ppermute(x, 'tensor', [(t, t ^ bit) for t in range(4)])  15.2 us
    unnamed x43, local copies, waits for them, and re-layouts  13.5 us
    ppermute x9, starting transfers between devices, outer(): lax.ppermute(x, 'cand', [(0, 1), (1, 0), (2, 3), (3, 2)])  10.7 us
    pallas_call x4, Pallas kernels, output_blocks(): pl.pallas_call(output_body, in_specs=[pl.BlockSpec(memory_space=pltpu.SME...  8.33 us
  transfers between devices with their start and end apart: 37, of which 12 were waited for; matrix products, arithmetic and copies ran while one was open for 4% of the time, Pallas kernels for 20%

profile of v5, /device:TPU:0, one launch (start us, length us, event | category | flops | bytes accessed | tf_op | source)
XLA Modules:
  0.0 157.6 jit_solution(16177726251953860446)
XLA Ops:
  0.7 1.7 %fusion.1 = (f32[512]{0:T(512)S(1)}, bf16[512,1152]{1,0:T(8,128)(2,1)S(1)}) fusion(bf16[512,1152]{1,0:T(8,128)(2,1)} %param.9, f32[1152]{0:T(1024)S(1)} %convert_reduce_fusion.1), kind=kLoop, calls=%fused_computation.3 | loop fusion | flops 2948608 | bytes 2365952 | tf_op jit(solution)/shard_map/reduce_sum | solution.py:232
  2.5 3.0 %collective-permute-start.1 = (f32[512]{0:T(512)S(1)}, f32[512]{0:T(512)S(1)}, u32[]{:S(2)}, u32[]{:S(2)}) collective-permute-start(f32[512]{0:T(512)S(1)} %get-tuple-element.21), channel_id=1, source_target_pairs={{0,2},{1,3},{2,0},{3,1},{4,6},{5,7},{6,4},{7,5},{8,10},{9,11},{10,... | collective-permute-start | bytes 6152 | tf_op jit(solution)/shard_map/ppermute | solution.py:194
  5.7 1.9 %collective-permute-start.4 = (bf16[128,1152]{1,0:T(8,128)(2,1)S(1)}, bf16[128,1152]{1,0:T(8,128)(2,1)S(1)}, u32[]{:S(2)}, u32[]{:S(2)}) collective-permute-start(bf16[128,1152]{1,0:T(8,128)(2,1)S(1)} %get-tuple-element.23.refs_0_), channel_id=1, source_target_pairs={{0,2},{1,3},{2,0},{3,1},{4,6},{5,7},{6,4},{7,5},{8,10},{9,11},{10,... | collective-permute-start | bytes 884744 | tf_op jit(solution)/shard_map/ppermute | solution.py:194
  10.8 4.8 %collective-permute-done.4.refs_2_ = bf16[128,1152]{1,0:T(8,128)(2,1)S(1)} collective-permute-done((bf16[128,1152]{1,0:T(8,128)(2,1)S(1)}, bf16[128,1152]{1,0:T(8,128)(2,1)S(1)}, u32[]{:S(2)}, u32[]{:S(2)}) %collective-permute-start.4) | collective-permute-done | bytes 294944 | tf_op jit(solution)/shard_map/ppermute | solution.py:194
  16.6 2.0 %collective-permute-start.10 = (bf16[256,1152]{1,0:T(8,128)(2,1)S(1)}, bf16[256,1152]{1,0:T(8,128)(2,1)S(1)}, u32[]{:S(2)}, u32[]{:S(2)}) collective-permute-start(bf16[256,1152]{1,0:T(8,128)(2,1)S(1)} %slice.87.refs_8_.refs_0_), channel_id=1, source_target_pairs={{0,2},{1,3},{2,0},{3,1},{4,6},{5,7},{6,4},{7,5},{8,10},{9,11},{10,... | collective-permute-start | bytes 1769480 | tf_op jit(solution)/shard_map/ppermute | solution.py:194
  18.5 3.5 %collective-permute-done.7.refs_2_.refs_6_ = bf16[128,1152]{1,0:T(8,128)(2,1)} collective-permute-done((bf16[128,1152]{1,0:T(8,128)(2,1)S(1)}, bf16[128,1152]{1,0:T(8,128)(2,1)}, u32[]{:S(2)}, u32[]{:S(2)}) %collective-permute-start.7) | collective-permute-done | bytes 294944 | tf_op jit(solution)/shard_map/ppermute | solution.py:194
  22.0 2.3 %copy-done.1 = bf16[4608,512]{1,0:T(8,128)(2,1)S(1)} copy-done((bf16[4608,512]{1,0:T(8,128)(2,1)S(1)}, bf16[4608,512]{1,0:T(8,128)(2,1)}, u32[]{:S(2)}) %copy-start.1) | copy-done | bytes 4718616
  24.4 2.3 %copy-done.2 = bf16[4608,512]{1,0:T(8,128)(2,1)S(1)} copy-done((bf16[4608,512]{1,0:T(8,128)(2,1)S(1)}, bf16[4608,512]{1,0:T(8,128)(2,1)}, u32[]{:S(2)}) %copy-start.2) | copy-done | bytes 4718616
  26.7 2.7 %project.4 = bf16[2,128,512]{2,1,0:T(8,128)(2,1)S(1)} custom-call(s32[4]{0:T(128)S(1)} %pad_add_fusion.2.rank_ref, f32[128,1]{1,0:T(8,128)S(1)} %copy.12.inverse_ref, bf16[128,1152]{1,0:T(8,128)(2,1)S(1)} %get-tuple-element.23.refs_0_, bf16[128,1152]{1,0:T(8,128)(2,1)S(1)} %collective-permute-done.3.refs_1_, ...), custom_call_target="tpu_custom_call" | custom-call | flops 10000000000 | bytes 1000000 | tf_op jit(solution)/shard_map/project/pallas_call | solution.py:63
  29.4 2.1 %collective-permute-start.12 = (bf16[2,128,512]{2,1,0:T(8,128)(2,1)S(1)}, bf16[2,128,512]{2,1,0:T(8,128)(2,1)}, u32[]{:S(2)}, u32[]{:S(2)}) collective-permute-start(bf16[2,128,512]{2,1,0:T(8,128)(2,1)S(1)} %project.4), channel_id=1, source_target_pairs={{0,4},{4,0},{8,12},{12,8},{1,5},{5,1},{9,13},{13,9},{2,6},{6,2},{1... | collective-permute-start | bytes 786440 | tf_op jit(solution)/shard_map/ppermute | solution.py:244
  33.9 2.8 %project.5 = bf16[2,128,512]{2,1,0:T(8,128)(2,1)S(1)} custom-call(s32[4]{0:T(128)S(1)} %pad_add_fusion.2.rank_ref, f32[128,1]{1,0:T(8,128)S(1)} %copy.13.inverse_ref, bf16[128,1152]{1,0:T(8,128)(2,1)S(1)} %get-tuple-element.25.refs_0_.refs_4_, bf16[128,1152]{1,0:T(8,128)(2,1)S(1)} %collective-permute-done.6.refs_1_.refs_5_, ...), custom_call_target="tpu_custom_call" | custom-call | flops 10000000000 | bytes 1000000 | tf_op jit(solution)/shard_map/project/pallas_call | solution.py:63
  36.8 3.4 %project.7 = bf16[2,256,512]{2,1,0:T(8,128)(2,1)S(1)} custom-call(s32[4]{0:T(128)S(1)} %pad_add_fusion.2.rank_ref, f32[256,1]{1,0:T(8,128)S(1)} %copy.15.inverse_ref, bf16[256,1152]{1,0:T(8,128)(2,1)S(1)} %slice.87.refs_8_.refs_0_, bf16[256,1152]{1,0:T(8,128)(2,1)S(1)} %collective-permute-done.9.refs_9_.refs_1_, ...), custom_call_target="tpu_custom_call" | custom-call | flops 10000000000 | bytes 1000000 | tf_op jit(solution)/shard_map/project/pallas_call | solution.py:63
  40.2 1.8 %collective-permute-start.14 = (bf16[2,256,512]{2,1,0:T(8,128)(2,1)S(1)}, bf16[2,256,512]{2,1,0:T(8,128)(2,1)}, u32[]{:S(2)}, u32[]{:S(2)}) collective-permute-start(bf16[2,256,512]{2,1,0:T(8,128)(2,1)S(1)} %project.7), channel_id=1, source_target_pairs={{0,4},{4,0},{8,12},{12,8},{1,5},{5,1},{9,13},{13,9},{2,6},{6,2},{1... | collective-permute-start | bytes 1572872 | tf_op jit(solution)/shard_map/ppermute | solution.py:244
  43.8 1.7 %collective-permute-start.13 = (bf16[2,128,512]{2,1,0:T(8,128)(2,1)S(1)}, bf16[2,128,512]{2,1,0:T(8,128)(2,1)S(1)}, u32[]{:S(2)}, u32[]{:S(2)}) collective-permute-start(bf16[2,128,512]{2,1,0:T(8,128)(2,1)S(1)} %project.5), channel_id=1, source_target_pairs={{0,4},{4,0},{8,12},{12,8},{1,5},{5,1},{9,13},{13,9},{2,6},{6,2},{1... | collective-permute-start | bytes 786440 | tf_op jit(solution)/shard_map/ppermute | solution.py:244
  47.5 9.4 %collective-permute-done.19 = bf16[2,256,512]{2,1,0:T(8,128)(2,1)} collective-permute-done((bf16[2,256,512]{2,1,0:T(8,128)(2,1)S(1)}, bf16[2,256,512]{2,1,0:T(8,128)(2,1)}, u32[]{:S(2)}, u32[]{:S(2)}) %collective-permute-start.19) | collective-permute-done | bytes 524320 | tf_op jit(solution)/shard_map/ppermute | solution.py:249
  59.6 3.7 %copy-done = bf16[4608,1024]{1,0:T(8,128)(2,1)S(1)} copy-done((bf16[4608,1024]{1,0:T(8,128)(2,1)S(1)}, bf16[4608,1024]{1,0:T(8,128)(2,1)}, u32[]{:S(2)}) %copy-start) | copy-done | bytes 9437208
  68.3 6.7 %project.6.q_ref = bf16[1,512,1024]{2,1,0:T(8,128)(2,1)S(1)} custom-call(s32[4]{0:T(128)S(1)} %pad_add_fusion.2.rank_ref, f32[512,1]{1,0:T(8,128)S(1)} %copy.14.inverse_ref, bf16[128,1152]{1,0:T(8,128)(2,1)S(1)} %get-tuple-element.23.refs_0_, bf16[128,1152]{1,0:T(8,128)(2,1)S(1)} %copy-done.8, bf16[128,1152]{1,0:T(8,128)(2,1)S(1)} %collective-permute-done.4.refs_2_, ...), custom_call_target="tpu_custom_call" | custom-call | flops 10000000000 | bytes 1000000 | tf_op jit(solution)/shard_map/project/pallas_call | solution.py:63
  79.3 5.2 %collective-permute-done.21 = bf16[2,128,512]{2,1,0:T(8,128)(2,1)S(1)} collective-permute-done((bf16[2,128,512]{2,1,0:T(8,128)(2,1)}, bf16[2,128,512]{2,1,0:T(8,128)(2,1)S(1)}, u32[]{:S(2)}, u32[]{:S(2)}) %collective-permute-start.21) | collective-permute-done | bytes 262176 | tf_op jit(solution)/shard_map/ppermute | solution.py:249
  85.0 2.4 %collective-permute-done.23 = bf16[2,128,512]{2,1,0:T(8,128)(2,1)S(1)} collective-permute-done((bf16[2,128,512]{2,1,0:T(8,128)(2,1)S(1)}, bf16[2,128,512]{2,1,0:T(8,128)(2,1)S(1)}, u32[]{:S(2)}, u32[]{:S(2)}) %collective-permute-start.23) | collective-permute-done | bytes 262176 | tf_op jit(solution)/shard_map/ppermute | solution.py:249
  87.9 1.6 %collective-permute-start.26 = (bf16[2,256,512]{2,1,0:T(8,128)(2,1)S(1)}, bf16[2,256,512]{2,1,0:T(8,128)(2,1)S(1)}, u32[]{:S(2)}, u32[]{:S(2)}) collective-permute-start(bf16[2,256,512]{2,1,0:T(8,128)(2,1)S(1)} %collective-permute-done.25), channel_id=1, source_target_pairs={{0,4},{4,0},{8,12},{12,8},{1,5},{5,1},{9,13},{13,9},{2,6},{6,2},{1... | collective-permute-start | bytes 1572872 | tf_op jit(solution)/shard_map/ppermute | solution.py:244
  89.5 1.6 maximum_select_fusion.refs_4_.refs_5_
  91.1 11.8 %attention.2 = (f32[512,1024]{1,0:T(8,128)S(1)}, f32[512,512]{1,0:T(8,128)S(1)}) custom-call(f32[4,1536]{1,0:T(4,128)S(1)} %slice.88.bias_ref, bf16[1,512,1024]{2,1,0:T(8,128)(2,1)S(1)} %project.6.q_ref, bf16[2,512,512]{2,1,0:T(8,128)(2,1)S(1)} %pad_maximum_fusion.1.refs_0_.refs_1_, bf16[2,512,512]{2,1,0:T(8,128)(2,1)S(1)} %pad_maximum_fusion.1.refs_0_.refs_1_, ...), custom_call_target="tpu_custom_call" | custom-call | flops 10000000000 | bytes 1000000 | tf_op jit(solution)/shard_map/attention/pallas_call | solution.py:157
  102.9 4.3 %collective-permute-done.26 = bf16[2,256,512]{2,1,0:T(8,128)(2,1)S(1)} collective-permute-done((bf16[2,256,512]{2,1,0:T(8,128)(2,1)S(1)}, bf16[2,256,512]{2,1,0:T(8,128)(2,1)S(1)}, u32[]{:S(2)}, u32[]{:S(2)}) %collective-permute-start.26) | collective-permute-done | bytes 524320 | tf_op jit(solution)/shard_map/ppermute | solution.py:244
  107.5 7.6 %attention.3 = bf16[512,1024]{1,0:T(8,128)(2,1)S(1)} custom-call(f32[4,512]{1,0:T(4,128)S(1)} %slice.84.bias_ref, bf16[1,512,1024]{2,1,0:T(8,128)(2,1)S(1)} %project.6.q_ref, bf16[2,512,512]{2,1,0:T(8,128)(2,1)S(1)} %maximum_select_fusion.1.refs_0_.refs_1_, bf16[2,512,512]{2,1,0:T(8,128)(2,1)S(1)} %maximum_select_fusion.1.refs_0_.refs_1_, ...), custom_call_target="tpu_custom_call" | custom-call | flops 10000000000 | bytes 1000000 | tf_op jit(solution)/shard_map/attention/pallas_call | solution.py:157
  115.2 2.1 %output.5 = bf16[2,256,1152]{2,1,0:T(8,128)(2,1)S(1)} custom-call(s32[2]{0:T(128)S(1)} %pad_add_fusion.3.block_ref, bf16[256,1024]{1,0:T(8,128)(2,1)S(1)} %get-tuple-element.41.x_ref, bf16[1024,4608]{1,0:T(8,128)(2,1)S(1)} %bitcast.41), custom_call_target="tpu_custom_call" | custom-call | flops 10000000000 | bytes 1000000 | tf_op jit(solution)/shard_map/output/pallas_call | solution.py:178
  117.5 2.1 %output.4 = bf16[2,256,1152]{2,1,0:T(8,128)(2,1)S(1)} custom-call(s32[2]{0:T(128)S(1)} %pad_add_fusion.block_ref, bf16[256,1024]{1,0:T(8,128)(2,1)S(1)} %get-tuple-element.41.x_ref, bf16[1024,4608]{1,0:T(8,128)(2,1)S(1)} %bitcast.41), custom_call_target="tpu_custom_call" | custom-call | flops 10000000000 | bytes 1000000 | tf_op jit(solution)/shard_map/output/pallas_call | solution.py:178
  120.4 2.1 %output.7 = bf16[2,256,1152]{2,1,0:T(8,128)(2,1)S(1)} custom-call(s32[2]{0:T(128)S(1)} %pad_add_fusion.3.block_ref, bf16[256,1024]{1,0:T(8,128)(2,1)S(1)} %get-tuple-element.36.x_ref, bf16[1024,4608]{1,0:T(8,128)(2,1)S(1)} %bitcast.41), custom_call_target="tpu_custom_call" | custom-call | flops 10000000000 | bytes 1000000 | tf_op jit(solution)/shard_map/output/pallas_call | solution.py:178
  124.1 2.1 %output.6 = bf16[2,256,1152]{2,1,0:T(8,128)(2,1)S(1)} custom-call(s32[2]{0:T(128)S(1)} %pad_add_fusion.block_ref, bf16[256,1024]{1,0:T(8,128)(2,1)S(1)} %get-tuple-element.36.x_ref, bf16[1024,4608]{1,0:T(8,128)(2,1)S(1)} %bitcast.41), custom_call_target="tpu_custom_call" | custom-call | flops 10000000000 | bytes 1000000 | tf_op jit(solution)/shard_map/output/pallas_call | solution.py:178
  127.1 11.8 %collective-permute-done.28 = bf16[256,1152]{1,0:T(8,128)(2,1)S(1)} collective-permute-done((bf16[256,1152]{1,0:T(8,128)(2,1)S(1)}, bf16[256,1152]{1,0:T(8,128)(2,1)S(1)}, u32[]{:S(2)}, u32[]{:S(2)}) %collective-permute-start.28) | collective-permute-done | bytes 589856 | tf_op jit(solution)/shard_map/ppermute | solution.py:194
  139.2 1.5 collective-permute-start.30
  141.4 9.5 %collective-permute-done.33 = bf16[256,1152]{1,0:T(8,128)(2,1)S(1)} collective-permute-done((bf16[256,1152]{1,0:T(8,128)(2,1)S(1)}, bf16[256,1152]{1,0:T(8,128)(2,1)S(1)}, u32[]{:S(2)}, u32[]{:S(2)}) %collective-permute-start.33) | collective-permute-done | bytes 589856 | tf_op jit(solution)/shard_map/ppermute | solution.py:194
  151.3 1.5 collective-permute-start.35
  (137 shorter events, 33.9 us)
Async XLA Ops:
  2.5 7.6 %collective-permute-start.1 = (f32[512]{0:T(512)S(1)}, f32[512]{0:T(512)S(1)}, u32[]{:S(2)}, u32[]{:S(2)}) collective-permute-start(f32[512]{0:T(512)S(1)} %get-tuple-element.21), channel_id=1, source_target_pairs={{0,2},{1,3},{2,0},{3,1},{4,6},{5,7},{6,4},{7,5},{8,10},{9,11},{10,... | collective-permute-start | bytes 6152 | tf_op jit(solution)/shard_map/ppermute | solution.py:194
  5.5 4.6 %collective-permute-start.2 = (f32[512]{0:T(512)S(1)}, f32[512]{0:T(512)S(1)}, u32[]{:S(2)}, u32[]{:S(2)}) collective-permute-start(f32[512]{0:T(512)S(1)} %get-tuple-element.21), channel_id=1, source_target_pairs={{0,3},{1,2},{2,1},{3,0},{4,7},{5,6},{6,5},{7,4},{8,11},{9,10},{10,... | collective-permute-start | bytes 6152 | tf_op jit(solution)/shard_map/ppermute | solution.py:194
  5.5 4.6 %collective-permute-start = (f32[512]{0:T(512)S(1)}, f32[512]{0:T(512)S(1)}, u32[]{:S(2)}, u32[]{:S(2)}) collective-permute-start(f32[512]{0:T(512)S(1)} %get-tuple-element.21), channel_id=1, source_target_pairs={{0,1},{1,0},{2,3},{3,2},{4,5},{5,4},{6,7},{7,6},{8,9},{9,8},{10,11... | collective-permute-start | bytes 6152 | tf_op jit(solution)/shard_map/ppermute | solution.py:194
  5.7 9.9 %collective-permute-start.4 = (bf16[128,1152]{1,0:T(8,128)(2,1)S(1)}, bf16[128,1152]{1,0:T(8,128)(2,1)S(1)}, u32[]{:S(2)}, u32[]{:S(2)}) collective-permute-start(bf16[128,1152]{1,0:T(8,128)(2,1)S(1)} %get-tuple-element.23.refs_0_), channel_id=1, source_target_pairs={{0,2},{1,3},{2,0},{3,1},{4,6},{5,7},{6,4},{7,5},{8,10},{9,11},{10,... | collective-permute-start | bytes 884744 | tf_op jit(solution)/shard_map/ppermute | solution.py:194
  7.7 8.9 %collective-permute-start.3 = (bf16[128,1152]{1,0:T(8,128)(2,1)S(1)}, bf16[128,1152]{1,0:T(8,128)(2,1)S(1)}, u32[]{:S(2)}, u32[]{:S(2)}) collective-permute-start(bf16[128,1152]{1,0:T(8,128)(2,1)S(1)} %get-tuple-element.23.refs_0_), channel_id=1, source_target_pairs={{0,1},{1,0},{2,3},{3,2},{4,5},{5,4},{6,7},{7,6},{8,9},{9,8},{10,11... | collective-permute-start | bytes 884744 | tf_op jit(solution)/shard_map/ppermute | solution.py:194
  10.1 21.4 %collective-permute-start.6 = (bf16[128,1152]{1,0:T(8,128)(2,1)S(1)}, bf16[128,1152]{1,0:T(8,128)(2,1)S(1)}, u32[]{:S(2)}, u32[]{:S(2)}) collective-permute-start(bf16[128,1152]{1,0:T(8,128)(2,1)S(1)} %get-tuple-element.25.refs_0_.refs_4_), channel_id=1, source_target_pairs={{0,1},{1,0},{2,3},{3,2},{4,5},{5,4},{6,7},{7,6},{8,9},{9,8},{10,11... | collective-permute-start | bytes 884744 | tf_op jit(solution)/shard_map/ppermute | solution.py:194
  10.7 11.3 %collective-permute-start.7 = (bf16[128,1152]{1,0:T(8,128)(2,1)S(1)}, bf16[128,1152]{1,0:T(8,128)(2,1)}, u32[]{:S(2)}, u32[]{:S(2)}) collective-permute-start(bf16[128,1152]{1,0:T(8,128)(2,1)S(1)} %get-tuple-element.25.refs_0_.refs_4_), channel_id=1, source_target_pairs={{0,2},{1,3},{2,0},{3,1},{4,6},{5,7},{6,4},{7,5},{8,10},{9,11},{10,... | collective-permute-start | bytes 884744 | tf_op jit(solution)/shard_map/ppermute | solution.py:194
  15.6 6.4 %collective-permute-start.5 = (bf16[128,1152]{1,0:T(8,128)(2,1)S(1)}, bf16[128,1152]{1,0:T(8,128)(2,1)}, u32[]{:S(2)}, u32[]{:S(2)}) collective-permute-start(bf16[128,1152]{1,0:T(8,128)(2,1)S(1)} %collective-permute-done.4.refs_2_), channel_id=1, source_target_pairs={{0,1},{1,0},{2,3},{3,2},{4,5},{5,4},{6,7},{7,6},{8,9},{9,8},{10,11... | collective-permute-start | bytes 884744 | tf_op jit(solution)/shard_map/ppermute | solution.py:194
  16.0 20.8 %collective-permute-start.9 = (bf16[256,1152]{1,0:T(8,128)(2,1)S(1)}, bf16[256,1152]{1,0:T(8,128)(2,1)S(1)}, u32[]{:S(2)}, u32[]{:S(2)}) collective-permute-start(bf16[256,1152]{1,0:T(8,128)(2,1)S(1)} %slice.87.refs_8_.refs_0_), channel_id=1, source_target_pairs={{0,1},{1,0},{2,3},{3,2},{4,5},{5,4},{6,7},{7,6},{8,9},{9,8},{10,11... | collective-permute-start | bytes 1769480 | tf_op jit(solution)/shard_map/ppermute | solution.py:194
  16.6 17.3 %collective-permute-start.10 = (bf16[256,1152]{1,0:T(8,128)(2,1)S(1)}, bf16[256,1152]{1,0:T(8,128)(2,1)S(1)}, u32[]{:S(2)}, u32[]{:S(2)}) collective-permute-start(bf16[256,1152]{1,0:T(8,128)(2,1)S(1)} %slice.87.refs_8_.refs_0_), channel_id=1, source_target_pairs={{0,2},{1,3},{2,0},{3,1},{4,6},{5,7},{6,4},{7,5},{8,10},{9,11},{10,... | collective-permute-start | bytes 1769480 | tf_op jit(solution)/shard_map/ppermute | solution.py:194
  22.0 11.9 %collective-permute-start.8 = (bf16[128,1152]{1,0:T(8,128)(2,1)}, bf16[128,1152]{1,0:T(8,128)(2,1)S(1)}, u32[]{:S(2)}, u32[]{:S(2)}) collective-permute-start(bf16[128,1152]{1,0:T(8,128)(2,1)} %collective-permute-done.7.refs_2_.refs_6_), channel_id=1, source_target_pairs={{0,1},{1,0},{2,3},{3,2},{4,5},{5,4},{6,7},{7,6},{8,9},{9,8},{10,11... | collective-permute-start | bytes 884744 | tf_op jit(solution)/shard_map/ppermute | solution.py:194
  29.4 16.1 %collective-permute-start.12 = (bf16[2,128,512]{2,1,0:T(8,128)(2,1)S(1)}, bf16[2,128,512]{2,1,0:T(8,128)(2,1)}, u32[]{:S(2)}, u32[]{:S(2)}) collective-permute-start(bf16[2,128,512]{2,1,0:T(8,128)(2,1)S(1)} %project.4), channel_id=1, source_target_pairs={{0,4},{4,0},{8,12},{12,8},{1,5},{5,1},{9,13},{13,9},{2,6},{6,2},{1... | collective-permute-start | bytes 786440 | tf_op jit(solution)/shard_map/ppermute | solution.py:244
  31.5 15.5 %collective-permute-start.15 = (bf16[2,128,512]{2,1,0:T(8,128)(2,1)S(1)}, bf16[2,128,512]{2,1,0:T(8,128)(2,1)}, u32[]{:S(2)}, u32[]{:S(2)}) collective-permute-start(bf16[2,128,512]{2,1,0:T(8,128)(2,1)S(1)} %project.4), channel_id=1, source_target_pairs={{0,16},{16,0},{12,28},{28,12},{4,8},{8,4},{20,24},{24,20},{1,17},{... | collective-permute-start | bytes 786440 | tf_op jit(solution)/shard_map/ppermute | solution.py:249
  40.2 17.8 %collective-permute-start.14 = (bf16[2,256,512]{2,1,0:T(8,128)(2,1)S(1)}, bf16[2,256,512]{2,1,0:T(8,128)(2,1)}, u32[]{:S(2)}, u32[]{:S(2)}) collective-permute-start(bf16[2,256,512]{2,1,0:T(8,128)(2,1)S(1)} %project.7), channel_id=1, source_target_pairs={{0,4},{4,0},{8,12},{12,8},{1,5},{5,1},{9,13},{13,9},{2,6},{6,2},{1... | collective-permute-start | bytes 1572872 | tf_op jit(solution)/shard_map/ppermute | solution.py:244
  42.0 14.9 %collective-permute-start.19 = (bf16[2,256,512]{2,1,0:T(8,128)(2,1)S(1)}, bf16[2,256,512]{2,1,0:T(8,128)(2,1)}, u32[]{:S(2)}, u32[]{:S(2)}) collective-permute-start(bf16[2,256,512]{2,1,0:T(8,128)(2,1)S(1)} %project.7), channel_id=1, source_target_pairs={{0,16},{16,0},{12,28},{28,12},{4,8},{8,4},{20,24},{24,20},{1,17},{... | collective-permute-start | bytes 1572872 | tf_op jit(solution)/shard_map/ppermute | solution.py:249
  43.8 31.2 %collective-permute-start.13 = (bf16[2,128,512]{2,1,0:T(8,128)(2,1)S(1)}, bf16[2,128,512]{2,1,0:T(8,128)(2,1)S(1)}, u32[]{:S(2)}, u32[]{:S(2)}) collective-permute-start(bf16[2,128,512]{2,1,0:T(8,128)(2,1)S(1)} %project.5), channel_id=1, source_target_pairs={{0,4},{4,0},{8,12},{12,8},{1,5},{5,1},{9,13},{13,9},{2,6},{6,2},{1... | collective-permute-start | bytes 786440 | tf_op jit(solution)/shard_map/ppermute | solution.py:244
  45.5 30.1 %collective-permute-start.17 = (bf16[2,128,512]{2,1,0:T(8,128)(2,1)S(1)}, bf16[2,128,512]{2,1,0:T(8,128)(2,1)S(1)}, u32[]{:S(2)}, u32[]{:S(2)}) collective-permute-start(bf16[2,128,512]{2,1,0:T(8,128)(2,1)S(1)} %project.5), channel_id=1, source_target_pairs={{0,16},{16,0},{12,28},{28,12},{4,8},{8,4},{20,24},{24,20},{1,17},{... | collective-permute-start | bytes 786440 | tf_op jit(solution)/shard_map/ppermute | solution.py:249
  47.1 29.4 %collective-permute-start.16 = (bf16[2,128,512]{2,1,0:T(8,128)(2,1)}, bf16[2,128,512]{2,1,0:T(8,128)(2,1)S(1)}, u32[]{:S(2)}, u32[]{:S(2)}) collective-permute-start(bf16[2,128,512]{2,1,0:T(8,128)(2,1)} %collective-permute-done.15), channel_id=1, source_target_pairs={{0,4},{4,0},{8,12},{12,8},{1,5},{5,1},{9,13},{13,9},{2,6},{6,2},{1... | collective-permute-start | bytes 786440 | tf_op jit(solution)/shard_map/ppermute | solution.py:244
  56.9 32.6 %collective-permute-start.20 = (bf16[2,256,512]{2,1,0:T(8,128)(2,1)}, bf16[2,256,512]{2,1,0:T(8,128)(2,1)S(1)}, u32[]{:S(2)}, u32[]{:S(2)}) collective-permute-start(bf16[2,256,512]{2,1,0:T(8,128)(2,1)} %collective-permute-done.19), channel_id=1, source_target_pairs={{0,4},{4,0},{8,12},{12,8},{1,5},{5,1},{9,13},{13,9},{2,6},{6,2},{1... | collective-permute-start | bytes 1572872 | tf_op jit(solution)/shard_map/ppermute | solution.py:244
  58.1 29.8 %collective-permute-start.25 = (bf16[2,256,512]{2,1,0:T(8,128)(2,1)}, bf16[2,256,512]{2,1,0:T(8,128)(2,1)S(1)}, u32[]{:S(2)}, u32[]{:S(2)}) collective-permute-start(bf16[2,256,512]{2,1,0:T(8,128)(2,1)} %collective-permute-done.14), channel_id=1, source_target_pairs={{0,16},{16,0},{12,28},{28,12},{4,8},{8,4},{20,24},{24,20},{1,17},{... | collective-permute-start | bytes 1572872 | tf_op jit(solution)/shard_map/ppermute | solution.py:249
  75.0 9.5 %collective-permute-start.21 = (bf16[2,128,512]{2,1,0:T(8,128)(2,1)}, bf16[2,128,512]{2,1,0:T(8,128)(2,1)S(1)}, u32[]{:S(2)}, u32[]{:S(2)}) collective-permute-start(bf16[2,128,512]{2,1,0:T(8,128)(2,1)} %collective-permute-done.12), channel_id=1, source_target_pairs={{0,16},{16,0},{12,28},{28,12},{4,8},{8,4},{20,24},{24,20},{1,17},{... | collective-permute-start | bytes 786440 | tf_op jit(solution)/shard_map/ppermute | solution.py:249
  75.6 13.9 %collective-permute-start.18 = (bf16[2,128,512]{2,1,0:T(8,128)(2,1)S(1)}, bf16[2,128,512]{2,1,0:T(8,128)(2,1)S(1)}, u32[]{:S(2)}, u32[]{:S(2)}) collective-permute-start(bf16[2,128,512]{2,1,0:T(8,128)(2,1)S(1)} %collective-permute-done.17), channel_id=1, source_target_pairs={{0,4},{4,0},{8,12},{12,8},{1,5},{5,1},{9,13},{13,9},{2,6},{6,2},{1... | collective-permute-start | bytes 786440 | tf_op jit(solution)/shard_map/ppermute | solution.py:244
  76.5 11.0 %collective-permute-start.23 = (bf16[2,128,512]{2,1,0:T(8,128)(2,1)S(1)}, bf16[2,128,512]{2,1,0:T(8,128)(2,1)S(1)}, u32[]{:S(2)}, u32[]{:S(2)}) collective-permute-start(bf16[2,128,512]{2,1,0:T(8,128)(2,1)S(1)} %collective-permute-done.13), channel_id=1, source_target_pairs={{0,16},{16,0},{12,28},{28,12},{4,8},{8,4},{20,24},{24,20},{1,17},{... | collective-permute-start | bytes 786440 | tf_op jit(solution)/shard_map/ppermute | solution.py:249
  84.5 18.4 %collective-permute-start.22 = (bf16[2,128,512]{2,1,0:T(8,128)(2,1)S(1)}, bf16[2,128,512]{2,1,0:T(8,128)(2,1)S(1)}, u32[]{:S(2)}, u32[]{:S(2)}) collective-permute-start(bf16[2,128,512]{2,1,0:T(8,128)(2,1)S(1)} %collective-permute-done.21), channel_id=1, source_target_pairs={{0,4},{4,0},{8,12},{12,8},{1,5},{5,1},{9,13},{13,9},{2,6},{6,2},{1... | collective-permute-start | bytes 786440 | tf_op jit(solution)/shard_map/ppermute | solution.py:244
  87.5 15.4 %collective-permute-start.24 = (bf16[2,128,512]{2,1,0:T(8,128)(2,1)S(1)}, bf16[2,128,512]{2,1,0:T(8,128)(2,1)S(1)}, u32[]{:S(2)}, u32[]{:S(2)}) collective-permute-start(bf16[2,128,512]{2,1,0:T(8,128)(2,1)S(1)} %collective-permute-done.23), channel_id=1, source_target_pairs={{0,4},{4,0},{8,12},{12,8},{1,5},{5,1},{9,13},{13,9},{2,6},{6,2},{1... | collective-permute-start | bytes 786440 | tf_op jit(solution)/shard_map/ppermute | solution.py:244
  87.9 19.3 %collective-permute-start.26 = (bf16[2,256,512]{2,1,0:T(8,128)(2,1)S(1)}, bf16[2,256,512]{2,1,0:T(8,128)(2,1)S(1)}, u32[]{:S(2)}, u32[]{:S(2)}) collective-permute-start(bf16[2,256,512]{2,1,0:T(8,128)(2,1)S(1)} %collective-permute-done.25), channel_id=1, source_target_pairs={{0,4},{4,0},{8,12},{12,8},{1,5},{5,1},{9,13},{13,9},{2,6},{6,2},{1... | collective-permute-start | bytes 1572872 | tf_op jit(solution)/shard_map/ppermute | solution.py:244
  122.5 3.8 %collective-permute-start.32 = (bf16[2,256,1152]{2,1,0:T(8,128)(2,1)S(1)}, bf16[2,256,1152]{2,1,0:T(8,128)(2,1)S(1)}, u32[]{:S(2)}, u32[]{:S(2)}) collective-permute-start(bf16[2,256,1152]{2,1,0:T(8,128)(2,1)S(1)} %output.7), channel_id=1, source_target_pairs={{0,1},{1,0},{2,3},{3,2},{4,5},{5,4},{6,7},{7,6},{8,9},{9,8},{10,11... | collective-permute-start | bytes 3538952 | tf_op jit(solution)/shard_map/ppermute | solution.py:194
  122.7 16.2 %collective-permute-start.28 = (bf16[256,1152]{1,0:T(8,128)(2,1)S(1)}, bf16[256,1152]{1,0:T(8,128)(2,1)S(1)}, u32[]{:S(2)}, u32[]{:S(2)}) collective-permute-start(bf16[256,1152]{1,0:T(8,128)(2,1)S(1)} %fusion.3), channel_id=1, source_target_pairs={{0,2},{1,3},{2,0},{3,1},{4,6},{5,7},{6,4},{7,5},{8,10},{9,11},{10,... | collective-permute-start | bytes 1769480 | tf_op jit(solution)/shard_map/ppermute | solution.py:194
  126.4 24.5 %collective-permute-start.33 = (bf16[256,1152]{1,0:T(8,128)(2,1)S(1)}, bf16[256,1152]{1,0:T(8,128)(2,1)S(1)}, u32[]{:S(2)}, u32[]{:S(2)}) collective-permute-start(bf16[256,1152]{1,0:T(8,128)(2,1)S(1)} %fusion.4), channel_id=1, source_target_pairs={{0,2},{1,3},{2,0},{3,1},{4,6},{5,7},{6,4},{7,5},{8,10},{9,11},{10,... | collective-permute-start | bytes 1769480 | tf_op jit(solution)/shard_map/ppermute | solution.py:194
  139.2 13.6 %collective-permute-start.30 = (f32[256]{0:T(256)S(1)}, f32[256]{0:T(256)S(1)}, u32[]{:S(2)}, u32[]{:S(2)}) collective-permute-start(f32[256]{0:T(256)S(1)} %multiply_reduce_fusion.1), channel_id=1, source_target_pairs={{0,2},{1,3},{2,0},{3,1},{4,6},{5,7},{6,4},{7,5},{8,10},{9,11},{10,... | collective-permute-start | bytes 3080 | tf_op jit(solution)/shard_map/ppermute | solution.py:194
  140.8 12.7 %collective-permute-start.31 = (f32[256]{0:T(256)S(1)}, f32[256]{0:T(256)S(1)}, u32[]{:S(2)}, u32[]{:S(2)}) collective-permute-start(f32[256]{0:T(256)S(1)} %multiply_reduce_fusion.1), channel_id=1, source_target_pairs={{0,3},{1,2},{2,1},{3,0},{4,7},{5,6},{6,5},{7,4},{8,11},{9,10},{10,... | collective-permute-start | bytes 3080 | tf_op jit(solution)/shard_map/ppermute | solution.py:194
  140.8 12.7 %collective-permute-start.29 = (f32[256]{0:T(256)S(1)}, f32[256]{0:T(256)S(1)}, u32[]{:S(2)}, u32[]{:S(2)}) collective-permute-start(f32[256]{0:T(256)S(1)} %multiply_reduce_fusion.1), channel_id=1, source_target_pairs={{0,1},{1,0},{2,3},{3,2},{4,5},{5,4},{6,7},{7,6},{8,9},{9,8},{10,11... | collective-permute-start | bytes 3080 | tf_op jit(solution)/shard_map/ppermute | solution.py:194
  (26 other events, 107.1 us)

commit v6 on v5

--- a/solution.py
+++ b/solution.py
@@ -284,13 +284,19 @@
     other_core = jnp.stack([rank ^ 3, rank ^ 1])
     this_core = jnp.stack([rank ^ 2, rank])
     step = row_count // OUTPUT_CHUNKS
-    attended = attention(bias[:, seen:], queries, [last_slot], state=state)
+    cands = step // CTOK
     pending = []
     for c in range(OUTPUT_CHUNKS):
-        rows = attended[c * step : (c + 1) * step]
+        span = slice(c * step, (c + 1) * step)
         if c:
-            rows, far = lax.optimization_barrier((rows, pending[-1][2]))
+            last_slot, far = lax.optimization_barrier((last_slot, pending[-1][2]))
             pending[-1] = (*pending[-1][:2], far)
+        rows = attention(
+            bias[c * cands : (c + 1) * cands, seen:],
+            queries[:, span],
+            [last_slot],
+            state=[x[span] for x in state],
+        )
         away = swap(output_blocks(other_core, rows, w_out, features), 1)
         home = output_blocks(this_core, rows, w_out, features)
         far = (home[0].astype(jnp.float32) + away[0].astype(jnp.float32)).astype(jnp.bfloat16)

time: 158 us -> 154 us (0.975)
  local copies, waits for them, and re-layouts: 15.3 us -> 5.89 us
  waiting for transfers between devices: 54.9 us -> 62.1 us
  other arithmetic: 8.62 us -> 6.27 us
  starting transfers between devices: 34 us -> 35.7 us
    unnamed x43 -> x27, local copies, waits for them, and re-layouts: 13.5 us -> 4.82 us
    ppermute x6, waiting for transfers between devices: 17.1 us -> 22.9 us  [inner(): return [lax.ppermute(x, ('groups', 'cand'), inner_pairs) for x in parts]]
    ppermute x9, starting transfers between devices: 10.7 us -> 13.2 us  [outer(): lax.ppermute(x, 'cand', [(0, 1), (1, 0), (2, 3), (3, 2)])]
    pallas_call x4, Pallas kernels: 15.6 us -> 13.7 us  [project(): pl.pallas_call(functools.partial(project_body, chunks=len(chunks)), in_sp...]
    pallas_call x2 -> x3, Pallas kernels: 19.4 us -> 20.7 us  [attention(): pl.pallas_call(functools.partial(attention_body, slots=len(slots), begun=...]
  transfers between devices with their start and end apart: 37 -> 37, of which waited for: 12 -> 13; matrix products, arithmetic and copies ran while one was open for 4% -> 2% of each run, Pallas kernels for 20% -> 19%
where the time goes in v6:
time: 154 us
  waiting for transfers between devices  62.1 us (40%)
  Pallas kernels  42.8 us (28%)
  starting transfers between devices  35.7 us (23%)
  other arithmetic  6.27 us (4%)
  local copies, waits for them, and re-layouts  5.89 us (4%)
    ppermute x22, waiting for transfers between devices, swap(): return lax.ppermute(x, 'tensor', [(t, t ^ bit) for t in range(4)])  34.9 us
    ppermute x6, waiting for transfers between devices, inner(): return [lax.ppermute(x, ('groups', 'cand'), inner_pairs) for x in parts]  22.9 us
    pallas_call x3, Pallas kernels, attention(): pl.pallas_call(functools.partial(attention_body, slots=len(slots), begun=...  20.7 us
    ppermute x22, starting transfers between devices, swap(): return lax.ppermute(x, 'tensor', [(t, t ^ bit) for t in range(4)])  15.3 us
    pallas_call x4, Pallas kernels, project(): pl.pallas_call(functools.partial(project_body, chunks=len(chunks)), in_sp...  13.7 us
    ppermute x9, starting transfers between devices, outer(): lax.ppermute(x, 'cand', [(0, 1), (1, 0), (2, 3), (3, 2)])  13.2 us
    pallas_call x4, Pallas kernels, output_blocks(): pl.pallas_call(output_body, in_specs=[pl.BlockSpec(memory_space=pltpu.SME...  8.32 us
    ppermute x6, starting transfers between devices, inner(): return [lax.ppermute(x, ('groups', 'cand'), inner_pairs) for x in parts]  7.21 us
  transfers between devices with their start and end apart: 37, of which 13 were waited for; matrix products, arithmetic and copies ran while one was open for 2% of the time, Pallas kernels for 19%

profile of v6, /device:TPU:0, one launch (start us, length us, event | category | flops | bytes accessed | tf_op | source)
XLA Modules:
  0.0 154.1 jit_solution(4836611366501536014)
XLA Ops:
  2.5 3.0 %collective-permute-start.1 = (f32[512]{0:T(512)S(1)}, f32[512]{0:T(512)S(1)}, u32[]{:S(2)}, u32[]{:S(2)}) collective-permute-start(f32[512]{0:T(512)S(1)} %get-tuple-element.21), channel_id=1, source_target_pairs={{0,2},{1,3},{2,0},{3,1},{4,6},{5,7},{6,4},{7,5},{8,10},{9,11},{10,... | collective-permute-start | bytes 6152 | tf_op jit(solution)/shard_map/ppermute | solution.py:194
  5.7 1.9 %collective-permute-start.4 = (bf16[128,1152]{1,0:T(8,128)(2,1)S(1)}, bf16[128,1152]{1,0:T(8,128)(2,1)S(1)}, u32[]{:S(2)}, u32[]{:S(2)}) collective-permute-start(bf16[128,1152]{1,0:T(8,128)(2,1)S(1)} %get-tuple-element.23.refs_0_), channel_id=1, source_target_pairs={{0,2},{1,3},{2,0},{3,1},{4,6},{5,7},{6,4},{7,5},{8,10},{9,11},{10,... | collective-permute-start | bytes 884744 | tf_op jit(solution)/shard_map/ppermute | solution.py:194
  9.8 5.8 %collective-permute-done.4.refs_2_ = bf16[128,1152]{1,0:T(8,128)(2,1)S(1)} collective-permute-done((bf16[128,1152]{1,0:T(8,128)(2,1)S(1)}, bf16[128,1152]{1,0:T(8,128)(2,1)S(1)}, u32[]{:S(2)}, u32[]{:S(2)}) %collective-permute-start.4) | collective-permute-done | bytes 294944 | tf_op jit(solution)/shard_map/ppermute | solution.py:194
  16.7 1.9 %collective-permute-start.10 = (bf16[256,1152]{1,0:T(8,128)(2,1)S(1)}, bf16[256,1152]{1,0:T(8,128)(2,1)S(1)}, u32[]{:S(2)}, u32[]{:S(2)}) collective-permute-start(bf16[256,1152]{1,0:T(8,128)(2,1)S(1)} %slice.107.refs_8_.refs_0_), channel_id=1, source_target_pairs={{0,2},{1,3},{2,0},{3,1},{4,6},{5,7},{6,4},{7,5},{8,10},{9,11},{10,... | collective-permute-start | bytes 1769480 | tf_op jit(solution)/shard_map/ppermute | solution.py:194
  18.7 3.2 %collective-permute-done.7.refs_2_.refs_6_ = bf16[128,1152]{1,0:T(8,128)(2,1)S(1)} collective-permute-done((bf16[128,1152]{1,0:T(8,128)(2,1)S(1)}, bf16[128,1152]{1,0:T(8,128)(2,1)S(1)}, u32[]{:S(2)}, u32[]{:S(2)}) %collective-permute-start.7) | collective-permute-done | bytes 294944 | tf_op jit(solution)/shard_map/ppermute | solution.py:194
  21.9 2.3 %copy-done = bf16[4608,512]{1,0:T(8,128)(2,1)S(1)} copy-done((bf16[4608,512]{1,0:T(8,128)(2,1)S(1)}, bf16[4608,512]{1,0:T(8,128)(2,1)}, u32[]{:S(2)}) %copy-start) | copy-done | bytes 4718616
  24.2 2.3 %copy-done.1 = bf16[4608,512]{1,0:T(8,128)(2,1)S(1)} copy-done((bf16[4608,512]{1,0:T(8,128)(2,1)S(1)}, bf16[4608,512]{1,0:T(8,128)(2,1)}, u32[]{:S(2)}) %copy-start.1) | copy-done | bytes 4718616
  26.6 2.1 %project.4 = bf16[2,128,512]{2,1,0:T(8,128)(2,1)S(1)} custom-call(s32[4]{0:T(128)S(1)} %pad_add_fusion.2.rank_ref, f32[128,1]{1,0:T(8,128)S(1)} %copy.12.inverse_ref, bf16[128,1152]{1,0:T(8,128)(2,1)S(1)} %get-tuple-element.23.refs_0_, bf16[128,1152]{1,0:T(8,128)(2,1)S(1)} %collective-permute-done.3.refs_1_, ...), custom_call_target="tpu_custom_call" | custom-call | flops 10000000000 | bytes 1000000 | tf_op jit(solution)/shard_map/project/pallas_call | solution.py:63
  28.7 2.1 %collective-permute-start.12 = (bf16[2,128,512]{2,1,0:T(8,128)(2,1)S(1)}, bf16[2,128,512]{2,1,0:T(8,128)(2,1)S(1)}, u32[]{:S(2)}, u32[]{:S(2)}) collective-permute-start(bf16[2,128,512]{2,1,0:T(8,128)(2,1)S(1)} %project.4), channel_id=1, source_target_pairs={{0,4},{4,0},{8,12},{12,8},{1,5},{5,1},{9,13},{13,9},{2,6},{6,2},{1... | collective-permute-start | bytes 786440 | tf_op jit(solution)/shard_map/ppermute | solution.py:244
  33.9 2.1 %project.5 = bf16[2,128,512]{2,1,0:T(8,128)(2,1)S(1)} custom-call(s32[4]{0:T(128)S(1)} %pad_add_fusion.2.rank_ref, f32[128,1]{1,0:T(8,128)S(1)} %copy.13.inverse_ref, bf16[128,1152]{1,0:T(8,128)(2,1)S(1)} %get-tuple-element.25.refs_0_.refs_4_, bf16[128,1152]{1,0:T(8,128)(2,1)S(1)} %collective-permute-done.6.refs_1_.refs_5_, ...), custom_call_target="tpu_custom_call" | custom-call | flops 10000000000 | bytes 1000000 | tf_op jit(solution)/shard_map/project/pallas_call | solution.py:63
  36.0 1.8 %collective-permute-start.13 = (bf16[2,128,512]{2,1,0:T(8,128)(2,1)S(1)}, bf16[2,128,512]{2,1,0:T(8,128)(2,1)S(1)}, u32[]{:S(2)}, u32[]{:S(2)}) collective-permute-start(bf16[2,128,512]{2,1,0:T(8,128)(2,1)S(1)} %project.5), channel_id=1, source_target_pairs={{0,4},{4,0},{8,12},{12,8},{1,5},{5,1},{9,13},{13,9},{2,6},{6,2},{1... | collective-permute-start | bytes 786440 | tf_op jit(solution)/shard_map/ppermute | solution.py:244
  37.8 3.4 %project.7 = bf16[2,256,512]{2,1,0:T(8,128)(2,1)S(1)} custom-call(s32[4]{0:T(128)S(1)} %pad_add_fusion.2.rank_ref, f32[256,1]{1,0:T(8,128)S(1)} %copy.15.inverse_ref, bf16[256,1152]{1,0:T(8,128)(2,1)S(1)} %slice.107.refs_8_.refs_0_, bf16[256,1152]{1,0:T(8,128)(2,1)S(1)} %collective-permute-done.9.refs_9_.refs_1_, ...), custom_call_target="tpu_custom_call" | custom-call | flops 10000000000 | bytes 1000000 | tf_op jit(solution)/shard_map/project/pallas_call | solution.py:63
  43.3 6.1 %project.6.q_ref = bf16[1,512,1024]{2,1,0:T(8,128)(2,1)S(1)} custom-call(s32[4]{0:T(128)S(1)} %pad_add_fusion.2.rank_ref, f32[512,1]{1,0:T(8,128)S(1)} %copy.14.inverse_ref, bf16[128,1152]{1,0:T(8,128)(2,1)S(1)} %get-tuple-element.23.refs_0_, bf16[128,1152]{1,0:T(8,128)(2,1)S(1)} %collective-permute-done.3.refs_1_, ...), custom_call_target="tpu_custom_call" | custom-call | flops 10000000000 | bytes 1000000 | tf_op jit(solution)/shard_map/project/pallas_call | solution.py:63
  49.9 1.7 %collective-permute-start.16 = (bf16[2,128,512]{2,1,0:T(8,128)(2,1)S(1)}, bf16[2,128,512]{2,1,0:T(8,128)(2,1)S(1)}, u32[]{:S(2)}, u32[]{:S(2)}) collective-permute-start(bf16[2,128,512]{2,1,0:T(8,128)(2,1)S(1)} %collective-permute-done.15), channel_id=1, source_target_pairs={{0,4},{4,0},{8,12},{12,8},{1,5},{5,1},{9,13},{13,9},{2,6},{6,2},{1... | collective-permute-start | bytes 786440 | tf_op jit(solution)/shard_map/ppermute | solution.py:244
  51.6 4.8 %collective-permute-done.19 = bf16[2,256,512]{2,1,0:T(8,128)(2,1)S(1)} collective-permute-done((bf16[2,256,512]{2,1,0:T(8,128)(2,1)S(1)}, bf16[2,256,512]{2,1,0:T(8,128)(2,1)S(1)}, u32[]{:S(2)}, u32[]{:S(2)}) %collective-permute-start.19) | collective-permute-done | bytes 524320 | tf_op jit(solution)/shard_map/ppermute | solution.py:249
  56.4 1.7 %collective-permute-start.20 = (bf16[2,256,512]{2,1,0:T(8,128)(2,1)S(1)}, bf16[2,256,512]{2,1,0:T(8,128)(2,1)S(1)}, u32[]{:S(2)}, u32[]{:S(2)}) collective-permute-start(bf16[2,256,512]{2,1,0:T(8,128)(2,1)S(1)} %collective-permute-done.19), channel_id=1, source_target_pairs={{0,4},{4,0},{8,12},{12,8},{1,5},{5,1},{9,13},{13,9},{2,6},{6,2},{1... | collective-permute-start | bytes 1572872 | tf_op jit(solution)/shard_map/ppermute | solution.py:244
  60.3 1.7 %collective-permute-done.17 = bf16[2,128,512]{2,1,0:T(8,128)(2,1)S(1)} collective-permute-done((bf16[2,128,512]{2,1,0:T(8,128)(2,1)S(1)}, bf16[2,128,512]{2,1,0:T(8,128)(2,1)S(1)}, u32[]{:S(2)}, u32[]{:S(2)}) %collective-permute-start.17) | collective-permute-done | bytes 262176 | tf_op jit(solution)/shard_map/ppermute | solution.py:249
  62.0 1.7 %collective-permute-start.18 = (bf16[2,128,512]{2,1,0:T(8,128)(2,1)S(1)}, bf16[2,128,512]{2,1,0:T(8,128)(2,1)S(1)}, u32[]{:S(2)}, u32[]{:S(2)}) collective-permute-start(bf16[2,128,512]{2,1,0:T(8,128)(2,1)S(1)} %collective-permute-done.17), channel_id=1, source_target_pairs={{0,4},{4,0},{8,12},{12,8},{1,5},{5,1},{9,13},{13,9},{2,6},{6,2},{1... | collective-permute-start | bytes 786440 | tf_op jit(solution)/shard_map/ppermute | solution.py:244
  65.4 13.5 %collective-permute-done.21 = bf16[2,128,512]{2,1,0:T(8,128)(2,1)S(1)} collective-permute-done((bf16[2,128,512]{2,1,0:T(8,128)(2,1)S(1)}, bf16[2,128,512]{2,1,0:T(8,128)(2,1)S(1)}, u32[]{:S(2)}, u32[]{:S(2)}) %collective-permute-start.21) | collective-permute-done | bytes 262176 | tf_op jit(solution)/shard_map/ppermute | solution.py:249
  78.9 1.7 %collective-permute-start.22 = (bf16[2,128,512]{2,1,0:T(8,128)(2,1)S(1)}, bf16[2,128,512]{2,1,0:T(8,128)(2,1)S(1)}, u32[]{:S(2)}, u32[]{:S(2)}) collective-permute-start(bf16[2,128,512]{2,1,0:T(8,128)(2,1)S(1)} %collective-permute-done.21), channel_id=1, source_target_pairs={{0,4},{4,0},{8,12},{12,8},{1,5},{5,1},{9,13},{13,9},{2,6},{6,2},{1... | collective-permute-start | bytes 786440 | tf_op jit(solution)/shard_map/ppermute | solution.py:244
  80.6 2.9 %collective-permute-done.23 = bf16[2,128,512]{2,1,0:T(8,128)(2,1)S(1)} collective-permute-done((bf16[2,128,512]{2,1,0:T(8,128)(2,1)S(1)}, bf16[2,128,512]{2,1,0:T(8,128)(2,1)S(1)}, u32[]{:S(2)}, u32[]{:S(2)}) %collective-permute-start.23) | collective-permute-done | bytes 262176 | tf_op jit(solution)/shard_map/ppermute | solution.py:249
  85.8 12.0 %attention.3 = (f32[512,1024]{1,0:T(8,128)S(1)}, f32[512,512]{1,0:T(8,128)S(1)}) custom-call(f32[4,1536]{1,0:T(4,128)S(1)} %slice.109.bias_ref, bf16[1,512,1024]{2,1,0:T(8,128)(2,1)S(1)} %project.6.q_ref, bf16[2,512,512]{2,1,0:T(8,128)(2,1)S(1)} %pad_maximum_fusion.1.refs_0_.refs_1_, bf16[2,512,512]{2,1,0:T(8,128)(2,1)S(1)} %pad_maximum_fusion.1.refs_0_.refs_1_, ...), custom_call_target="tpu_custom_call" | custom-call | flops 10000000000 | bytes 1000000 | tf_op jit(solution)/shard_map/attention/pallas_call | solution.py:157
  97.8 4.3 %collective-permute-done.26 = bf16[2,256,512]{2,1,0:T(8,128)(2,1)S(1)} collective-permute-done((bf16[2,256,512]{2,1,0:T(8,128)(2,1)S(1)}, bf16[2,256,512]{2,1,0:T(8,128)(2,1)S(1)}, u32[]{:S(2)}, u32[]{:S(2)}) %collective-permute-start.26) | collective-permute-done | bytes 524320 | tf_op jit(solution)/shard_map/ppermute | solution.py:244
  102.8 4.4 %attention.4.x_ref = bf16[256,1024]{1,0:T(8,128)(2,1)S(1)} custom-call(f32[2,512]{1,0:T(2,128)S(1)} %get-tuple-element.47.bias_ref, bf16[1,256,1024]{2,1,0:T(8,128)(2,1)S(1)} %get-tuple-element.45.q_ref, bf16[2,512,512]{2,1,0:T(8,128)(2,1)S(1)} %maximum_select_fusion.1.refs_0_.refs_1_, bf16[2,512,512]{2,1,0:T(8,128)(2,1)S(1)} %maximum_select_fusion.1.refs_0_.refs_1_, ...), custom_call_target="tpu_custom_call" | custom-call | flops 10000000000 | bytes 1000000 | tf_op jit(solution)/shard_map/attention/pallas_call | solution.py:157
  107.2 2.1 %output.5 = bf16[2,256,1152]{2,1,0:T(8,128)(2,1)S(1)} custom-call(s32[2]{0:T(128)S(1)} %pad_add_fusion.3.block_ref, bf16[256,1024]{1,0:T(8,128)(2,1)S(1)} %attention.4.x_ref, bf16[1024,4608]{1,0:T(8,128)(2,1)S(1)} %bitcast.43), custom_call_target="tpu_custom_call" | custom-call | flops 10000000000 | bytes 1000000 | tf_op jit(solution)/shard_map/output/pallas_call | solution.py:178
  109.4 2.1 %output.4 = bf16[2,256,1152]{2,1,0:T(8,128)(2,1)S(1)} custom-call(s32[2]{0:T(128)S(1)} %pad_add_fusion.block_ref, bf16[256,1024]{1,0:T(8,128)(2,1)S(1)} %attention.4.x_ref, bf16[1024,4608]{1,0:T(8,128)(2,1)S(1)} %bitcast.43), custom_call_target="tpu_custom_call" | custom-call | flops 10000000000 | bytes 1000000 | tf_op jit(solution)/shard_map/output/pallas_call | solution.py:178
  112.4 4.4 %attention.5.x_ref = bf16[256,1024]{1,0:T(8,128)(2,1)S(1)} custom-call(f32[2,512]{1,0:T(2,128)S(1)} %get-tuple-element.48.bias_ref, bf16[1,256,1024]{2,1,0:T(8,128)(2,1)S(1)} %get-tuple-element.46.q_ref, bf16[2,512,512]{2,1,0:T(8,128)(2,1)S(1)} %maximum_select_fusion.1.refs_0_.refs_1_, bf16[2,512,512]{2,1,0:T(8,128)(2,1)S(1)} %maximum_select_fusion.1.refs_0_.refs_1_, ...), custom_call_target="tpu_custom_call" | custom-call | flops 10000000000 | bytes 1000000 | tf_op jit(solution)/shard_map/attention/pallas_call | solution.py:157
  116.8 2.1 %output.7 = bf16[2,256,1152]{2,1,0:T(8,128)(2,1)S(1)} custom-call(s32[2]{0:T(128)S(1)} %pad_add_fusion.3.block_ref, bf16[256,1024]{1,0:T(8,128)(2,1)S(1)} %attention.5.x_ref, bf16[1024,4608]{1,0:T(8,128)(2,1)S(1)} %bitcast.43), custom_call_target="tpu_custom_call" | custom-call | flops 10000000000 | bytes 1000000 | tf_op jit(solution)/shard_map/output/pallas_call | solution.py:178
  120.7 2.1 %output.6 = bf16[2,256,1152]{2,1,0:T(8,128)(2,1)S(1)} custom-call(s32[2]{0:T(128)S(1)} %pad_add_fusion.block_ref, bf16[256,1024]{1,0:T(8,128)(2,1)S(1)} %attention.5.x_ref, bf16[1024,4608]{1,0:T(8,128)(2,1)S(1)} %bitcast.43), custom_call_target="tpu_custom_call" | custom-call | flops 10000000000 | bytes 1000000 | tf_op jit(solution)/shard_map/output/pallas_call | solution.py:178
  123.6 11.6 %collective-permute-done.28 = bf16[256,1152]{1,0:T(8,128)(2,1)S(1)} collective-permute-done((bf16[256,1152]{1,0:T(8,128)(2,1)S(1)}, bf16[256,1152]{1,0:T(8,128)(2,1)S(1)}, u32[]{:S(2)}, u32[]{:S(2)}) %collective-permute-start.28) | collective-permute-done | bytes 589856 | tf_op jit(solution)/shard_map/ppermute | solution.py:194
  135.6 1.7 %collective-permute-start.30 = (f32[256]{0:T(256)S(1)}, f32[256]{0:T(256)S(1)}, u32[]{:S(2)}, u32[]{:S(2)}) collective-permute-start(f32[256]{0:T(256)S(1)} %multiply_reduce_fusion.1), channel_id=1, source_target_pairs={{0,2},{1,3},{2,0},{3,1},{4,6},{5,7},{6,4},{7,5},{8,10},{9,11},{10,... | collective-permute-start | bytes 3080 | tf_op jit(solution)/shard_map/ppermute | solution.py:194
  137.8 9.5 %collective-permute-done.33 = bf16[256,1152]{1,0:T(8,128)(2,1)S(1)} collective-permute-done((bf16[256,1152]{1,0:T(8,128)(2,1)S(1)}, bf16[256,1152]{1,0:T(8,128)(2,1)S(1)}, u32[]{:S(2)}, u32[]{:S(2)}) %collective-permute-start.33) | collective-permute-done | bytes 589856 | tf_op jit(solution)/shard_map/ppermute | solution.py:194
  (125 shorter events, 29.5 us)
Async XLA Ops:
  2.5 6.7 %collective-permute-start.1 = (f32[512]{0:T(512)S(1)}, f32[512]{0:T(512)S(1)}, u32[]{:S(2)}, u32[]{:S(2)}) collective-permute-start(f32[512]{0:T(512)S(1)} %get-tuple-element.21), channel_id=1, source_target_pairs={{0,2},{1,3},{2,0},{3,1},{4,6},{5,7},{6,4},{7,5},{8,10},{9,11},{10,... | collective-permute-start | bytes 6152 | tf_op jit(solution)/shard_map/ppermute | solution.py:194
  5.5 3.6 %collective-permute-start = (f32[512]{0:T(512)S(1)}, f32[512]{0:T(512)S(1)}, u32[]{:S(2)}, u32[]{:S(2)}) collective-permute-start(f32[512]{0:T(512)S(1)} %get-tuple-element.21), channel_id=1, source_target_pairs={{0,1},{1,0},{2,3},{3,2},{4,5},{5,4},{6,7},{7,6},{8,9},{9,8},{10,11... | collective-permute-start | bytes 6152 | tf_op jit(solution)/shard_map/ppermute | solution.py:194
  5.7 9.9 %collective-permute-start.4 = (bf16[128,1152]{1,0:T(8,128)(2,1)S(1)}, bf16[128,1152]{1,0:T(8,128)(2,1)S(1)}, u32[]{:S(2)}, u32[]{:S(2)}) collective-permute-start(bf16[128,1152]{1,0:T(8,128)(2,1)S(1)} %get-tuple-element.23.refs_0_), channel_id=1, source_target_pairs={{0,2},{1,3},{2,0},{3,1},{4,6},{5,7},{6,4},{7,5},{8,10},{9,11},{10,... | collective-permute-start | bytes 884744 | tf_op jit(solution)/shard_map/ppermute | solution.py:194
  7.6 9.1 %collective-permute-start.3 = (bf16[128,1152]{1,0:T(8,128)(2,1)S(1)}, bf16[128,1152]{1,0:T(8,128)(2,1)S(1)}, u32[]{:S(2)}, u32[]{:S(2)}) collective-permute-start(bf16[128,1152]{1,0:T(8,128)(2,1)S(1)} %get-tuple-element.23.refs_0_), channel_id=1, source_target_pairs={{0,1},{1,0},{2,3},{3,2},{4,5},{5,4},{6,7},{7,6},{8,9},{9,8},{10,11... | collective-permute-start | bytes 884744 | tf_op jit(solution)/shard_map/ppermute | solution.py:194
  9.2 21.6 %collective-permute-start.6 = (bf16[128,1152]{1,0:T(8,128)(2,1)S(1)}, bf16[128,1152]{1,0:T(8,128)(2,1)S(1)}, u32[]{:S(2)}, u32[]{:S(2)}) collective-permute-start(bf16[128,1152]{1,0:T(8,128)(2,1)S(1)} %get-tuple-element.25.refs_0_.refs_4_), channel_id=1, source_target_pairs={{0,1},{1,0},{2,3},{3,2},{4,5},{5,4},{6,7},{7,6},{8,9},{9,8},{10,11... | collective-permute-start | bytes 884744 | tf_op jit(solution)/shard_map/ppermute | solution.py:194
  9.7 12.2 %collective-permute-start.7 = (bf16[128,1152]{1,0:T(8,128)(2,1)S(1)}, bf16[128,1152]{1,0:T(8,128)(2,1)S(1)}, u32[]{:S(2)}, u32[]{:S(2)}) collective-permute-start(bf16[128,1152]{1,0:T(8,128)(2,1)S(1)} %get-tuple-element.25.refs_0_.refs_4_), channel_id=1, source_target_pairs={{0,2},{1,3},{2,0},{3,1},{4,6},{5,7},{6,4},{7,5},{8,10},{9,11},{10,... | collective-permute-start | bytes 884744 | tf_op jit(solution)/shard_map/ppermute | solution.py:194
  15.6 6.3 %collective-permute-start.5 = (bf16[128,1152]{1,0:T(8,128)(2,1)S(1)}, bf16[128,1152]{1,0:T(8,128)(2,1)S(1)}, u32[]{:S(2)}, u32[]{:S(2)}) collective-permute-start(bf16[128,1152]{1,0:T(8,128)(2,1)S(1)} %collective-permute-done.4.refs_2_), channel_id=1, source_target_pairs={{0,1},{1,0},{2,3},{3,2},{4,5},{5,4},{6,7},{7,6},{8,9},{9,8},{10,11... | collective-permute-start | bytes 884744 | tf_op jit(solution)/shard_map/ppermute | solution.py:194
  16.1 21.7 %collective-permute-start.9 = (bf16[256,1152]{1,0:T(8,128)(2,1)S(1)}, bf16[256,1152]{1,0:T(8,128)(2,1)S(1)}, u32[]{:S(2)}, u32[]{:S(2)}) collective-permute-start(bf16[256,1152]{1,0:T(8,128)(2,1)S(1)} %slice.107.refs_8_.refs_0_), channel_id=1, source_target_pairs={{0,1},{1,0},{2,3},{3,2},{4,5},{5,4},{6,7},{7,6},{8,9},{9,8},{10,11... | collective-permute-start | bytes 1769480 | tf_op jit(solution)/shard_map/ppermute | solution.py:194
  16.7 17.2 %collective-permute-start.10 = (bf16[256,1152]{1,0:T(8,128)(2,1)S(1)}, bf16[256,1152]{1,0:T(8,128)(2,1)S(1)}, u32[]{:S(2)}, u32[]{:S(2)}) collective-permute-start(bf16[256,1152]{1,0:T(8,128)(2,1)S(1)} %slice.107.refs_8_.refs_0_), channel_id=1, source_target_pairs={{0,2},{1,3},{2,0},{3,1},{4,6},{5,7},{6,4},{7,5},{8,10},{9,11},{10,... | collective-permute-start | bytes 1769480 | tf_op jit(solution)/shard_map/ppermute | solution.py:194
  21.9 12.0 %collective-permute-start.8 = (bf16[128,1152]{1,0:T(8,128)(2,1)S(1)}, bf16[128,1152]{1,0:T(8,128)(2,1)S(1)}, u32[]{:S(2)}, u32[]{:S(2)}) collective-permute-start(bf16[128,1152]{1,0:T(8,128)(2,1)S(1)} %collective-permute-done.7.refs_2_.refs_6_), channel_id=1, source_target_pairs={{0,1},{1,0},{2,3},{3,2},{4,5},{5,4},{6,7},{7,6},{8,9},{9,8},{10,11... | collective-permute-start | bytes 884744 | tf_op jit(solution)/shard_map/ppermute | solution.py:194
  28.7 20.8 %collective-permute-start.12 = (bf16[2,128,512]{2,1,0:T(8,128)(2,1)S(1)}, bf16[2,128,512]{2,1,0:T(8,128)(2,1)S(1)}, u32[]{:S(2)}, u32[]{:S(2)}) collective-permute-start(bf16[2,128,512]{2,1,0:T(8,128)(2,1)S(1)} %project.4), channel_id=1, source_target_pairs={{0,4},{4,0},{8,12},{12,8},{1,5},{5,1},{9,13},{13,9},{2,6},{6,2},{1... | collective-permute-start | bytes 786440 | tf_op jit(solution)/shard_map/ppermute | solution.py:244
  30.8 19.1 %collective-permute-start.15 = (bf16[2,128,512]{2,1,0:T(8,128)(2,1)S(1)}, bf16[2,128,512]{2,1,0:T(8,128)(2,1)S(1)}, u32[]{:S(2)}, u32[]{:S(2)}) collective-permute-start(bf16[2,128,512]{2,1,0:T(8,128)(2,1)S(1)} %project.4), channel_id=1, source_target_pairs={{0,16},{16,0},{12,28},{28,12},{4,8},{8,4},{20,24},{24,20},{1,17},{... | collective-permute-start | bytes 786440 | tf_op jit(solution)/shard_map/ppermute | solution.py:249
  33.9 3.9 %collective-permute-start.11 = (bf16[256,1152]{1,0:T(8,128)(2,1)S(1)}, bf16[256,1152]{1,0:T(8,128)(2,1)S(1)}, u32[]{:S(2)}, u32[]{:S(2)}) collective-permute-start(bf16[256,1152]{1,0:T(8,128)(2,1)S(1)} %collective-permute-done.10.refs_10_.refs_2_), channel_id=1, source_target_pairs={{0,1},{1,0},{2,3},{3,2},{4,5},{5,4},{6,7},{7,6},{8,9},{9,8},{10,11... | collective-permute-start | bytes 1769480 | tf_op jit(solution)/shard_map/ppermute | solution.py:194
  36.0 23.7 %collective-permute-start.13 = (bf16[2,128,512]{2,1,0:T(8,128)(2,1)S(1)}, bf16[2,128,512]{2,1,0:T(8,128)(2,1)S(1)}, u32[]{:S(2)}, u32[]{:S(2)}) collective-permute-start(bf16[2,128,512]{2,1,0:T(8,128)(2,1)S(1)} %project.5), channel_id=1, source_target_pairs={{0,4},{4,0},{8,12},{12,8},{1,5},{5,1},{9,13},{13,9},{2,6},{6,2},{1... | collective-permute-start | bytes 786440 | tf_op jit(solution)/shard_map/ppermute | solution.py:244
  41.2 16.9 %collective-permute-start.14 = (bf16[2,256,512]{2,1,0:T(8,128)(2,1)S(1)}, bf16[2,256,512]{2,1,0:T(8,128)(2,1)S(1)}, u32[]{:S(2)}, u32[]{:S(2)}) collective-permute-start(bf16[2,256,512]{2,1,0:T(8,128)(2,1)S(1)} %project.7), channel_id=1, source_target_pairs={{0,4},{4,0},{8,12},{12,8},{1,5},{5,1},{9,13},{13,9},{2,6},{6,2},{1... | collective-permute-start | bytes 1572872 | tf_op jit(solution)/shard_map/ppermute | solution.py:244
  41.6 14.8 %collective-permute-start.19 = (bf16[2,256,512]{2,1,0:T(8,128)(2,1)S(1)}, bf16[2,256,512]{2,1,0:T(8,128)(2,1)S(1)}, u32[]{:S(2)}, u32[]{:S(2)}) collective-permute-start(bf16[2,256,512]{2,1,0:T(8,128)(2,1)S(1)} %project.7), channel_id=1, source_target_pairs={{0,16},{16,0},{12,28},{28,12},{4,8},{8,4},{20,24},{24,20},{1,17},{... | collective-permute-start | bytes 1572872 | tf_op jit(solution)/shard_map/ppermute | solution.py:249
  49.5 12.6 %collective-permute-start.17 = (bf16[2,128,512]{2,1,0:T(8,128)(2,1)S(1)}, bf16[2,128,512]{2,1,0:T(8,128)(2,1)S(1)}, u32[]{:S(2)}, u32[]{:S(2)}) collective-permute-start(bf16[2,128,512]{2,1,0:T(8,128)(2,1)S(1)} %project.5), channel_id=1, source_target_pairs={{0,16},{16,0},{12,28},{28,12},{4,8},{8,4},{20,24},{24,20},{1,17},{... | collective-permute-start | bytes 786440 | tf_op jit(solution)/shard_map/ppermute | solution.py:249
  49.9 13.9 %collective-permute-start.16 = (bf16[2,128,512]{2,1,0:T(8,128)(2,1)S(1)}, bf16[2,128,512]{2,1,0:T(8,128)(2,1)S(1)}, u32[]{:S(2)}, u32[]{:S(2)}) collective-permute-start(bf16[2,128,512]{2,1,0:T(8,128)(2,1)S(1)} %collective-permute-done.15), channel_id=1, source_target_pairs={{0,4},{4,0},{8,12},{12,8},{1,5},{5,1},{9,13},{13,9},{2,6},{6,2},{1... | collective-permute-start | bytes 786440 | tf_op jit(solution)/shard_map/ppermute | solution.py:244
  56.4 29.1 %collective-permute-start.20 = (bf16[2,256,512]{2,1,0:T(8,128)(2,1)S(1)}, bf16[2,256,512]{2,1,0:T(8,128)(2,1)S(1)}, u32[]{:S(2)}, u32[]{:S(2)}) collective-permute-start(bf16[2,256,512]{2,1,0:T(8,128)(2,1)S(1)} %collective-permute-done.19), channel_id=1, source_target_pairs={{0,4},{4,0},{8,12},{12,8},{1,5},{5,1},{9,13},{13,9},{2,6},{6,2},{1... | collective-permute-start | bytes 1572872 | tf_op jit(solution)/shard_map/ppermute | solution.py:244
  58.1 27.0 %collective-permute-start.25 = (bf16[2,256,512]{2,1,0:T(8,128)(2,1)S(1)}, bf16[2,256,512]{2,1,0:T(8,128)(2,1)S(1)}, u32[]{:S(2)}, u32[]{:S(2)}) collective-permute-start(bf16[2,256,512]{2,1,0:T(8,128)(2,1)S(1)} %collective-permute-done.14), channel_id=1, source_target_pairs={{0,16},{16,0},{12,28},{28,12},{4,8},{8,4},{20,24},{24,20},{1,17},{... | collective-permute-start | bytes 1572872 | tf_op jit(solution)/shard_map/ppermute | solution.py:249
  59.7 19.1 %collective-permute-start.21 = (bf16[2,128,512]{2,1,0:T(8,128)(2,1)S(1)}, bf16[2,128,512]{2,1,0:T(8,128)(2,1)S(1)}, u32[]{:S(2)}, u32[]{:S(2)}) collective-permute-start(bf16[2,128,512]{2,1,0:T(8,128)(2,1)S(1)} %collective-permute-done.12), channel_id=1, source_target_pairs={{0,16},{16,0},{12,28},{28,12},{4,8},{8,4},{20,24},{24,20},{1,17},{... | collective-permute-start | bytes 786440 | tf_op jit(solution)/shard_map/ppermute | solution.py:249
  62.0 23.5 %collective-permute-start.18 = (bf16[2,128,512]{2,1,0:T(8,128)(2,1)S(1)}, bf16[2,128,512]{2,1,0:T(8,128)(2,1)S(1)}, u32[]{:S(2)}, u32[]{:S(2)}) collective-permute-start(bf16[2,128,512]{2,1,0:T(8,128)(2,1)S(1)} %collective-permute-done.17), channel_id=1, source_target_pairs={{0,4},{4,0},{8,12},{12,8},{1,5},{5,1},{9,13},{13,9},{2,6},{6,2},{1... | collective-permute-start | bytes 786440 | tf_op jit(solution)/shard_map/ppermute | solution.py:244
  63.7 19.8 %collective-permute-start.23 = (bf16[2,128,512]{2,1,0:T(8,128)(2,1)S(1)}, bf16[2,128,512]{2,1,0:T(8,128)(2,1)S(1)}, u32[]{:S(2)}, u32[]{:S(2)}) collective-permute-start(bf16[2,128,512]{2,1,0:T(8,128)(2,1)S(1)} %collective-permute-done.13), channel_id=1, source_target_pairs={{0,16},{16,0},{12,28},{28,12},{4,8},{8,4},{20,24},{24,20},{1,17},{... | collective-permute-start | bytes 786440 | tf_op jit(solution)/shard_map/ppermute | solution.py:249
  78.9 18.9 %collective-permute-start.22 = (bf16[2,128,512]{2,1,0:T(8,128)(2,1)S(1)}, bf16[2,128,512]{2,1,0:T(8,128)(2,1)S(1)}, u32[]{:S(2)}, u32[]{:S(2)}) collective-permute-start(bf16[2,128,512]{2,1,0:T(8,128)(2,1)S(1)} %collective-permute-done.21), channel_id=1, source_target_pairs={{0,4},{4,0},{8,12},{12,8},{1,5},{5,1},{9,13},{13,9},{2,6},{6,2},{1... | collective-permute-start | bytes 786440 | tf_op jit(solution)/shard_map/ppermute | solution.py:244
  83.5 14.3 %collective-permute-start.24 = (bf16[2,128,512]{2,1,0:T(8,128)(2,1)S(1)}, bf16[2,128,512]{2,1,0:T(8,128)(2,1)S(1)}, u32[]{:S(2)}, u32[]{:S(2)}) collective-permute-start(bf16[2,128,512]{2,1,0:T(8,128)(2,1)S(1)} %collective-permute-done.23), channel_id=1, source_target_pairs={{0,4},{4,0},{8,12},{12,8},{1,5},{5,1},{9,13},{13,9},{2,6},{6,2},{1... | collective-permute-start | bytes 786440 | tf_op jit(solution)/shard_map/ppermute | solution.py:244
  85.2 16.9 %collective-permute-start.26 = (bf16[2,256,512]{2,1,0:T(8,128)(2,1)S(1)}, bf16[2,256,512]{2,1,0:T(8,128)(2,1)S(1)}, u32[]{:S(2)}, u32[]{:S(2)}) collective-permute-start(bf16[2,256,512]{2,1,0:T(8,128)(2,1)S(1)} %collective-permute-done.25), channel_id=1, source_target_pairs={{0,4},{4,0},{8,12},{12,8},{1,5},{5,1},{9,13},{13,9},{2,6},{6,2},{1... | collective-permute-start | bytes 1572872 | tf_op jit(solution)/shard_map/ppermute | solution.py:244
  118.8 3.9 %collective-permute-start.32 = (bf16[2,256,1152]{2,1,0:T(8,128)(2,1)S(1)}, bf16[2,256,1152]{2,1,0:T(8,128)(2,1)S(1)}, u32[]{:S(2)}, u32[]{:S(2)}) collective-permute-start(bf16[2,256,1152]{2,1,0:T(8,128)(2,1)S(1)} %output.7), channel_id=1, source_target_pairs={{0,1},{1,0},{2,3},{3,2},{4,5},{5,4},{6,7},{7,6},{8,9},{9,8},{10,11... | collective-permute-start | bytes 3538952 | tf_op jit(solution)/shard_map/ppermute | solution.py:194
  119.0 16.2 %collective-permute-start.28 = (bf16[256,1152]{1,0:T(8,128)(2,1)S(1)}, bf16[256,1152]{1,0:T(8,128)(2,1)S(1)}, u32[]{:S(2)}, u32[]{:S(2)}) collective-permute-start(bf16[256,1152]{1,0:T(8,128)(2,1)S(1)} %fusion.3), channel_id=1, source_target_pairs={{0,2},{1,3},{2,0},{3,1},{4,6},{5,7},{6,4},{7,5},{8,10},{9,11},{10,... | collective-permute-start | bytes 1769480 | tf_op jit(solution)/shard_map/ppermute | solution.py:194
  123.0 24.4 %collective-permute-start.33 = (bf16[256,1152]{1,0:T(8,128)(2,1)S(1)}, bf16[256,1152]{1,0:T(8,128)(2,1)S(1)}, u32[]{:S(2)}, u32[]{:S(2)}) collective-permute-start(bf16[256,1152]{1,0:T(8,128)(2,1)S(1)} %fusion.4), channel_id=1, source_target_pairs={{0,2},{1,3},{2,0},{3,1},{4,6},{5,7},{6,4},{7,5},{8,10},{9,11},{10,... | collective-permute-start | bytes 1769480 | tf_op jit(solution)/shard_map/ppermute | solution.py:194
  135.6 13.8 %collective-permute-start.30 = (f32[256]{0:T(256)S(1)}, f32[256]{0:T(256)S(1)}, u32[]{:S(2)}, u32[]{:S(2)}) collective-permute-start(f32[256]{0:T(256)S(1)} %multiply_reduce_fusion.1), channel_id=1, source_target_pairs={{0,2},{1,3},{2,0},{3,1},{4,6},{5,7},{6,4},{7,5},{8,10},{9,11},{10,... | collective-permute-start | bytes 3080 | tf_op jit(solution)/shard_map/ppermute | solution.py:194
  137.3 12.6 %collective-permute-start.31 = (f32[256]{0:T(256)S(1)}, f32[256]{0:T(256)S(1)}, u32[]{:S(2)}, u32[]{:S(2)}) collective-permute-start(f32[256]{0:T(256)S(1)} %multiply_reduce_fusion.1), channel_id=1, source_target_pairs={{0,3},{1,2},{2,1},{3,0},{4,7},{5,6},{6,5},{7,4},{8,11},{9,10},{10,... | collective-permute-start | bytes 3080 | tf_op jit(solution)/shard_map/ppermute | solution.py:194
  137.3 12.6 %collective-permute-start.29 = (f32[256]{0:T(256)S(1)}, f32[256]{0:T(256)S(1)}, u32[]{:S(2)}, u32[]{:S(2)}) collective-permute-start(f32[256]{0:T(256)S(1)} %multiply_reduce_fusion.1), channel_id=1, source_target_pairs={{0,1},{1,0},{2,3},{3,2},{4,5},{5,4},{6,7},{7,6},{8,9},{9,8},{10,11... | collective-permute-start | bytes 3080 | tf_op jit(solution)/shard_map/ppermute | solution.py:194
  (18 other events, 95.3 us)

commit v7 on v6

--- a/solution.py
+++ b/solution.py
@@ -37,10 +37,11 @@
 SHORT = pl.CostEstimate(flops=1, transcendentals=0, bytes_accessed=1)
 
 
-def project_body(rank_ref, inverse_ref, *refs, chunks):
+def project_body(rank_ref, inverse_ref, after_ref, *refs, chunks):
     x_refs = refs[: 4 * chunks]
-    w_refs = refs[4 * chunks : -1]
-    out_ref = refs[-1]
+    w_refs = refs[4 * chunks : -2]
+    out_ref, mark_ref = refs[-2:]
+    mark_ref[...] = after_ref[...]
     features = x_refs[0].shape[1]
     start = 0
     for c in range(chunks):
@@ -57,21 +58,24 @@
             out_ref[i, span] = (total * inverse_ref[span]).astype(jnp.bfloat16)
 
 
-def project(ranks, chunks, inverse, weights):
+def project(ranks, after, chunks, inverse, weights):
     vmem = pl.BlockSpec(memory_space=pltpu.VMEM)
     blocks = [x for chunk in chunks for x in chunk]
     return pl.pallas_call(
         functools.partial(project_body, chunks=len(chunks)),
         in_specs=[pl.BlockSpec(memory_space=pltpu.SMEM)]
-        + [vmem] * (1 + len(blocks) + len(weights)),
-        out_specs=vmem,
-        out_shape=jax.ShapeDtypeStruct(
-            (len(weights), inverse.shape[0], weights[0].shape[1]), jnp.bfloat16
+        + [vmem] * (2 + len(blocks) + len(weights)),
+        out_specs=(vmem, vmem),
+        out_shape=(
+            jax.ShapeDtypeStruct(
+                (len(weights), inverse.shape[0], weights[0].shape[1]), jnp.bfloat16
+            ),
+            jax.ShapeDtypeStruct(after.shape, after.dtype),
         ),
         compiler_params=pltpu.CompilerParams(vmem_limit_bytes=24 * 2**20),
         cost_estimate=LONG,
         name="project",
-    )(ranks, inverse, *blocks, *weights)
+    )(ranks, inverse, after, *blocks, *weights)
 
 
 def scaled_scores(q, k, bias):
@@ -232,14 +236,19 @@
             squares = jnp.sum(wide * wide, axis=1)
             squares, own = lax.optimization_barrier((squares, own))
             square_sum = sum_over_tensor(squares)
-        blocks.append([own, swap(own, 1), far, swap(far, 1)])
+        blocks.append([own, swap(own, 1), far])
     inverse = lax.rsqrt(square_sum / model_width + epsilon)[:, None]
 
+    mark = blocks[0][0][:16, :HEAD]
     key_values = []
     for c, span in enumerate(spans):
+        if c in (1,):
+            blocks[c][2], mark = lax.optimization_barrier((blocks[c][2], mark))
+        blocks[c].append(swap(blocks[c][2], 1))
         if c:
             blocks[c][0], key_values[-1] = lax.optimization_barrier((blocks[c][0], key_values[-1]))
-        key_values.append(project(ranks, [blocks[c]], inverse[span], [w_key, w_value]))
+        projected, mark = project(ranks, mark, [blocks[c]], inverse[span], [w_key, w_value])
+        key_values.append(projected)
     def outer(parts):
         return [lax.ppermute(x, "cand", [(0, 1), (1, 0), (2, 3), (3, 2)]) for x in parts]
 
@@ -275,7 +284,7 @@
         [s * cand_local + jnp.arange(cand_local, dtype=jnp.int32) for s in shards]
     )
     bias = bias_rows(cand_lengths, pair_mask, place * cand_local, cand_local, key_cand)
-    queries = project(ranks, blocks, inverse, [w_query])
+    queries, _ = project(ranks, blocks[0][0][:16, :HEAD], blocks, inverse, [w_query])
     seen = 3 * row_count
     state = attention(bias[:, :seen], queries, slots, ends=False)
     state, last_slot = lax.optimization_barrier((state, last_slot))

time: 154 us -> 163 us (1.058)
  local copies, waits for them, and re-layouts: 5.89 us -> 12.2 us
  starting transfers between devices: 35.7 us -> 32.9 us
  Pallas kernels: 42.8 us -> 44.6 us
  waiting for transfers between devices: 62.1 us -> 63.8 us
    ppermute x6, waiting for transfers between devices: 22.9 us -> 30.3 us  [inner(): return [lax.ppermute(x, ('groups', 'cand'), inner_pairs) for x in parts]]
    unnamed x27 -> x33, local copies, waits for them, and re-layouts: 4.82 us -> 11.1 us
    ppermute x22, waiting for transfers between devices: 34.9 us -> 30.1 us  [swap(): return lax.ppermute(x, 'tensor', [(t, t ^ bit) for t in range(4)])]
    ppermute x9, starting transfers between devices: 13.2 us -> 10.8 us  [outer(): lax.ppermute(x, 'cand', [(0, 1), (1, 0), (2, 3), (3, 2)])]
    pallas_call x4, Pallas kernels: 13.7 us -> 15.7 us  [project(): pl.pallas_call(functools.partial(project_body, chunks=len(chunks)), in_sp...]
  transfers between devices with their start and end apart: 37 -> 37, of which waited for: 13 -> 12; matrix products, arithmetic and copies ran while one was open for 2% -> 3% of each run, Pallas kernels for 19% -> 19%
where the time goes in v7:
time: 163 us; the launch traced here: 162 us
  waiting for transfers between devices  63.8 us (39%)
  Pallas kernels  44.6 us (27%)
  starting transfers between devices  32.9 us (20%)
  local copies, waits for them, and re-layouts  12.2 us (7%)
  other arithmetic  7.31 us (4%)
    ppermute x6, waiting for transfers between devices, inner(): return [lax.ppermute(x, ('groups', 'cand'), inner_pairs) for x in parts]  30.3 us
    ppermute x22, waiting for transfers between devices, swap(): return lax.ppermute(x, 'tensor', [(t, t ^ bit) for t in range(4)])  30.1 us
    pallas_call x3, Pallas kernels, attention(): pl.pallas_call(functools.partial(attention_body, slots=len(slots), begun=...  20.6 us
    pallas_call x4, Pallas kernels, project(): pl.pallas_call(functools.partial(project_body, chunks=len(chunks)), in_sp...  15.7 us
    ppermute x22, starting transfers between devices, swap(): return lax.ppermute(x, 'tensor', [(t, t ^ bit) for t in range(4)])  15 us
    unnamed x33, local copies, waits for them, and re-layouts  11.1 us
    ppermute x9, starting transfers between devices, outer(): lax.ppermute(x, 'cand', [(0, 1), (1, 0), (2, 3), (3, 2)])  10.8 us
    pallas_call x4, Pallas kernels, output_blocks(): pl.pallas_call(output_body, in_specs=[pl.BlockSpec(memory_space=pltpu.SME...  8.31 us
  transfers between devices with their start and end apart: 37, of which 12 were waited for; matrix products, arithmetic and copies ran while one was open for 3% of the time, Pallas kernels for 19%

profile of v7, /device:TPU:0, one launch (start us, length us, event | category | flops | bytes accessed | tf_op | source)
XLA Modules:
  0.0 162.2 jit_solution(14531067720260206178)
XLA Ops:
  0.7 1.7 %fusion.1 = (f32[512]{0:T(512)S(1)}, bf16[512,1152]{1,0:T(8,128)(2,1)S(1)}) fusion(bf16[512,1152]{1,0:T(8,128)(2,1)} %param.9, f32[1152]{0:T(1024)S(1)} %convert_reduce_fusion.1), kind=kLoop, calls=%fused_computation.3 | loop fusion | flops 2948608 | bytes 2365952 | tf_op jit(solution)/shard_map/reduce_sum | solution.py:236
  2.5 3.0 %collective-permute-start.1 = (f32[512]{0:T(512)S(1)}, f32[512]{0:T(512)S(1)}, u32[]{:S(2)}, u32[]{:S(2)}) collective-permute-start(f32[512]{0:T(512)S(1)} %get-tuple-element.29), channel_id=1, source_target_pairs={{0,2},{1,3},{2,0},{3,1},{4,6},{5,7},{6,4},{7,5},{8,10},{9,11},{10,... | collective-permute-start | bytes 6152 | tf_op jit(solution)/shard_map/ppermute | solution.py:198
  5.7 1.9 %collective-permute-start.4 = (bf16[128,1152]{1,0:T(8,128)(2,1)S(1)}, bf16[128,1152]{1,0:T(8,128)(2,1)S(1)}, u32[]{:S(2)}, u32[]{:S(2)}) collective-permute-start(bf16[128,1152]{1,0:T(8,128)(2,1)S(1)} %get-tuple-element.31.refs_0_), channel_id=1, source_target_pairs={{0,2},{1,3},{2,0},{3,1},{4,6},{5,7},{6,4},{7,5},{8,10},{9,11},{10,... | collective-permute-start | bytes 884744 | tf_op jit(solution)/shard_map/ppermute | solution.py:198
  9.7 5.9 %collective-permute-done.4.refs_2_ = bf16[128,1152]{1,0:T(8,128)(2,1)S(1)} collective-permute-done((bf16[128,1152]{1,0:T(8,128)(2,1)S(1)}, bf16[128,1152]{1,0:T(8,128)(2,1)S(1)}, u32[]{:S(2)}, u32[]{:S(2)}) %collective-permute-start.4) | collective-permute-done | bytes 294944 | tf_op jit(solution)/shard_map/ppermute | solution.py:198
  15.7 2.0 %collective-permute-start.10 = (bf16[256,1152]{1,0:T(8,128)(2,1)S(1)}, bf16[256,1152]{1,0:T(8,128)(2,1)S(1)}, u32[]{:S(2)}, u32[]{:S(2)}) collective-permute-start(bf16[256,1152]{1,0:T(8,128)(2,1)S(1)} %slice.112.refs_8_.refs_0_), channel_id=1, source_target_pairs={{0,2},{1,3},{2,0},{3,1},{4,6},{5,7},{6,4},{7,5},{8,10},{9,11},{10,... | collective-permute-start | bytes 1769480 | tf_op jit(solution)/shard_map/ppermute | solution.py:198
  18.4 2.3 %copy-done = bf16[4608,512]{1,0:T(8,128)(2,1)S(1)} copy-done((bf16[4608,512]{1,0:T(8,128)(2,1)S(1)}, bf16[4608,512]{1,0:T(8,128)(2,1)}, u32[]{:S(2)}) %copy-start) | copy-done | bytes 4718616
  20.8 2.3 %copy-done.3 = bf16[4608,512]{1,0:T(8,128)(2,1)S(1)} copy-done((bf16[4608,512]{1,0:T(8,128)(2,1)S(1)}, bf16[4608,512]{1,0:T(8,128)(2,1)}, u32[]{:S(2)}) %copy-start.3) | copy-done | bytes 4718616
  24.1 2.1 %project.4 = (bf16[2,128,512]{2,1,0:T(8,128)(2,1)S(1)}, bf16[16,128]{1,0:T(8,128)(2,1)S(1)}) custom-call(s32[4]{0:T(128)S(1)} %pad_add_fusion.2.rank_ref, f32[128,1]{1,0:T(8,128)S(1)} %copy.12.inverse_ref, bf16[16,128]{1,0:T(8,128)(2,1)S(1)} %slice.85.after_ref, bf16[128,1152]{1,0:T(8,128)(2,1)S(1)} %get-tuple-element.31.refs_0_, ...), custom_call_target="tpu_custom_call" | custom-call | flops 10000000000 | bytes 1000000 | tf_op jit(solution)/shard_map/project/pallas_call | solution.py:64
  28.6 1.7 %collective-permute-start.12 = (bf16[2,128,512]{2,1,0:T(8,128)(2,1)S(1)}, bf16[2,128,512]{2,1,0:T(8,128)(2,1)S(1)}, u32[]{:S(2)}, u32[]{:S(2)}) collective-permute-start(bf16[2,128,512]{2,1,0:T(8,128)(2,1)S(1)} %get-tuple-element.42), channel_id=1, source_target_pairs={{0,4},{4,0},{8,12},{12,8},{1,5},{5,1},{9,13},{13,9},{2,6},{6,2},{1... | collective-permute-start | bytes 786440 | tf_op jit(solution)/shard_map/ppermute | solution.py:253
  30.3 4.8 %collective-permute-done.15 = bf16[2,128,512]{2,1,0:T(8,128)(2,1)} collective-permute-done((bf16[2,128,512]{2,1,0:T(8,128)(2,1)S(1)}, bf16[2,128,512]{2,1,0:T(8,128)(2,1)}, u32[]{:S(2)}, u32[]{:S(2)}) %collective-permute-start.15) | collective-permute-done | bytes 262176 | tf_op jit(solution)/shard_map/ppermute | solution.py:258
  35.0 1.6 collective-permute-start.16
  36.7 2.3 %copy-done.1 = bf16[4608,512]{1,0:T(8,128)(2,1)S(1)} copy-done((bf16[4608,512]{1,0:T(8,128)(2,1)S(1)}, bf16[4608,512]{1,0:T(8,128)(2,1)}, u32[]{:S(2)}) %copy-start.1) | copy-done | bytes 4718616
  39.0 2.3 %copy-done.4 = bf16[4608,512]{1,0:T(8,128)(2,1)S(1)} copy-done((bf16[4608,512]{1,0:T(8,128)(2,1)S(1)}, bf16[4608,512]{1,0:T(8,128)(2,1)}, u32[]{:S(2)}) %copy-start.4) | copy-done | bytes 4718616
  41.3 2.8 %project.5 = (bf16[2,128,512]{2,1,0:T(8,128)(2,1)S(1)}, bf16[16,128]{1,0:T(8,128)(2,1)S(1)}) custom-call(s32[4]{0:T(128)S(1)} %pad_add_fusion.2.rank_ref, f32[128,1]{1,0:T(8,128)S(1)} %copy.13.inverse_ref, bf16[16,128]{1,0:T(8,128)(2,1)S(1)} %get-tuple-element.38.after_ref, bf16[128,1152]{1,0:T(8,128)(2,1)S(1)} %get-tuple-element.34.refs_0_.refs_4_, ...), custom_call_target="tpu_custom_call" | custom-call | flops 10000000000 | bytes 1000000 | tf_op jit(solution)/shard_map/project/pallas_call | solution.py:64
  44.6 3.8 %project.7 = (bf16[2,256,512]{2,1,0:T(8,128)(2,1)S(1)}, bf16[16,128]{1,0:T(8,128)(2,1)}) custom-call(s32[4]{0:T(128)S(1)} %pad_add_fusion.2.rank_ref, f32[256,1]{1,0:T(8,128)S(1)} %copy.15.inverse_ref, bf16[16,128]{1,0:T(8,128)(2,1)S(1)} %get-tuple-element.44.after_ref, bf16[256,1152]{1,0:T(8,128)(2,1)S(1)} %slice.112.refs_8_.refs_0_, ...), custom_call_target="tpu_custom_call" | custom-call | flops 10000000000 | bytes 1000000 | tf_op jit(solution)/shard_map/project/pallas_call | solution.py:64
  48.4 1.6 collective-permute-start.14
  51.5 7.1 %project.6 = (bf16[1,512,1024]{2,1,0:T(8,128)(2,1)S(1)}, bf16[16,128]{1,0:T(8,128)(2,1)}) custom-call(s32[4]{0:T(128)S(1)} %pad_add_fusion.2.rank_ref, f32[512,1]{1,0:T(8,128)S(1)} %copy.14.inverse_ref, bf16[16,128]{1,0:T(8,128)(2,1)S(1)} %slice.85.after_ref, bf16[128,1152]{1,0:T(8,128)(2,1)S(1)} %get-tuple-element.31.refs_0_, ...), custom_call_target="tpu_custom_call" | custom-call | flops 10000000000 | bytes 1000000 | tf_op jit(solution)/shard_map/project/pallas_call | solution.py:64
  59.1 5.7 %collective-permute-done.19 = bf16[2,256,512]{2,1,0:T(8,128)(2,1)S(1)} collective-permute-done((bf16[2,256,512]{2,1,0:T(8,128)(2,1)S(1)}, bf16[2,256,512]{2,1,0:T(8,128)(2,1)S(1)}, u32[]{:S(2)}, u32[]{:S(2)}) %collective-permute-start.19) | collective-permute-done | bytes 524320 | tf_op jit(solution)/shard_map/ppermute | solution.py:258
  65.9 1.5 collective-permute-start.25
  68.1 2.3 %collective-permute-done.17 = bf16[2,128,512]{2,1,0:T(8,128)(2,1)S(1)} collective-permute-done((bf16[2,128,512]{2,1,0:T(8,128)(2,1)S(1)}, bf16[2,128,512]{2,1,0:T(8,128)(2,1)S(1)}, u32[]{:S(2)}, u32[]{:S(2)}) %collective-permute-start.17) | collective-permute-done | bytes 262176 | tf_op jit(solution)/shard_map/ppermute | solution.py:258
  73.2 14.0 %collective-permute-done.21 = bf16[2,128,512]{2,1,0:T(8,128)(2,1)S(1)} collective-permute-done((bf16[2,128,512]{2,1,0:T(8,128)(2,1)S(1)}, bf16[2,128,512]{2,1,0:T(8,128)(2,1)S(1)}, u32[]{:S(2)}, u32[]{:S(2)}) %collective-permute-start.21) | collective-permute-done | bytes 262176 | tf_op jit(solution)/shard_map/ppermute | solution.py:258
  88.4 3.5 %collective-permute-done.23 = bf16[2,128,512]{2,1,0:T(8,128)(2,1)S(1)} collective-permute-done((bf16[2,128,512]{2,1,0:T(8,128)(2,1)S(1)}, bf16[2,128,512]{2,1,0:T(8,128)(2,1)S(1)}, u32[]{:S(2)}, u32[]{:S(2)}) %collective-permute-start.23) | collective-permute-done | bytes 262176 | tf_op jit(solution)/shard_map/ppermute | solution.py:258
  95.3 11.8 %attention.3 = (f32[512,1024]{1,0:T(8,128)S(1)}, f32[512,512]{1,0:T(8,128)S(1)}) custom-call(f32[4,1536]{1,0:T(4,128)S(1)} %slice.113.bias_ref, bf16[1,512,1024]{2,1,0:T(8,128)(2,1)S(1)} %get-tuple-element.41.q_ref, bf16[2,512,512]{2,1,0:T(8,128)(2,1)S(1)} %pad_maximum_fusion.1.refs_0_.refs_1_, bf16[2,512,512]{2,1,0:T(8,128)(2,1)S(1)} %pad_maximum_fusion.1.refs_0_.refs_1_, ...), custom_call_target="tpu_custom_call" | custom-call | flops 10000000000 | bytes 1000000 | tf_op jit(solution)/shard_map/attention/pallas_call | solution.py:161
  107.1 3.3 %collective-permute-done.26 = bf16[2,256,512]{2,1,0:T(8,128)(2,1)S(1)} collective-permute-done((bf16[2,256,512]{2,1,0:T(8,128)(2,1)S(1)}, bf16[2,256,512]{2,1,0:T(8,128)(2,1)S(1)}, u32[]{:S(2)}, u32[]{:S(2)}) %collective-permute-start.26) | collective-permute-done | bytes 524320 | tf_op jit(solution)/shard_map/ppermute | solution.py:253
  111.1 4.4 %attention.4.x_ref = bf16[256,1024]{1,0:T(8,128)(2,1)S(1)} custom-call(f32[2,512]{1,0:T(2,128)S(1)} %get-tuple-element.63.bias_ref, bf16[1,256,1024]{2,1,0:T(8,128)(2,1)S(1)} %get-tuple-element.61.q_ref, bf16[2,512,512]{2,1,0:T(8,128)(2,1)S(1)} %maximum_select_fusion.1.refs_0_.refs_1_, bf16[2,512,512]{2,1,0:T(8,128)(2,1)S(1)} %maximum_select_fusion.1.refs_0_.refs_1_, ...), custom_call_target="tpu_custom_call" | custom-call | flops 10000000000 | bytes 1000000 | tf_op jit(solution)/shard_map/attention/pallas_call | solution.py:161
  115.6 2.1 %output.5 = bf16[2,256,1152]{2,1,0:T(8,128)(2,1)S(1)} custom-call(s32[2]{0:T(128)S(1)} %pad_add_fusion.3.block_ref, bf16[256,1024]{1,0:T(8,128)(2,1)S(1)} %attention.4.x_ref, bf16[1024,4608]{1,0:T(8,128)(2,1)S(1)} %bitcast.43), custom_call_target="tpu_custom_call" | custom-call | flops 10000000000 | bytes 1000000 | tf_op jit(solution)/shard_map/output/pallas_call | solution.py:182
  117.8 2.1 %output.4 = bf16[2,256,1152]{2,1,0:T(8,128)(2,1)S(1)} custom-call(s32[2]{0:T(128)S(1)} %pad_add_fusion.block_ref, bf16[256,1024]{1,0:T(8,128)(2,1)S(1)} %attention.4.x_ref, bf16[1024,4608]{1,0:T(8,128)(2,1)S(1)} %bitcast.43), custom_call_target="tpu_custom_call" | custom-call | flops 10000000000 | bytes 1000000 | tf_op jit(solution)/shard_map/output/pallas_call | solution.py:182
  120.7 4.4 %attention.5.x_ref = bf16[256,1024]{1,0:T(8,128)(2,1)S(1)} custom-call(f32[2,512]{1,0:T(2,128)S(1)} %get-tuple-element.64.bias_ref, bf16[1,256,1024]{2,1,0:T(8,128)(2,1)S(1)} %get-tuple-element.62.q_ref, bf16[2,512,512]{2,1,0:T(8,128)(2,1)S(1)} %maximum_select_fusion.1.refs_0_.refs_1_, bf16[2,512,512]{2,1,0:T(8,128)(2,1)S(1)} %maximum_select_fusion.1.refs_0_.refs_1_, ...), custom_call_target="tpu_custom_call" | custom-call | flops 10000000000 | bytes 1000000 | tf_op jit(solution)/shard_map/attention/pallas_call | solution.py:161
  125.1 2.1 %output.7 = bf16[2,256,1152]{2,1,0:T(8,128)(2,1)S(1)} custom-call(s32[2]{0:T(128)S(1)} %pad_add_fusion.3.block_ref, bf16[256,1024]{1,0:T(8,128)(2,1)S(1)} %attention.5.x_ref, bf16[1024,4608]{1,0:T(8,128)(2,1)S(1)} %bitcast.43), custom_call_target="tpu_custom_call" | custom-call | flops 10000000000 | bytes 1000000 | tf_op jit(solution)/shard_map/output/pallas_call | solution.py:182
  128.8 2.1 %output.6 = bf16[2,256,1152]{2,1,0:T(8,128)(2,1)S(1)} custom-call(s32[2]{0:T(128)S(1)} %pad_add_fusion.block_ref, bf16[256,1024]{1,0:T(8,128)(2,1)S(1)} %attention.5.x_ref, bf16[1024,4608]{1,0:T(8,128)(2,1)S(1)} %bitcast.43), custom_call_target="tpu_custom_call" | custom-call | flops 10000000000 | bytes 1000000 | tf_op jit(solution)/shard_map/output/pallas_call | solution.py:182
  131.8 11.8 %collective-permute-done.28 = bf16[256,1152]{1,0:T(8,128)(2,1)S(1)} collective-permute-done((bf16[256,1152]{1,0:T(8,128)(2,1)S(1)}, bf16[256,1152]{1,0:T(8,128)(2,1)S(1)}, u32[]{:S(2)}, u32[]{:S(2)}) %collective-permute-start.28) | collective-permute-done | bytes 589856 | tf_op jit(solution)/shard_map/ppermute | solution.py:198
  146.2 9.5 %collective-permute-done.33 = bf16[256,1152]{1,0:T(8,128)(2,1)S(1)} collective-permute-done((bf16[256,1152]{1,0:T(8,128)(2,1)S(1)}, bf16[256,1152]{1,0:T(8,128)(2,1)S(1)}, u32[]{:S(2)}, u32[]{:S(2)}) %collective-permute-start.33) | collective-permute-done | bytes 589856 | tf_op jit(solution)/shard_map/ppermute | solution.py:198
  (131 shorter events, 31.9 us)
Async XLA Ops:
  2.5 6.6 %collective-permute-start.1 = (f32[512]{0:T(512)S(1)}, f32[512]{0:T(512)S(1)}, u32[]{:S(2)}, u32[]{:S(2)}) collective-permute-start(f32[512]{0:T(512)S(1)} %get-tuple-element.29), channel_id=1, source_target_pairs={{0,2},{1,3},{2,0},{3,1},{4,6},{5,7},{6,4},{7,5},{8,10},{9,11},{10,... | collective-permute-start | bytes 6152 | tf_op jit(solution)/shard_map/ppermute | solution.py:198
  5.5 3.5 %collective-permute-start = (f32[512]{0:T(512)S(1)}, f32[512]{0:T(512)S(1)}, u32[]{:S(2)}, u32[]{:S(2)}) collective-permute-start(f32[512]{0:T(512)S(1)} %get-tuple-element.29), channel_id=1, source_target_pairs={{0,1},{1,0},{2,3},{3,2},{4,5},{5,4},{6,7},{7,6},{8,9},{9,8},{10,11... | collective-permute-start | bytes 6152 | tf_op jit(solution)/shard_map/ppermute | solution.py:198
  5.7 9.9 %collective-permute-start.4 = (bf16[128,1152]{1,0:T(8,128)(2,1)S(1)}, bf16[128,1152]{1,0:T(8,128)(2,1)S(1)}, u32[]{:S(2)}, u32[]{:S(2)}) collective-permute-start(bf16[128,1152]{1,0:T(8,128)(2,1)S(1)} %get-tuple-element.31.refs_0_), channel_id=1, source_target_pairs={{0,2},{1,3},{2,0},{3,1},{4,6},{5,7},{6,4},{7,5},{8,10},{9,11},{10,... | collective-permute-start | bytes 884744 | tf_op jit(solution)/shard_map/ppermute | solution.py:198
  7.6 10.1 %collective-permute-start.3 = (bf16[128,1152]{1,0:T(8,128)(2,1)S(1)}, bf16[128,1152]{1,0:T(8,128)(2,1)S(1)}, u32[]{:S(2)}, u32[]{:S(2)}) collective-permute-start(bf16[128,1152]{1,0:T(8,128)(2,1)S(1)} %get-tuple-element.31.refs_0_), channel_id=1, source_target_pairs={{0,1},{1,0},{2,3},{3,2},{4,5},{5,4},{6,7},{7,6},{8,9},{9,8},{10,11... | collective-permute-start | bytes 884744 | tf_op jit(solution)/shard_map/ppermute | solution.py:198
  9.1 19.5 %collective-permute-start.6 = (bf16[128,1152]{1,0:T(8,128)(2,1)S(1)}, bf16[128,1152]{1,0:T(8,128)(2,1)S(1)}, u32[]{:S(2)}, u32[]{:S(2)}) collective-permute-start(bf16[128,1152]{1,0:T(8,128)(2,1)S(1)} %get-tuple-element.34.refs_0_.refs_4_), channel_id=1, source_target_pairs={{0,1},{1,0},{2,3},{3,2},{4,5},{5,4},{6,7},{7,6},{8,9},{9,8},{10,11... | collective-permute-start | bytes 884744 | tf_op jit(solution)/shard_map/ppermute | solution.py:198
  9.6 16.5 %collective-permute-start.7 = (bf16[128,1152]{1,0:T(8,128)(2,1)S(1)}, bf16[128,1152]{1,0:T(8,128)(2,1)}, u32[]{:S(2)}, u32[]{:S(2)}) collective-permute-start(bf16[128,1152]{1,0:T(8,128)(2,1)S(1)} %get-tuple-element.34.refs_0_.refs_4_), channel_id=1, source_target_pairs={{0,2},{1,3},{2,0},{3,1},{4,6},{5,7},{6,4},{7,5},{8,10},{9,11},{10,... | collective-permute-start | bytes 884744 | tf_op jit(solution)/shard_map/ppermute | solution.py:198
  15.7 20.9 %collective-permute-start.10 = (bf16[256,1152]{1,0:T(8,128)(2,1)S(1)}, bf16[256,1152]{1,0:T(8,128)(2,1)S(1)}, u32[]{:S(2)}, u32[]{:S(2)}) collective-permute-start(bf16[256,1152]{1,0:T(8,128)(2,1)S(1)} %slice.112.refs_8_.refs_0_), channel_id=1, source_target_pairs={{0,2},{1,3},{2,0},{3,1},{4,6},{5,7},{6,4},{7,5},{8,10},{9,11},{10,... | collective-permute-start | bytes 1769480 | tf_op jit(solution)/shard_map/ppermute | solution.py:198
  26.2 10.5 %collective-permute-start.8 = (bf16[128,1152]{1,0:T(8,128)(2,1)}, bf16[128,1152]{1,0:T(8,128)(2,1)}, u32[]{:S(2)}, u32[]{:S(2)}) collective-permute-start(bf16[128,1152]{1,0:T(8,128)(2,1)} %collective-permute-done.7.refs_2_.refs_6_), channel_id=1, source_target_pairs={{0,1},{1,0},{2,3},{3,2},{4,5},{5,4},{6,7},{7,6},{8,9},{9,8},{10,11... | collective-permute-start | bytes 884744 | tf_op jit(solution)/shard_map/ppermute | solution.py:198
  26.4 8.6 %collective-permute-start.15 = (bf16[2,128,512]{2,1,0:T(8,128)(2,1)S(1)}, bf16[2,128,512]{2,1,0:T(8,128)(2,1)}, u32[]{:S(2)}, u32[]{:S(2)}) collective-permute-start(bf16[2,128,512]{2,1,0:T(8,128)(2,1)S(1)} %get-tuple-element.42), channel_id=1, source_target_pairs={{0,16},{16,0},{12,28},{28,12},{4,8},{8,4},{20,24},{24,20},{1,17},{... | collective-permute-start | bytes 786440 | tf_op jit(solution)/shard_map/ppermute | solution.py:258
  28.5 16.1 %collective-permute-start.9 = (bf16[256,1152]{1,0:T(8,128)(2,1)S(1)}, bf16[256,1152]{1,0:T(8,128)(2,1)S(1)}, u32[]{:S(2)}, u32[]{:S(2)}) collective-permute-start(bf16[256,1152]{1,0:T(8,128)(2,1)S(1)} %slice.112.refs_8_.refs_0_), channel_id=1, source_target_pairs={{0,1},{1,0},{2,3},{3,2},{4,5},{5,4},{6,7},{7,6},{8,9},{9,8},{10,11... | collective-permute-start | bytes 1769480 | tf_op jit(solution)/shard_map/ppermute | solution.py:198
  28.6 30.1 %collective-permute-start.12 = (bf16[2,128,512]{2,1,0:T(8,128)(2,1)S(1)}, bf16[2,128,512]{2,1,0:T(8,128)(2,1)S(1)}, u32[]{:S(2)}, u32[]{:S(2)}) collective-permute-start(bf16[2,128,512]{2,1,0:T(8,128)(2,1)S(1)} %get-tuple-element.42), channel_id=1, source_target_pairs={{0,4},{4,0},{8,12},{12,8},{1,5},{5,1},{9,13},{13,9},{2,6},{6,2},{1... | collective-permute-start | bytes 786440 | tf_op jit(solution)/shard_map/ppermute | solution.py:253
  35.0 32.5 %collective-permute-start.16 = (bf16[2,128,512]{2,1,0:T(8,128)(2,1)}, bf16[2,128,512]{2,1,0:T(8,128)(2,1)S(1)}, u32[]{:S(2)}, u32[]{:S(2)}) collective-permute-start(bf16[2,128,512]{2,1,0:T(8,128)(2,1)} %collective-permute-done.15), channel_id=1, source_target_pairs={{0,4},{4,0},{8,12},{12,8},{1,5},{5,1},{9,13},{13,9},{2,6},{6,2},{1... | collective-permute-start | bytes 786440 | tf_op jit(solution)/shard_map/ppermute | solution.py:253
  36.6 8.0 %collective-permute-start.11 = (bf16[256,1152]{1,0:T(8,128)(2,1)S(1)}, bf16[256,1152]{1,0:T(8,128)(2,1)S(1)}, u32[]{:S(2)}, u32[]{:S(2)}) collective-permute-start(bf16[256,1152]{1,0:T(8,128)(2,1)S(1)} %collective-permute-done.10.refs_10_.refs_2_), channel_id=1, source_target_pairs={{0,1},{1,0},{2,3},{3,2},{4,5},{5,4},{6,7},{7,6},{8,9},{9,8},{10,11... | collective-permute-start | bytes 1769480 | tf_op jit(solution)/shard_map/ppermute | solution.py:198
  44.1 27.5 %collective-permute-start.13 = (bf16[2,128,512]{2,1,0:T(8,128)(2,1)S(1)}, bf16[2,128,512]{2,1,0:T(8,128)(2,1)S(1)}, u32[]{:S(2)}, u32[]{:S(2)}) collective-permute-start(bf16[2,128,512]{2,1,0:T(8,128)(2,1)S(1)} %get-tuple-element.43), channel_id=1, source_target_pairs={{0,4},{4,0},{8,12},{12,8},{1,5},{5,1},{9,13},{13,9},{2,6},{6,2},{1... | collective-permute-start | bytes 786440 | tf_op jit(solution)/shard_map/ppermute | solution.py:253
  48.4 17.5 %collective-permute-start.14 = (bf16[2,256,512]{2,1,0:T(8,128)(2,1)S(1)}, bf16[2,256,512]{2,1,0:T(8,128)(2,1)S(1)}, u32[]{:S(2)}, u32[]{:S(2)}) collective-permute-start(bf16[2,256,512]{2,1,0:T(8,128)(2,1)S(1)} %get-tuple-element.45), channel_id=1, source_target_pairs={{0,4},{4,0},{8,12},{12,8},{1,5},{5,1},{9,13},{13,9},{2,6},{6,2},{1... | collective-permute-start | bytes 1572872 | tf_op jit(solution)/shard_map/ppermute | solution.py:253
  50.0 14.8 %collective-permute-start.19 = (bf16[2,256,512]{2,1,0:T(8,128)(2,1)S(1)}, bf16[2,256,512]{2,1,0:T(8,128)(2,1)S(1)}, u32[]{:S(2)}, u32[]{:S(2)}) collective-permute-start(bf16[2,256,512]{2,1,0:T(8,128)(2,1)S(1)} %get-tuple-element.45), channel_id=1, source_target_pairs={{0,16},{16,0},{12,28},{28,12},{4,8},{8,4},{20,24},{24,20},{1,17},{... | collective-permute-start | bytes 1572872 | tf_op jit(solution)/shard_map/ppermute | solution.py:258
  58.6 11.8 %collective-permute-start.17 = (bf16[2,128,512]{2,1,0:T(8,128)(2,1)S(1)}, bf16[2,128,512]{2,1,0:T(8,128)(2,1)S(1)}, u32[]{:S(2)}, u32[]{:S(2)}) collective-permute-start(bf16[2,128,512]{2,1,0:T(8,128)(2,1)S(1)} %get-tuple-element.43), channel_id=1, source_target_pairs={{0,16},{16,0},{12,28},{28,12},{4,8},{8,4},{20,24},{24,20},{1,17},{... | collective-permute-start | bytes 786440 | tf_op jit(solution)/shard_map/ppermute | solution.py:258
  64.8 29.1 %collective-permute-start.20 = (bf16[2,256,512]{2,1,0:T(8,128)(2,1)S(1)}, bf16[2,256,512]{2,1,0:T(8,128)(2,1)S(1)}, u32[]{:S(2)}, u32[]{:S(2)}) collective-permute-start(bf16[2,256,512]{2,1,0:T(8,128)(2,1)S(1)} %collective-permute-done.19), channel_id=1, source_target_pairs={{0,4},{4,0},{8,12},{12,8},{1,5},{5,1},{9,13},{13,9},{2,6},{6,2},{1... | collective-permute-start | bytes 1572872 | tf_op jit(solution)/shard_map/ppermute | solution.py:253
  65.9 27.3 %collective-permute-start.25 = (bf16[2,256,512]{2,1,0:T(8,128)(2,1)S(1)}, bf16[2,256,512]{2,1,0:T(8,128)(2,1)S(1)}, u32[]{:S(2)}, u32[]{:S(2)}) collective-permute-start(bf16[2,256,512]{2,1,0:T(8,128)(2,1)S(1)} %collective-permute-done.14), channel_id=1, source_target_pairs={{0,16},{16,0},{12,28},{28,12},{4,8},{8,4},{20,24},{24,20},{1,17},{... | collective-permute-start | bytes 1572872 | tf_op jit(solution)/shard_map/ppermute | solution.py:258
  67.5 19.7 %collective-permute-start.21 = (bf16[2,128,512]{2,1,0:T(8,128)(2,1)S(1)}, bf16[2,128,512]{2,1,0:T(8,128)(2,1)S(1)}, u32[]{:S(2)}, u32[]{:S(2)}) collective-permute-start(bf16[2,128,512]{2,1,0:T(8,128)(2,1)S(1)} %collective-permute-done.12), channel_id=1, source_target_pairs={{0,16},{16,0},{12,28},{28,12},{4,8},{8,4},{20,24},{24,20},{1,17},{... | collective-permute-start | bytes 786440 | tf_op jit(solution)/shard_map/ppermute | solution.py:258
  70.4 23.5 %collective-permute-start.18 = (bf16[2,128,512]{2,1,0:T(8,128)(2,1)S(1)}, bf16[2,128,512]{2,1,0:T(8,128)(2,1)S(1)}, u32[]{:S(2)}, u32[]{:S(2)}) collective-permute-start(bf16[2,128,512]{2,1,0:T(8,128)(2,1)S(1)} %collective-permute-done.17), channel_id=1, source_target_pairs={{0,4},{4,0},{8,12},{12,8},{1,5},{5,1},{9,13},{13,9},{2,6},{6,2},{1... | collective-permute-start | bytes 786440 | tf_op jit(solution)/shard_map/ppermute | solution.py:253
  71.5 20.3 %collective-permute-start.23 = (bf16[2,128,512]{2,1,0:T(8,128)(2,1)S(1)}, bf16[2,128,512]{2,1,0:T(8,128)(2,1)S(1)}, u32[]{:S(2)}, u32[]{:S(2)}) collective-permute-start(bf16[2,128,512]{2,1,0:T(8,128)(2,1)S(1)} %collective-permute-done.13), channel_id=1, source_target_pairs={{0,16},{16,0},{12,28},{28,12},{4,8},{8,4},{20,24},{24,20},{1,17},{... | collective-permute-start | bytes 786440 | tf_op jit(solution)/shard_map/ppermute | solution.py:258
  87.3 19.9 %collective-permute-start.22 = (bf16[2,128,512]{2,1,0:T(8,128)(2,1)S(1)}, bf16[2,128,512]{2,1,0:T(8,128)(2,1)S(1)}, u32[]{:S(2)}, u32[]{:S(2)}) collective-permute-start(bf16[2,128,512]{2,1,0:T(8,128)(2,1)S(1)} %collective-permute-done.21), channel_id=1, source_target_pairs={{0,4},{4,0},{8,12},{12,8},{1,5},{5,1},{9,13},{13,9},{2,6},{6,2},{1... | collective-permute-start | bytes 786440 | tf_op jit(solution)/shard_map/ppermute | solution.py:253
  91.9 15.3 %collective-permute-start.24 = (bf16[2,128,512]{2,1,0:T(8,128)(2,1)S(1)}, bf16[2,128,512]{2,1,0:T(8,128)(2,1)S(1)}, u32[]{:S(2)}, u32[]{:S(2)}) collective-permute-start(bf16[2,128,512]{2,1,0:T(8,128)(2,1)S(1)} %collective-permute-done.23), channel_id=1, source_target_pairs={{0,4},{4,0},{8,12},{12,8},{1,5},{5,1},{9,13},{13,9},{2,6},{6,2},{1... | collective-permute-start | bytes 786440 | tf_op jit(solution)/shard_map/ppermute | solution.py:253
  93.3 17.2 %collective-permute-start.26 = (bf16[2,256,512]{2,1,0:T(8,128)(2,1)S(1)}, bf16[2,256,512]{2,1,0:T(8,128)(2,1)S(1)}, u32[]{:S(2)}, u32[]{:S(2)}) collective-permute-start(bf16[2,256,512]{2,1,0:T(8,128)(2,1)S(1)} %collective-permute-done.25), channel_id=1, source_target_pairs={{0,4},{4,0},{8,12},{12,8},{1,5},{5,1},{9,13},{13,9},{2,6},{6,2},{1... | collective-permute-start | bytes 1572872 | tf_op jit(solution)/shard_map/ppermute | solution.py:253
  127.2 3.7 %collective-permute-start.32 = (bf16[2,256,1152]{2,1,0:T(8,128)(2,1)S(1)}, bf16[2,256,1152]{2,1,0:T(8,128)(2,1)S(1)}, u32[]{:S(2)}, u32[]{:S(2)}) collective-permute-start(bf16[2,256,1152]{2,1,0:T(8,128)(2,1)S(1)} %output.7), channel_id=1, source_target_pairs={{0,1},{1,0},{2,3},{3,2},{4,5},{5,4},{6,7},{7,6},{8,9},{9,8},{10,11... | collective-permute-start | bytes 3538952 | tf_op jit(solution)/shard_map/ppermute | solution.py:198
  127.4 16.2 %collective-permute-start.28 = (bf16[256,1152]{1,0:T(8,128)(2,1)S(1)}, bf16[256,1152]{1,0:T(8,128)(2,1)S(1)}, u32[]{:S(2)}, u32[]{:S(2)}) collective-permute-start(bf16[256,1152]{1,0:T(8,128)(2,1)S(1)} %fusion.3), channel_id=1, source_target_pairs={{0,2},{1,3},{2,0},{3,1},{4,6},{5,7},{6,4},{7,5},{8,10},{9,11},{10,... | collective-permute-start | bytes 1769480 | tf_op jit(solution)/shard_map/ppermute | solution.py:198
  131.0 24.6 %collective-permute-start.33 = (bf16[256,1152]{1,0:T(8,128)(2,1)S(1)}, bf16[256,1152]{1,0:T(8,128)(2,1)S(1)}, u32[]{:S(2)}, u32[]{:S(2)}) collective-permute-start(bf16[256,1152]{1,0:T(8,128)(2,1)S(1)} %fusion.4), channel_id=1, source_target_pairs={{0,2},{1,3},{2,0},{3,1},{4,6},{5,7},{6,4},{7,5},{8,10},{9,11},{10,... | collective-permute-start | bytes 1769480 | tf_op jit(solution)/shard_map/ppermute | solution.py:198
  143.9 13.5 %collective-permute-start.30 = (f32[256]{0:T(256)S(1)}, f32[256]{0:T(256)S(1)}, u32[]{:S(2)}, u32[]{:S(2)}) collective-permute-start(f32[256]{0:T(256)S(1)} %multiply_reduce_fusion.1), channel_id=1, source_target_pairs={{0,2},{1,3},{2,0},{3,1},{4,6},{5,7},{6,4},{7,5},{8,10},{9,11},{10,... | collective-permute-start | bytes 3080 | tf_op jit(solution)/shard_map/ppermute | solution.py:198
  145.4 12.8 %collective-permute-start.31 = (f32[256]{0:T(256)S(1)}, f32[256]{0:T(256)S(1)}, u32[]{:S(2)}, u32[]{:S(2)}) collective-permute-start(f32[256]{0:T(256)S(1)} %multiply_reduce_fusion.1), channel_id=1, source_target_pairs={{0,3},{1,2},{2,1},{3,0},{4,7},{5,6},{6,5},{7,4},{8,11},{9,10},{10,... | collective-permute-start | bytes 3080 | tf_op jit(solution)/shard_map/ppermute | solution.py:198
  145.4 12.8 %collective-permute-start.29 = (f32[256]{0:T(256)S(1)}, f32[256]{0:T(256)S(1)}, u32[]{:S(2)}, u32[]{:S(2)}) collective-permute-start(f32[256]{0:T(256)S(1)} %multiply_reduce_fusion.1), channel_id=1, source_target_pairs={{0,1},{1,0},{2,3},{3,2},{4,5},{5,4},{6,7},{7,6},{8,9},{9,8},{10,11... | collective-permute-start | bytes 3080 | tf_op jit(solution)/shard_map/ppermute | solution.py:198
  156.0 3.6 %collective-permute-start.35 = (f32[256]{0:T(256)S(1)}, f32[256]{0:T(256)S(1)}, u32[]{:S(2)}, u32[]{:S(2)}) collective-permute-start(f32[256]{0:T(256)S(1)} %multiply_reduce_fusion), channel_id=1, source_target_pairs={{0,2},{1,3},{2,0},{3,1},{4,6},{5,7},{6,4},{7,5},{8,10},{9,11},{10,... | collective-permute-start | bytes 3080 | tf_op jit(solution)/shard_map/ppermute | solution.py:198
  (21 other events, 83.9 us)

commit v8 on v6

--- a/solution.py
+++ b/solution.py
@@ -198,7 +198,7 @@
     return x + swap(x, 1) + (swap(x, 2) + swap(x, 3))
 
 
-TOKEN_CHUNKS = (1, 1, 2)
+TOKEN_CHUNKS = (1, 1, 2, 4)
 OUTPUT_CHUNKS = 2
 CAND_AXIS = 4
 

time: 154 us -> 166 us (1.078)
  starting transfers between devices: 35.7 us -> 43 us
  Pallas kernels: 42.8 us -> 47.3 us
    ppermute x6 -> x8, waiting for transfers between devices: 22.9 us -> 10.7 us  [inner(): return [lax.ppermute(x, ('groups', 'cand'), inner_pairs) for x in parts]]
    ppermute x9 -> x12, waiting for transfers between devices: 4.29 us -> 15.3 us  [outer(): lax.ppermute(x, 'cand', [(0, 1), (1, 0), (2, 3), (3, 2)])]
    pallas_call x4 -> x5, Pallas kernels: 13.7 us -> 18.4 us  [project(): pl.pallas_call(functools.partial(project_body, chunks=len(chunks)), in_sp...]
    ppermute x6 -> x8, starting transfers between devices: 7.21 us -> 11.4 us  [inner(): return [lax.ppermute(x, ('groups', 'cand'), inner_pairs) for x in parts]]
    ppermute x9 -> x12, starting transfers between devices: 13.2 us -> 15.9 us  [outer(): lax.ppermute(x, 'cand', [(0, 1), (1, 0), (2, 3), (3, 2)])]
    ppermute x22 -> x25, waiting for transfers between devices: 34.9 us -> 35.5 us  [swap(): return lax.ppermute(x, 'tensor', [(t, t ^ bit) for t in range(4)])]
    ppermute x22 -> x25, starting transfers between devices: 15.3 us -> 15.8 us  [swap(): return lax.ppermute(x, 'tensor', [(t, t ^ bit) for t in range(4)])]
  transfers between devices with their start and end apart: 37 -> 45, of which waited for: 13 -> 13; matrix products, arithmetic and copies ran while one was open for 2% -> 2% of each run, Pallas kernels for 19% -> 21%
where the time goes in v8:
time: 166 us; the launch traced here: 165 us
  waiting for transfers between devices  61.5 us (37%)
  Pallas kernels  47.3 us (28%)
  starting transfers between devices  43 us (26%)
  other arithmetic  6.26 us (4%)
  local copies, waits for them, and re-layouts  5.99 us (4%)
    ppermute x25, waiting for transfers between devices, swap(): return lax.ppermute(x, 'tensor', [(t, t ^ bit) for t in range(4)])  35.5 us
    pallas_call x3, Pallas kernels, attention(): pl.pallas_call(functools.partial(attention_body, slots=len(slots), begun=...  20.6 us
    pallas_call x5, Pallas kernels, project(): pl.pallas_call(functools.partial(project_body, chunks=len(chunks)), in_sp...  18.4 us
    ppermute x12, starting transfers between devices, outer(): lax.ppermute(x, 'cand', [(0, 1), (1, 0), (2, 3), (3, 2)])  15.9 us
    ppermute x25, starting transfers between devices, swap(): return lax.ppermute(x, 'tensor', [(t, t ^ bit) for t in range(4)])  15.8 us
    ppermute x12, waiting for transfers between devices, outer(): lax.ppermute(x, 'cand', [(0, 1), (1, 0), (2, 3), (3, 2)])  15.3 us
    ppermute x8, starting transfers between devices, inner(): return [lax.ppermute(x, ('groups', 'cand'), inner_pairs) for x in parts]  11.4 us
    ppermute x8, waiting for transfers between devices, inner(): return [lax.ppermute(x, ('groups', 'cand'), inner_pairs) for x in parts]  10.7 us
  transfers between devices with their start and end apart: 45, of which 13 were waited for; matrix products, arithmetic and copies ran while one was open for 2% of the time, Pallas kernels for 21%

profile of v8, /device:TPU:0, one launch (start us, length us, event | category | flops | bytes accessed | tf_op | source)
XLA Modules:
  0.0 165.5 jit_solution(2806198542663240681)
XLA Ops:
  0.7 1.7 %fusion.1 = (f32[512]{0:T(512)S(1)}, bf16[512,1152]{1,0:T(8,128)(2,1)S(1)}) fusion(bf16[512,1152]{1,0:T(8,128)(2,1)} %param.9, f32[1152]{0:T(1024)S(1)} %convert_reduce_fusion.1), kind=kLoop, calls=%fused_computation.3 | loop fusion | flops 2948608 | bytes 2365952 | tf_op jit(solution)/shard_map/reduce_sum | solution.py:232
  2.4 3.0 %collective-permute-start.1 = (f32[512]{0:T(512)S(1)}, f32[512]{0:T(512)S(1)}, u32[]{:S(2)}, u32[]{:S(2)}) collective-permute-start(f32[512]{0:T(512)S(1)} %get-tuple-element.24), channel_id=1, source_target_pairs={{0,2},{1,3},{2,0},{3,1},{4,6},{5,7},{6,4},{7,5},{8,10},{9,11},{10,... | collective-permute-start | bytes 6152 | tf_op jit(solution)/shard_map/ppermute | solution.py:194
  5.7 1.9 %collective-permute-start.4 = (bf16[64,1152]{1,0:T(8,128)(2,1)S(1)}, bf16[64,1152]{1,0:T(8,128)(2,1)S(1)}, u32[]{:S(2)}, u32[]{:S(2)}) collective-permute-start(bf16[64,1152]{1,0:T(8,128)(2,1)S(1)} %get-tuple-element.26.refs_0_), channel_id=1, source_target_pairs={{0,2},{1,3},{2,0},{3,1},{4,6},{5,7},{6,4},{7,5},{8,10},{9,11},{10,... | collective-permute-start | bytes 442376 | tf_op jit(solution)/shard_map/ppermute | solution.py:194
  12.6 3.0 %collective-permute-done.7.refs_2_.refs_6_ = bf16[64,1152]{1,0:T(8,128)(2,1)S(1)} collective-permute-done((bf16[64,1152]{1,0:T(8,128)(2,1)S(1)}, bf16[64,1152]{1,0:T(8,128)(2,1)S(1)}, u32[]{:S(2)}, u32[]{:S(2)}) %collective-permute-start.7) | collective-permute-done | bytes 147488 | tf_op jit(solution)/shard_map/ppermute | solution.py:194
  17.1 2.3 %copy-done = bf16[4608,512]{1,0:T(8,128)(2,1)S(1)} copy-done((bf16[4608,512]{1,0:T(8,128)(2,1)S(1)}, bf16[4608,512]{1,0:T(8,128)(2,1)}, u32[]{:S(2)}) %copy-start) | copy-done | bytes 4718616
  19.4 2.3 %copy-done.1 = bf16[4608,512]{1,0:T(8,128)(2,1)S(1)} copy-done((bf16[4608,512]{1,0:T(8,128)(2,1)S(1)}, bf16[4608,512]{1,0:T(8,128)(2,1)}, u32[]{:S(2)}) %copy-start.1) | copy-done | bytes 4718616
  21.7 2.3 %project.5 = bf16[2,64,512]{2,1,0:T(8,128)(2,1)S(1)} custom-call(s32[4]{0:T(128)S(1)} %pad_add_fusion.2.rank_ref, f32[64,1]{1,0:T(8,128)S(1)} %copy.13.inverse_ref, bf16[64,1152]{1,0:T(8,128)(2,1)S(1)} %get-tuple-element.26.refs_0_, bf16[64,1152]{1,0:T(8,128)(2,1)S(1)} %collective-permute-done.3.refs_1_, ...), custom_call_target="tpu_custom_call" | custom-call | flops 10000000000 | bytes 1000000 | tf_op jit(solution)/shard_map/project/pallas_call | solution.py:63
  26.8 2.3 %project.6 = bf16[2,64,512]{2,1,0:T(8,128)(2,1)S(1)} custom-call(s32[4]{0:T(128)S(1)} %pad_add_fusion.2.rank_ref, f32[64,1]{1,0:T(8,128)S(1)} %copy.14.inverse_ref, bf16[64,1152]{1,0:T(8,128)(2,1)S(1)} %get-tuple-element.28.refs_0_.refs_4_, bf16[64,1152]{1,0:T(8,128)(2,1)S(1)} %collective-permute-done.6.refs_1_.refs_5_, ...), custom_call_target="tpu_custom_call" | custom-call | flops 10000000000 | bytes 1000000 | tf_op jit(solution)/shard_map/project/pallas_call | solution.py:63
  30.7 1.6 collective-permute-start.16
  32.3 7.1 %collective-permute-done.13.refs_14_.refs_2_ = bf16[256,1152]{1,0:T(8,128)(2,1)S(1)} collective-permute-done((bf16[256,1152]{1,0:T(8,128)(2,1)S(1)}, bf16[256,1152]{1,0:T(8,128)(2,1)S(1)}, u32[]{:S(2)}, u32[]{:S(2)}) %collective-permute-start.13) | collective-permute-done | bytes 589856 | tf_op jit(solution)/shard_map/ppermute | solution.py:194
  39.5 2.1 %project.7 = bf16[2,128,512]{2,1,0:T(8,128)(2,1)S(1)} custom-call(s32[4]{0:T(128)S(1)} %pad_add_fusion.2.rank_ref, f32[128,1]{1,0:T(8,128)S(1)} %copy.15.inverse_ref, bf16[128,1152]{1,0:T(8,128)(2,1)S(1)} %slice.119.refs_0_.refs_8_, bf16[128,1152]{1,0:T(8,128)(2,1)S(1)} %collective-permute-done.9.refs_1_.refs_9_, ...), custom_call_target="tpu_custom_call" | custom-call | flops 10000000000 | bytes 1000000 | tf_op jit(solution)/shard_map/project/pallas_call | solution.py:63
  43.2 1.6 collective-permute-start.20
  44.8 3.4 %project.9 = bf16[2,256,512]{2,1,0:T(8,128)(2,1)S(1)} custom-call(s32[4]{0:T(128)S(1)} %pad_add_fusion.2.rank_ref, f32[256,1]{1,0:T(8,128)S(1)} %copy.17.inverse_ref, bf16[256,1152]{1,0:T(8,128)(2,1)S(1)} %slice.120.refs_12_.refs_0_, bf16[256,1152]{1,0:T(8,128)(2,1)S(1)} %collective-permute-done.12.refs_13_.refs_1_, ...), custom_call_target="tpu_custom_call" | custom-call | flops 10000000000 | bytes 1000000 | tf_op jit(solution)/shard_map/project/pallas_call | solution.py:63
  49.9 8.3 %project.8.q_ref = bf16[1,512,1024]{2,1,0:T(8,128)(2,1)S(1)} custom-call(s32[4]{0:T(128)S(1)} %pad_add_fusion.2.rank_ref, f32[512,1]{1,0:T(8,128)S(1)} %copy.16.inverse_ref, bf16[64,1152]{1,0:T(8,128)(2,1)S(1)} %get-tuple-element.26.refs_0_, bf16[64,1152]{1,0:T(8,128)(2,1)S(1)} %collective-permute-done.3.refs_1_, ...), custom_call_target="tpu_custom_call" | custom-call | flops 10000000000 | bytes 1000000 | tf_op jit(solution)/shard_map/project/pallas_call | solution.py:63
  63.5 1.6 collective-permute-start.26
  66.7 1.6 collective-permute-start.22
  68.4 3.5 %collective-permute-done.23 = bf16[2,128,512]{2,1,0:T(8,128)(2,1)S(1)} collective-permute-done((bf16[2,128,512]{2,1,0:T(8,128)(2,1)S(1)}, bf16[2,128,512]{2,1,0:T(8,128)(2,1)S(1)}, u32[]{:S(2)}, u32[]{:S(2)}) %collective-permute-start.23) | collective-permute-done | bytes 262176 | tf_op jit(solution)/shard_map/ppermute | solution.py:249
  71.9 1.6 collective-permute-start.24
  75.1 7.6 %collective-permute-done.22 = bf16[2,64,512]{2,1,0:T(8,128)(2,1)S(1)} collective-permute-done((bf16[2,64,512]{2,1,0:T(8,128)(2,1)S(1)}, bf16[2,64,512]{2,1,0:T(8,128)(2,1)S(1)}, u32[]{:S(2)}, u32[]{:S(2)}) %collective-permute-start.22) | collective-permute-done | bytes 131104 | tf_op jit(solution)/shard_map/ppermute | solution.py:244
  84.3 5.9 %collective-permute-done.29 = bf16[2,64,512]{2,1,0:T(8,128)(2,1)S(1)} collective-permute-done((bf16[2,64,512]{2,1,0:T(8,128)(2,1)S(1)}, bf16[2,64,512]{2,1,0:T(8,128)(2,1)S(1)}, u32[]{:S(2)}, u32[]{:S(2)}) %collective-permute-start.29) | collective-permute-done | bytes 131104 | tf_op jit(solution)/shard_map/ppermute | solution.py:249
  90.3 1.6 collective-permute-start.28
  92.3 1.6 collective-permute-start.32
  94.7 11.8 %attention.3 = (f32[512,1024]{1,0:T(8,128)S(1)}, f32[512,512]{1,0:T(8,128)S(1)}) custom-call(f32[4,1536]{1,0:T(4,128)S(1)} %slice.122.bias_ref, bf16[1,512,1024]{2,1,0:T(8,128)(2,1)S(1)} %project.8.q_ref, bf16[2,512,512]{2,1,0:T(8,128)(2,1)S(1)} %pad_maximum_fusion.1.refs_0_.refs_1_, bf16[2,512,512]{2,1,0:T(8,128)(2,1)S(1)} %pad_maximum_fusion.1.refs_0_.refs_1_, ...), custom_call_target="tpu_custom_call" | custom-call | flops 10000000000 | bytes 1000000 | tf_op jit(solution)/shard_map/attention/pallas_call | solution.py:157
  106.5 7.6 %collective-permute-done.34 = bf16[2,256,512]{2,1,0:T(8,128)(2,1)S(1)} collective-permute-done((bf16[2,256,512]{2,1,0:T(8,128)(2,1)S(1)}, bf16[2,256,512]{2,1,0:T(8,128)(2,1)S(1)}, u32[]{:S(2)}, u32[]{:S(2)}) %collective-permute-start.34) | collective-permute-done | bytes 524320 | tf_op jit(solution)/shard_map/ppermute | solution.py:244
  114.7 4.4 %attention.4.x_ref = bf16[256,1024]{1,0:T(8,128)(2,1)S(1)} custom-call(f32[2,512]{1,0:T(2,128)S(1)} %get-tuple-element.53.bias_ref, bf16[1,256,1024]{2,1,0:T(8,128)(2,1)S(1)} %get-tuple-element.51.q_ref, bf16[2,512,512]{2,1,0:T(8,128)(2,1)S(1)} %maximum_select_fusion.1.refs_0_.refs_1_, bf16[2,512,512]{2,1,0:T(8,128)(2,1)S(1)} %maximum_select_fusion.1.refs_0_.refs_1_, ...), custom_call_target="tpu_custom_call" | custom-call | flops 10000000000 | bytes 1000000 | tf_op jit(solution)/shard_map/attention/pallas_call | solution.py:157
  119.2 2.1 %output.5 = bf16[2,256,1152]{2,1,0:T(8,128)(2,1)S(1)} custom-call(s32[2]{0:T(128)S(1)} %pad_add_fusion.3.block_ref, bf16[256,1024]{1,0:T(8,128)(2,1)S(1)} %attention.4.x_ref, bf16[1024,4608]{1,0:T(8,128)(2,1)S(1)} %bitcast.45), custom_call_target="tpu_custom_call" | custom-call | flops 10000000000 | bytes 1000000 | tf_op jit(solution)/shard_map/output/pallas_call | solution.py:178
  121.4 2.1 %output.4 = bf16[2,256,1152]{2,1,0:T(8,128)(2,1)S(1)} custom-call(s32[2]{0:T(128)S(1)} %pad_add_fusion.block_ref, bf16[256,1024]{1,0:T(8,128)(2,1)S(1)} %attention.4.x_ref, bf16[1024,4608]{1,0:T(8,128)(2,1)S(1)} %bitcast.45), custom_call_target="tpu_custom_call" | custom-call | flops 10000000000 | bytes 1000000 | tf_op jit(solution)/shard_map/output/pallas_call | solution.py:178
  124.3 4.4 %attention.5.x_ref = bf16[256,1024]{1,0:T(8,128)(2,1)S(1)} custom-call(f32[2,512]{1,0:T(2,128)S(1)} %get-tuple-element.54.bias_ref, bf16[1,256,1024]{2,1,0:T(8,128)(2,1)S(1)} %get-tuple-element.52.q_ref, bf16[2,512,512]{2,1,0:T(8,128)(2,1)S(1)} %maximum_select_fusion.1.refs_0_.refs_1_, bf16[2,512,512]{2,1,0:T(8,128)(2,1)S(1)} %maximum_select_fusion.1.refs_0_.refs_1_, ...), custom_call_target="tpu_custom_call" | custom-call | flops 10000000000 | bytes 1000000 | tf_op jit(solution)/shard_map/attention/pallas_call | solution.py:157
  128.7 2.1 %output.7 = bf16[2,256,1152]{2,1,0:T(8,128)(2,1)S(1)} custom-call(s32[2]{0:T(128)S(1)} %pad_add_fusion.3.block_ref, bf16[256,1024]{1,0:T(8,128)(2,1)S(1)} %attention.5.x_ref, bf16[1024,4608]{1,0:T(8,128)(2,1)S(1)} %bitcast.45), custom_call_target="tpu_custom_call" | custom-call | flops 10000000000 | bytes 1000000 | tf_op jit(solution)/shard_map/output/pallas_call | solution.py:178
  132.1 2.1 %output.6 = bf16[2,256,1152]{2,1,0:T(8,128)(2,1)S(1)} custom-call(s32[2]{0:T(128)S(1)} %pad_add_fusion.block_ref, bf16[256,1024]{1,0:T(8,128)(2,1)S(1)} %attention.5.x_ref, bf16[1024,4608]{1,0:T(8,128)(2,1)S(1)} %bitcast.45), custom_call_target="tpu_custom_call" | custom-call | flops 10000000000 | bytes 1000000 | tf_op jit(solution)/shard_map/output/pallas_call | solution.py:178
  135.4 11.8 %collective-permute-done.36 = bf16[256,1152]{1,0:T(8,128)(2,1)S(1)} collective-permute-done((bf16[256,1152]{1,0:T(8,128)(2,1)S(1)}, bf16[256,1152]{1,0:T(8,128)(2,1)S(1)}, u32[]{:S(2)}, u32[]{:S(2)}) %collective-permute-start.36) | collective-permute-done | bytes 589856 | tf_op jit(solution)/shard_map/ppermute | solution.py:194
  149.8 9.5 %collective-permute-done.41 = bf16[256,1152]{1,0:T(8,128)(2,1)S(1)} collective-permute-done((bf16[256,1152]{1,0:T(8,128)(2,1)S(1)}, bf16[256,1152]{1,0:T(8,128)(2,1)S(1)}, u32[]{:S(2)}, u32[]{:S(2)}) %collective-permute-start.41) | collective-permute-done | bytes 589856 | tf_op jit(solution)/shard_map/ppermute | solution.py:194
  (145 shorter events, 38.8 us)
Async XLA Ops:
  7.6 8.9 %collective-permute-start.3 = (bf16[64,1152]{1,0:T(8,128)(2,1)S(1)}, bf16[64,1152]{1,0:T(8,128)(2,1)S(1)}, u32[]{:S(2)}, u32[]{:S(2)}) collective-permute-start(bf16[64,1152]{1,0:T(8,128)(2,1)S(1)} %get-tuple-element.26.refs_0_), channel_id=1, source_target_pairs={{0,1},{1,0},{2,3},{3,2},{4,5},{5,4},{6,7},{7,6},{8,9},{9,8},{10,11... | collective-permute-start | bytes 442376 | tf_op jit(solution)/shard_map/ppermute | solution.py:194
  9.2 14.9 %collective-permute-start.6 = (bf16[64,1152]{1,0:T(8,128)(2,1)S(1)}, bf16[64,1152]{1,0:T(8,128)(2,1)S(1)}, u32[]{:S(2)}, u32[]{:S(2)}) collective-permute-start(bf16[64,1152]{1,0:T(8,128)(2,1)S(1)} %get-tuple-element.28.refs_0_.refs_4_), channel_id=1, source_target_pairs={{0,1},{1,0},{2,3},{3,2},{4,5},{5,4},{6,7},{7,6},{8,9},{9,8},{10,11... | collective-permute-start | bytes 442376 | tf_op jit(solution)/shard_map/ppermute | solution.py:194
  12.0 17.1 %collective-permute-start.9 = (bf16[128,1152]{1,0:T(8,128)(2,1)S(1)}, bf16[128,1152]{1,0:T(8,128)(2,1)S(1)}, u32[]{:S(2)}, u32[]{:S(2)}) collective-permute-start(bf16[128,1152]{1,0:T(8,128)(2,1)S(1)} %slice.119.refs_0_.refs_8_), channel_id=1, source_target_pairs={{0,1},{1,0},{2,3},{3,2},{4,5},{5,4},{6,7},{7,6},{8,9},{9,8},{10,11... | collective-permute-start | bytes 884744 | tf_op jit(solution)/shard_map/ppermute | solution.py:194
  15.6 11.2 %collective-permute-start.10 = (bf16[128,1152]{1,0:T(8,128)(2,1)S(1)}, bf16[128,1152]{1,0:T(8,128)(2,1)S(1)}, u32[]{:S(2)}, u32[]{:S(2)}) collective-permute-start(bf16[128,1152]{1,0:T(8,128)(2,1)S(1)} %slice.119.refs_0_.refs_8_), channel_id=1, source_target_pairs={{0,2},{1,3},{2,0},{3,1},{4,6},{5,7},{6,4},{7,5},{8,10},{9,11},{10,... | collective-permute-start | bytes 884744 | tf_op jit(solution)/shard_map/ppermute | solution.py:194
  16.5 26.6 %collective-permute-start.12 = (bf16[256,1152]{1,0:T(8,128)(2,1)S(1)}, bf16[256,1152]{1,0:T(8,128)(2,1)S(1)}, u32[]{:S(2)}, u32[]{:S(2)}) collective-permute-start(bf16[256,1152]{1,0:T(8,128)(2,1)S(1)} %slice.120.refs_12_.refs_0_), channel_id=1, source_target_pairs={{0,1},{1,0},{2,3},{3,2},{4,5},{5,4},{6,7},{7,6},{8,9},{9,8},{10,11... | collective-permute-start | bytes 1769480 | tf_op jit(solution)/shard_map/ppermute | solution.py:194
  16.6 8.6 %collective-permute-start.8 = (bf16[64,1152]{1,0:T(8,128)(2,1)S(1)}, bf16[64,1152]{1,0:T(8,128)(2,1)S(1)}, u32[]{:S(2)}, u32[]{:S(2)}) collective-permute-start(bf16[64,1152]{1,0:T(8,128)(2,1)S(1)} %collective-permute-done.7.refs_2_.refs_6_), channel_id=1, source_target_pairs={{0,1},{1,0},{2,3},{3,2},{4,5},{5,4},{6,7},{7,6},{8,9},{9,8},{10,11... | collective-permute-start | bytes 442376 | tf_op jit(solution)/shard_map/ppermute | solution.py:194
  24.1 15.4 %collective-permute-start.13 = (bf16[256,1152]{1,0:T(8,128)(2,1)S(1)}, bf16[256,1152]{1,0:T(8,128)(2,1)S(1)}, u32[]{:S(2)}, u32[]{:S(2)}) collective-permute-start(bf16[256,1152]{1,0:T(8,128)(2,1)S(1)} %slice.120.refs_12_.refs_0_), channel_id=1, source_target_pairs={{0,2},{1,3},{2,0},{3,1},{4,6},{5,7},{6,4},{7,5},{8,10},{9,11},{10,... | collective-permute-start | bytes 1769480 | tf_op jit(solution)/shard_map/ppermute | solution.py:194
  25.2 23.5 %collective-permute-start.15 = (bf16[2,64,512]{2,1,0:T(8,128)(2,1)S(1)}, bf16[2,64,512]{2,1,0:T(8,128)(2,1)S(1)}, u32[]{:S(2)}, u32[]{:S(2)}) collective-permute-start(bf16[2,64,512]{2,1,0:T(8,128)(2,1)S(1)} %project.5), channel_id=1, source_target_pairs={{0,4},{4,0},{8,12},{12,8},{1,5},{5,1},{9,13},{13,9},{2,6},{6,2},{1... | collective-permute-start | bytes 393224 | tf_op jit(solution)/shard_map/ppermute | solution.py:244
  29.1 12.5 %collective-permute-start.19 = (bf16[2,64,512]{2,1,0:T(8,128)(2,1)S(1)}, bf16[2,64,512]{2,1,0:T(8,128)(2,1)S(1)}, u32[]{:S(2)}, u32[]{:S(2)}) collective-permute-start(bf16[2,64,512]{2,1,0:T(8,128)(2,1)S(1)} %project.5), channel_id=1, source_target_pairs={{0,16},{16,0},{12,28},{28,12},{4,8},{8,4},{20,24},{24,20},{1,17},{... | collective-permute-start | bytes 393224 | tf_op jit(solution)/shard_map/ppermute | solution.py:249
  30.7 27.6 %collective-permute-start.16 = (bf16[2,64,512]{2,1,0:T(8,128)(2,1)S(1)}, bf16[2,64,512]{2,1,0:T(8,128)(2,1)S(1)}, u32[]{:S(2)}, u32[]{:S(2)}) collective-permute-start(bf16[2,64,512]{2,1,0:T(8,128)(2,1)S(1)} %project.6), channel_id=1, source_target_pairs={{0,4},{4,0},{8,12},{12,8},{1,5},{5,1},{9,13},{13,9},{2,6},{6,2},{1... | collective-permute-start | bytes 393224 | tf_op jit(solution)/shard_map/ppermute | solution.py:244
  41.6 17.6 %collective-permute-start.21 = (bf16[2,64,512]{2,1,0:T(8,128)(2,1)S(1)}, bf16[2,64,512]{2,1,0:T(8,128)(2,1)S(1)}, u32[]{:S(2)}, u32[]{:S(2)}) collective-permute-start(bf16[2,64,512]{2,1,0:T(8,128)(2,1)S(1)} %project.6), channel_id=1, source_target_pairs={{0,16},{16,0},{12,28},{28,12},{4,8},{8,4},{20,24},{24,20},{1,17},{... | collective-permute-start | bytes 393224 | tf_op jit(solution)/shard_map/ppermute | solution.py:249
  43.2 17.6 %collective-permute-start.20 = (bf16[2,64,512]{2,1,0:T(8,128)(2,1)S(1)}, bf16[2,64,512]{2,1,0:T(8,128)(2,1)S(1)}, u32[]{:S(2)}, u32[]{:S(2)}) collective-permute-start(bf16[2,64,512]{2,1,0:T(8,128)(2,1)S(1)} %collective-permute-done.19), channel_id=1, source_target_pairs={{0,4},{4,0},{8,12},{12,8},{1,5},{5,1},{9,13},{13,9},{2,6},{6,2},{1... | collective-permute-start | bytes 393224 | tf_op jit(solution)/shard_map/ppermute | solution.py:244
  48.2 16.9 %collective-permute-start.18 = (bf16[2,256,512]{2,1,0:T(8,128)(2,1)S(1)}, bf16[2,256,512]{2,1,0:T(8,128)(2,1)S(1)}, u32[]{:S(2)}, u32[]{:S(2)}) collective-permute-start(bf16[2,256,512]{2,1,0:T(8,128)(2,1)S(1)} %project.9), channel_id=1, source_target_pairs={{0,4},{4,0},{8,12},{12,8},{1,5},{5,1},{9,13},{13,9},{2,6},{6,2},{1... | collective-permute-start | bytes 1572872 | tf_op jit(solution)/shard_map/ppermute | solution.py:244
  48.7 14.8 %collective-permute-start.25 = (bf16[2,256,512]{2,1,0:T(8,128)(2,1)S(1)}, bf16[2,256,512]{2,1,0:T(8,128)(2,1)S(1)}, u32[]{:S(2)}, u32[]{:S(2)}) collective-permute-start(bf16[2,256,512]{2,1,0:T(8,128)(2,1)S(1)} %project.9), channel_id=1, source_target_pairs={{0,16},{16,0},{12,28},{28,12},{4,8},{8,4},{20,24},{24,20},{1,17},{... | collective-permute-start | bytes 1572872 | tf_op jit(solution)/shard_map/ppermute | solution.py:249
  58.2 8.5 %collective-permute-start.27 = (bf16[2,64,512]{2,1,0:T(8,128)(2,1)S(1)}, bf16[2,64,512]{2,1,0:T(8,128)(2,1)S(1)}, u32[]{:S(2)}, u32[]{:S(2)}) collective-permute-start(bf16[2,64,512]{2,1,0:T(8,128)(2,1)S(1)} %collective-permute-done.15), channel_id=1, source_target_pairs={{0,16},{16,0},{12,28},{28,12},{4,8},{8,4},{20,24},{24,20},{1,17},{... | collective-permute-start | bytes 393224 | tf_op jit(solution)/shard_map/ppermute | solution.py:249
  59.1 14.4 %collective-permute-start.17 = (bf16[2,128,512]{2,1,0:T(8,128)(2,1)S(1)}, bf16[2,128,512]{2,1,0:T(8,128)(2,1)S(1)}, u32[]{:S(2)}, u32[]{:S(2)}) collective-permute-start(bf16[2,128,512]{2,1,0:T(8,128)(2,1)S(1)} %project.7), channel_id=1, source_target_pairs={{0,4},{4,0},{8,12},{12,8},{1,5},{5,1},{9,13},{13,9},{2,6},{6,2},{1... | collective-permute-start | bytes 786440 | tf_op jit(solution)/shard_map/ppermute | solution.py:244
  60.8 11.1 %collective-permute-start.23 = (bf16[2,128,512]{2,1,0:T(8,128)(2,1)S(1)}, bf16[2,128,512]{2,1,0:T(8,128)(2,1)S(1)}, u32[]{:S(2)}, u32[]{:S(2)}) collective-permute-start(bf16[2,128,512]{2,1,0:T(8,128)(2,1)S(1)} %project.7), channel_id=1, source_target_pairs={{0,16},{16,0},{12,28},{28,12},{4,8},{8,4},{20,24},{24,20},{1,17},{... | collective-permute-start | bytes 786440 | tf_op jit(solution)/shard_map/ppermute | solution.py:249
  63.5 30.8 %collective-permute-start.26 = (bf16[2,256,512]{2,1,0:T(8,128)(2,1)S(1)}, bf16[2,256,512]{2,1,0:T(8,128)(2,1)S(1)}, u32[]{:S(2)}, u32[]{:S(2)}) collective-permute-start(bf16[2,256,512]{2,1,0:T(8,128)(2,1)S(1)} %collective-permute-done.25), channel_id=1, source_target_pairs={{0,4},{4,0},{8,12},{12,8},{1,5},{5,1},{9,13},{13,9},{2,6},{6,2},{1... | collective-permute-start | bytes 1572872 | tf_op jit(solution)/shard_map/ppermute | solution.py:244
  65.1 28.8 %collective-permute-start.33 = (bf16[2,256,512]{2,1,0:T(8,128)(2,1)S(1)}, bf16[2,256,512]{2,1,0:T(8,128)(2,1)S(1)}, u32[]{:S(2)}, u32[]{:S(2)}) collective-permute-start(bf16[2,256,512]{2,1,0:T(8,128)(2,1)S(1)} %collective-permute-done.18), channel_id=1, source_target_pairs={{0,16},{16,0},{12,28},{28,12},{4,8},{8,4},{20,24},{24,20},{1,17},{... | collective-permute-start | bytes 1572872 | tf_op jit(solution)/shard_map/ppermute | solution.py:249
  66.7 16.0 %collective-permute-start.22 = (bf16[2,64,512]{2,1,0:T(8,128)(2,1)S(1)}, bf16[2,64,512]{2,1,0:T(8,128)(2,1)S(1)}, u32[]{:S(2)}, u32[]{:S(2)}) collective-permute-start(bf16[2,64,512]{2,1,0:T(8,128)(2,1)S(1)} %collective-permute-done.21), channel_id=1, source_target_pairs={{0,4},{4,0},{8,12},{12,8},{1,5},{5,1},{9,13},{13,9},{2,6},{6,2},{1... | collective-permute-start | bytes 393224 | tf_op jit(solution)/shard_map/ppermute | solution.py:244
  71.9 20.0 %collective-permute-start.24 = (bf16[2,128,512]{2,1,0:T(8,128)(2,1)S(1)}, bf16[2,128,512]{2,1,0:T(8,128)(2,1)S(1)}, u32[]{:S(2)}, u32[]{:S(2)}) collective-permute-start(bf16[2,128,512]{2,1,0:T(8,128)(2,1)S(1)} %collective-permute-done.23), channel_id=1, source_target_pairs={{0,4},{4,0},{8,12},{12,8},{1,5},{5,1},{9,13},{13,9},{2,6},{6,2},{1... | collective-permute-start | bytes 786440 | tf_op jit(solution)/shard_map/ppermute | solution.py:244
  73.6 18.7 %collective-permute-start.31 = (bf16[2,128,512]{2,1,0:T(8,128)(2,1)S(1)}, bf16[2,128,512]{2,1,0:T(8,128)(2,1)S(1)}, u32[]{:S(2)}, u32[]{:S(2)}) collective-permute-start(bf16[2,128,512]{2,1,0:T(8,128)(2,1)S(1)} %collective-permute-done.17), channel_id=1, source_target_pairs={{0,16},{16,0},{12,28},{28,12},{4,8},{8,4},{20,24},{24,20},{1,17},{... | collective-permute-start | bytes 786440 | tf_op jit(solution)/shard_map/ppermute | solution.py:249
  82.8 7.5 %collective-permute-start.29 = (bf16[2,64,512]{2,1,0:T(8,128)(2,1)S(1)}, bf16[2,64,512]{2,1,0:T(8,128)(2,1)S(1)}, u32[]{:S(2)}, u32[]{:S(2)}) collective-permute-start(bf16[2,64,512]{2,1,0:T(8,128)(2,1)S(1)} %collective-permute-done.16), channel_id=1, source_target_pairs={{0,16},{16,0},{12,28},{28,12},{4,8},{8,4},{20,24},{24,20},{1,17},{... | collective-permute-start | bytes 393224 | tf_op jit(solution)/shard_map/ppermute | solution.py:249
  90.3 16.2 %collective-permute-start.28 = (bf16[2,64,512]{2,1,0:T(8,128)(2,1)S(1)}, bf16[2,64,512]{2,1,0:T(8,128)(2,1)S(1)}, u32[]{:S(2)}, u32[]{:S(2)}) collective-permute-start(bf16[2,64,512]{2,1,0:T(8,128)(2,1)S(1)} %collective-permute-done.27), channel_id=1, source_target_pairs={{0,4},{4,0},{8,12},{12,8},{1,5},{5,1},{9,13},{13,9},{2,6},{6,2},{1... | collective-permute-start | bytes 393224 | tf_op jit(solution)/shard_map/ppermute | solution.py:244
  91.9 14.6 %collective-permute-start.30 = (bf16[2,64,512]{2,1,0:T(8,128)(2,1)S(1)}, bf16[2,64,512]{2,1,0:T(8,128)(2,1)S(1)}, u32[]{:S(2)}, u32[]{:S(2)}) collective-permute-start(bf16[2,64,512]{2,1,0:T(8,128)(2,1)S(1)} %collective-permute-done.29), channel_id=1, source_target_pairs={{0,4},{4,0},{8,12},{12,8},{1,5},{5,1},{9,13},{13,9},{2,6},{6,2},{1... | collective-permute-start | bytes 393224 | tf_op jit(solution)/shard_map/ppermute | solution.py:244
  92.3 14.2 %collective-permute-start.32 = (bf16[2,128,512]{2,1,0:T(8,128)(2,1)S(1)}, bf16[2,128,512]{2,1,0:T(8,128)(2,1)S(1)}, u32[]{:S(2)}, u32[]{:S(2)}) collective-permute-start(bf16[2,128,512]{2,1,0:T(8,128)(2,1)S(1)} %collective-permute-done.31), channel_id=1, source_target_pairs={{0,4},{4,0},{8,12},{12,8},{1,5},{5,1},{9,13},{13,9},{2,6},{6,2},{1... | collective-permute-start | bytes 786440 | tf_op jit(solution)/shard_map/ppermute | solution.py:244
  93.9 20.2 %collective-permute-start.34 = (bf16[2,256,512]{2,1,0:T(8,128)(2,1)S(1)}, bf16[2,256,512]{2,1,0:T(8,128)(2,1)S(1)}, u32[]{:S(2)}, u32[]{:S(2)}) collective-permute-start(bf16[2,256,512]{2,1,0:T(8,128)(2,1)S(1)} %collective-permute-done.33), channel_id=1, source_target_pairs={{0,4},{4,0},{8,12},{12,8},{1,5},{5,1},{9,13},{13,9},{2,6},{6,2},{1... | collective-permute-start | bytes 1572872 | tf_op jit(solution)/shard_map/ppermute | solution.py:244
  131.0 16.2 %collective-permute-start.36 = (bf16[256,1152]{1,0:T(8,128)(2,1)S(1)}, bf16[256,1152]{1,0:T(8,128)(2,1)S(1)}, u32[]{:S(2)}, u32[]{:S(2)}) collective-permute-start(bf16[256,1152]{1,0:T(8,128)(2,1)S(1)} %fusion.3), channel_id=1, source_target_pairs={{0,2},{1,3},{2,0},{3,1},{4,6},{5,7},{6,4},{7,5},{8,10},{9,11},{10,... | collective-permute-start | bytes 1769480 | tf_op jit(solution)/shard_map/ppermute | solution.py:194
  134.3 25.0 %collective-permute-start.41 = (bf16[256,1152]{1,0:T(8,128)(2,1)S(1)}, bf16[256,1152]{1,0:T(8,128)(2,1)S(1)}, u32[]{:S(2)}, u32[]{:S(2)}) collective-permute-start(bf16[256,1152]{1,0:T(8,128)(2,1)S(1)} %fusion.4), channel_id=1, source_target_pairs={{0,2},{1,3},{2,0},{3,1},{4,6},{5,7},{6,4},{7,5},{8,10},{9,11},{10,... | collective-permute-start | bytes 1769480 | tf_op jit(solution)/shard_map/ppermute | solution.py:194
  147.6 13.2 %collective-permute-start.38 = (f32[256]{0:T(256)S(1)}, f32[256]{0:T(256)S(1)}, u32[]{:S(2)}, u32[]{:S(2)}) collective-permute-start(f32[256]{0:T(256)S(1)} %multiply_reduce_fusion.1), channel_id=1, source_target_pairs={{0,2},{1,3},{2,0},{3,1},{4,6},{5,7},{6,4},{7,5},{8,10},{9,11},{10,... | collective-permute-start | bytes 3080 | tf_op jit(solution)/shard_map/ppermute | solution.py:194
  148.7 13.2 %collective-permute-start.39 = (f32[256]{0:T(256)S(1)}, f32[256]{0:T(256)S(1)}, u32[]{:S(2)}, u32[]{:S(2)}) collective-permute-start(f32[256]{0:T(256)S(1)} %multiply_reduce_fusion.1), channel_id=1, source_target_pairs={{0,3},{1,2},{2,1},{3,0},{4,7},{5,6},{6,5},{7,4},{8,11},{9,10},{10,... | collective-permute-start | bytes 3080 | tf_op jit(solution)/shard_map/ppermute | solution.py:194
  148.7 13.2 %collective-permute-start.37 = (f32[256]{0:T(256)S(1)}, f32[256]{0:T(256)S(1)}, u32[]{:S(2)}, u32[]{:S(2)}) collective-permute-start(f32[256]{0:T(256)S(1)} %multiply_reduce_fusion.1), channel_id=1, source_target_pairs={{0,1},{1,0},{2,3},{3,2},{4,5},{5,4},{6,7},{7,6},{8,9},{9,8},{10,11... | collective-permute-start | bytes 3080 | tf_op jit(solution)/shard_map/ppermute | solution.py:194
  (26 other events, 150.7 us)
